TPU v7x, 768 devices: a whole 4x8x12 slice. The times are simulated.
768 devices in a mesh: dp: 32 (over y, x), head: 24 (over z, core).
Axes of the slice: x: 4, y: 8, z: 12, core: 2. Of those that a mesh axis runs over, the one named last changes fastest.
Arguments:
- queries: bfloat16 [12288, 3072], P('dp', 'head'), may hold values from -8 to 8
- keys: bfloat16 [12288, 384], P('dp'), may hold values from -5 to 5
- values: bfloat16 [12288, 384], P('dp'), may hold values from -6 to 6
- block_of_slot: int32 [64], replicated, may hold values from 0 to 63, as said below
- doc_lengths: int32 [4], replicated, may hold values from 1 to 6144, 12288 in all
- out_weight: bfloat16 [3072, 2048], P('head'), may hold values from -0.5 to 0.5
Outputs:
- mixed: bfloat16 [12288, 2048], P(('dp', 'head'))
Inputs may be any that keep to these rules, and one draw needn't show every extreme that they name: `block_of_slot`: a permutation of 0 .. 63; entries 2 i and 2 i + 1 are the two slots of index i of dp, and they add to 63.
All inputs are finite; a program needn't handle non-finite values.
Results may differ from a plain program's by a relative error of at most 0.02.
Values may be sent and summed in bfloat16 or wider, within the bound.
No kernel may reach another device: no remote copies, remote signals or barrier semaphores. Data moves between devices by JAX's collectives and lax.ppermute only.
A program may use at most 32 MiB of HBM per device.

v0:
```python
import math

import jax
import jax.numpy as jnp
from jax import lax
from jax.sharding import PartitionSpec as P


def slot_positions(first_row, row_count, table, half_rows):
    row_index = first_row + jnp.arange(row_count, dtype=jnp.int32)
    slot_index = row_index // half_rows
    all_slots = jnp.arange(table.shape[0], dtype=jnp.int32)
    block_id = jnp.sum(
        jnp.where(slot_index[:, None] == all_slots[None, :], table[None, :], 0), axis=1
    )
    return block_id * half_rows + row_index % half_rows


def document_ids(positions, bounds):
    return jnp.sum((positions[:, None] >= bounds[None, :]).astype(jnp.int32), axis=1)


def per_device(queries, keys, values, block_of_slot, doc_lengths, out_weight):
    tok_rows = queries.shape[0]
    head_size = queries.shape[1]
    half_rows = tok_rows // 2
    head_total = lax.axis_size("head")
    group_size = min(8, head_total)
    kv_start = lax.axis_index("head") // group_size * head_size
    own_keys = lax.dynamic_slice_in_dim(keys, kv_start, head_size, 1)
    own_values = lax.dynamic_slice_in_dim(values, kv_start, head_size, 1)
    bounds = jnp.cumsum(doc_lengths)[:-1]
    query_pos = slot_positions(lax.axis_index("dp") * tok_rows, tok_rows, block_of_slot, half_rows)
    query_doc = document_ids(query_pos, bounds)
    score_scale = 1.0 / math.sqrt(head_size)

    def attend(totals, key_block, value_block, allowed):
        run_max, run_sum, run_acc = totals
        scores = (
            jnp.einsum("qd,kd->qk", queries, key_block, preferred_element_type=jnp.float32)
            * score_scale
        )
        masked = jnp.where(allowed, scores, -1e30)
        new_max = jnp.maximum(run_max, jnp.max(masked, axis=1))
        weights = jnp.where(allowed, jnp.exp(masked - new_max[:, None]), 0.0)
        factor = jnp.exp(run_max - new_max)
        new_sum = run_sum * factor + jnp.sum(weights, axis=1)
        new_acc = run_acc * factor[:, None] + jnp.dot(
            weights.astype(jnp.bfloat16), value_block, preferred_element_type=jnp.float32
        )
        return (new_max, new_sum, new_acc)

    initial = (
        jnp.full((tok_rows,), -1e30, jnp.float32),
        jnp.zeros((tok_rows,), jnp.float32),
        jnp.zeros((tok_rows, head_size), jnp.float32),
    )
    totals = initial
    key_piece = lax.all_gather(own_keys, "dp", axis=0, tiled=True)
    value_piece = lax.all_gather(own_values, "dp", axis=0, tiled=True)
    shard_count = key_piece.shape[0] // tok_rows
    per_step = max(
        [1]
        + [
            option_width
            for option_width in range(1, shard_count + 1)
            if shard_count % option_width == 0 and option_width * tok_rows <= 1536
        ]
    )
    step_rows = per_step * tok_rows
    step_count = shard_count // per_step
    key_blocks = key_piece.reshape(step_count, step_rows, head_size)
    value_blocks = value_piece.reshape(step_count, step_rows, head_size)
    step_starts = step_rows * jnp.arange(step_count, dtype=jnp.int32)

    def advance(running, inputs):
        key_block, value_block, block_start = inputs
        key_pos = slot_positions(block_start, step_rows, block_of_slot, half_rows)
        key_doc = document_ids(key_pos, bounds)
        allowed = (query_doc[:, None] == key_doc[None, :]) & (
            key_pos[None, :] <= query_pos[:, None]
        )
        running = attend(running, key_block, value_block, allowed)
        return (running, None)

    totals, _ = lax.scan(advance, totals, (key_blocks, value_blocks, step_starts))
    run_max, run_sum, run_acc = totals
    attended = (run_acc / run_sum[:, None]).astype(jnp.bfloat16)
    partial_terms = jnp.dot(attended, out_weight, preferred_element_type=jnp.float32)
    mixed = lax.psum_scatter(
        partial_terms.astype(jnp.bfloat16), "head", scatter_dimension=0, tiled=True
    )
    return mixed


def solution(mesh):
    return jax.shard_map(
        per_device,
        mesh=mesh,
        in_specs=(P("dp", "head"), P("dp", None), P("dp", None), P(), P(), P("head", None)),
        out_specs=P(("dp", "head"), None),
        check_vma=False,
    )
```

profile of v0, /device:TPU:6, one launch (start us, length us, event | category | flops | bytes accessed | tf_op | source)
XLA Modules:
  0.0 361.6 jit_solution(3884719515901633309)
XLA Ops:
  6.5 1.6 constant_dynamic-slice_fusion.1
  8.2 1.5 constant_dynamic-slice_fusion
  9.9 0.8 reduce-window.4
  10.7 0.7 select_reduce_fusion.1
  11.6 94.7 %all-gather.3.cloned.1.call-done = bf16[12288,128]{1,0:T(8,128)(2,1)} async-done(((bf16[384,128]{1,0:T(8,128)(2,1)}), bf16[12288,128]{1,0:T(8,128)(2,1)}) %all-gather.3.cloned.1.call-update) | async-done | bytes 3145744 | tf_op jit(solution)/shard_map/all_gather | solution.py:59
  106.3 91.1 %all-gather.5.cloned.1.call-done = bf16[12288,128]{1,0:T(8,128)(2,1)} async-done(((bf16[384,128]{1,0:T(8,128)(2,1)}), bf16[12288,128]{1,0:T(8,128)(2,1)}) %all-gather.5.cloned.1.call-update) | async-done | bytes 3145744 | tf_op jit(solution)/shard_map/all_gather | solution.py:60
  197.4 68.2 %while.17 = (s32[]{:T(128)}, f32[384]{0:T(512)S(1)}, f32[384]{0:T(512)S(1)}, f32[384,128]{1,0:T(8,128)S(1)}, s32[384]{0:T(512)S(1)}, /*index=5*/s32[8]{0:T(128)S...) while((s32[]{:T(128)}, f32[384]{0:T(512)S(1)}, ...), condition=%wide.region_8.9_spmd.clone, body=%wide.region_3.8_spmd.clone.sunk | while | flops 313089408 | bytes 8470961 | solution.py:86
  198.6 0.8 select_reduce_fusion.3
  200.0 2.7 fusion.45
  202.8 1.0 fusion.46
  203.8 2.1 fusion.48
  205.9 0.6 dynamic_slice.48
  207.1 0.8 select_reduce_fusion.3
  208.6 2.7 fusion.45
  211.3 1.0 fusion.46
  212.3 2.1 fusion.48
  214.4 0.6 dynamic_slice.48
  215.6 0.8 select_reduce_fusion.3
  217.1 2.7 fusion.45
  219.8 1.0 fusion.46
  220.8 2.1 fusion.48
  223.0 0.6 dynamic_slice.48
  224.2 0.8 select_reduce_fusion.3
  225.6 2.7 fusion.45
  228.4 1.0 fusion.46
  229.3 2.1 fusion.48
  231.5 0.6 dynamic_slice.48
  232.7 0.8 select_reduce_fusion.3
  234.2 2.7 fusion.45
  236.9 1.0 fusion.46
  237.9 2.1 fusion.48
  240.0 0.6 dynamic_slice.48
  241.2 0.8 select_reduce_fusion.3
  242.7 2.7 fusion.45
  245.4 1.0 fusion.46
  246.4 2.1 fusion.48
  248.6 0.6 dynamic_slice.48
  249.7 0.8 select_reduce_fusion.3
  251.2 2.7 fusion.45
  254.0 1.0 fusion.46
  254.9 2.1 fusion.48
  257.1 0.6 dynamic_slice.48
  258.3 0.8 select_reduce_fusion.3
  259.8 2.7 fusion.45
  262.5 1.0 fusion.46
  263.5 2.1 fusion.48
  265.6 1.8 convolution_convert_fusion
  267.4 87.7 %reduce-scatter.2.cloned.1.call-done = bf16[16,2048]{1,0:T(8,128)(2,1)} async-done(((bf16[384,2048]{1,0:T(8,128)(2,1)}), bf16[16,2048]{1,0:T(8,128)(2,1)}) %reduce-scatter.2.cloned.1.call-update) | async-done | bytes 65552 | tf_op jit(solution)/shard_map/reduce_scatter | solution.py:90
  (65 shorter events, 11.2 us)
Async XLA Ops:
  6.5 259.1 %copy-start = (bf16[128,2048]{1,0:T(8,128)(2,1)S(1)}, bf16[128,2048]{1,0:T(8,128)(2,1)}, u32[]{:S(2)}) copy-start(bf16[128,2048]{1,0:T(8,128)(2,1)} %param.13) | copy-start | bytes 1572868
  6.5 99.8 %all-gather.3.cloned.1.call-start = ((), (), s32[]{:S(2)}) async-start(), calls=%async_computation.1 | async-start | bytes 3244032 | tf_op jit(solution)/shard_map/all_gather | solution.py:59
  8.1 189.2 %all-gather.5.cloned.1.call-start = ((), (), s32[]{:S(2)}) async-start(), calls=%async_computation.2 | async-start | bytes 3244032 | tf_op jit(solution)/shard_map/all_gather | solution.py:60
  9.8 345.3 %reduce-scatter.2.cloned.1.call-start = ((), (), s32[]{:S(2)}) async-start(), calls=%async_computation.3 | async-start | bytes 1638400 | tf_op jit(solution)/shard_map/reduce_scatter | solution.py:90
Sparse Core Ops, SparseCore 0:
  11.1 95.1 all-gather.2
  110.0 87.3 all-gather.4
  267.5 87.5 reduce-scatter.1
where the time goes:
time: 363 us; the launch traced here: 362 us
  waiting for transfers between devices  274 us (75%)
  matrix products  40.4 us (11%)
  other arithmetic  26 us (7%)
  between operations  13.2 us (4%)
  local copies, waits for them, and re-layouts  7.88 us (2%)
    all_gather x1, waiting for transfers between devices, per_device(): key_piece = lax.all_gather(own_keys, 'dp', axis=0, tiled=True)  94.7 us
    all_gather x1, waiting for transfers between devices, per_device(): value_piece = lax.all_gather(own_values, 'dp', axis=0, tiled=True)  91.1 us
    reduce_scatter x1, waiting for transfers between devices, per_device(): lax.psum_scatter(partial_terms.astype(jnp.bfloat16), 'head', scatter_dime...  87.7 us
    dot_general x8, matrix products, attend(): jnp.einsum('qd,kd->qk', queries, key_block, preferred_element_type=jnp.fl...  21.7 us
    dot_general x8, matrix products, attend(): jnp.dot(weights.astype(jnp.bfloat16), value_block, preferred_element_type...  17 us
    reduce_sum x8, other arithmetic, attend(): new_sum = run_sum * factor + jnp.sum(weights, axis=1)  7.65 us
  transfers between devices with their start and end apart: 3, of which 3 were waited for; matrix products, arithmetic and copies ran while one was open for 1% of the time, Pallas kernels for 0%

commit v1 on v0

v1 whole, which is shorter than its diff:
```python
import math

import jax
import jax.numpy as jnp
from jax import lax
from jax.experimental import pallas as pl
from jax.experimental.pallas import tpu as pltpu
from jax.sharding import Mesh, PartitionSpec as P

AXES = ("y", "xh", "xl", "zh", "zm", "zl", "core")
SIZES = (8, 2, 2, 3, 2, 2, 2)
DP = ("y", "xh", "xl")
HEAD = ("zh", "zm", "zl", "core")
KV_AXES = ("y", "xh")
TEAM = ("xl", "zl", "core")
Z6 = ("zh", "zm")

TOK = 384
HALF = 192
HD = 128
QUART = 48
SRC = 16
PIECES = 2 * SRC
CHUNK = 256
KEYS = PIECES * QUART
PAD = KEYS + CHUNK
TILE = 4 * HALF
TEAM_SIZE = 8
STAT = 16
SEND = TOK + STAT
LOW = -1e30
FAR = 1 << 20
SCALE = math.log2(math.e) / math.sqrt(HD)


def spread_kernel(at_ref, k_hbm, v_hbm, out_hbm, buf, in_sem, out_sem):
    row = pl.multiple_of(at_ref[0] * QUART, 16)
    col = pl.multiple_of(at_ref[1] * HD, HD)
    loads = []
    for n, src in enumerate((k_hbm, v_hbm)):
        for half in range(2):
            loads.append(
                pltpu.make_async_copy(
                    src.at[pl.ds(half * HALF + row, QUART), pl.ds(col, HD)],
                    buf.at[pl.ds((2 * n + half) * QUART, QUART), :],
                    in_sem.at[2 * n + half],
                )
            )
    for copy in loads:
        copy.start()
    for copy in loads:
        copy.wait()
    stores = [
        pltpu.make_async_copy(buf, out_hbm.at[n], out_sem.at[n]) for n in range(SRC)
    ]
    for copy in stores:
        copy.start()
    for copy in stores:
        copy.wait()


def attend_kernel(
    rank_ref,
    sorted_ref,
    tile_ref,
    kv_ref,
    q_ref,
    kpos_ref,
    qpos_ref,
    qstart_ref,
    out_ref,
    k_scr,
    v_scr,
    q_scr,
    s_scr,
    m_scr,
    l_scr,
    acc_scr,
    st_scr,
):
    for piece in range(PIECES):
        src, half = divmod(piece, 2)
        at = pl.multiple_of(rank_ref[piece] * QUART, 16)
        k_scr[pl.ds(at, QUART), :] = kv_ref[src, half * QUART : (half + 1) * QUART, :]
        v_scr[pl.ds(at, QUART), :] = kv_ref[
            src, (2 + half) * QUART : (3 + half) * QUART, :
        ]
    k_scr[KEYS:, :] = jnp.zeros((CHUNK, HD), jnp.bfloat16)
    v_scr[KEYS:, :] = jnp.zeros((CHUNK, HD), jnp.bfloat16)
    st_scr[...] = jnp.zeros_like(st_scr)
    for tile in range(4):
        xl, half = divmod(tile, 2)
        for d in range(4):
            for j in range(4):
                for z3 in range(3):
                    to = d * HALF + j * QUART + z3 * 16
                    of = half * HALF + z3 * 64 + d * 16
                    q_scr[tile, to : to + 16, :] = q_ref[xl * 4 + j, of : of + 16, :]

    def one_tile(tile, carry):
        low, steps, q_first, start_last = (tile_ref[tile, n] for n in range(4))
        m_scr[...] = jnp.full_like(m_scr, LOW)
        l_scr[...] = jnp.zeros_like(l_scr)
        acc_scr[...] = jnp.zeros_like(acc_scr)

        def one_step(step, carry):
            first = low * QUART + step * CHUNK
            at = pl.multiple_of(first, 16)
            s_scr[...] = lax.dot_general(
                k_scr[pl.ds(at, CHUNK), :],
                q_scr[tile],
                (((1,), (1,)), ((), ())),
                preferred_element_type=jnp.float32,
            )
            first_pos = sorted_ref[first // QUART] * HALF
            last_pos = sorted_ref[(first + CHUNK - 1) // QUART] * HALF + HALF - 1

            @pl.when((last_pos > q_first) | (first_pos < start_last))
            def _():
                key_pos = kpos_ref[pl.ds(at, CHUNK), :]
                allowed = (key_pos <= qpos_ref[pl.ds(tile, 1), :]) & (
                    key_pos >= qstart_ref[pl.ds(tile, 1), :]
                )
                s_scr[...] = jnp.where(allowed, s_scr[...], LOW)

            scores = s_scr[...]
            old = m_scr[...]
            new = jnp.maximum(old, jnp.max(scores, axis=0, keepdims=True))
            m_scr[...] = new
            probs = jnp.exp2((scores - new) * SCALE)
            factor = jnp.exp2((old - new) * SCALE)
            l_scr[...] = l_scr[...] * factor + jnp.sum(probs, axis=0, keepdims=True)
            acc_scr[...] = acc_scr[...] * factor + lax.dot_general(
                v_scr[pl.ds(at, CHUNK), :],
                probs.astype(jnp.bfloat16),
                (((0,), (0,)), ((), ())),
                preferred_element_type=jnp.float32,
            )
            return carry

        lax.fori_loop(0, steps, one_step, 0)
        total = jnp.where(l_scr[...] > 0, l_scr[...], 1.0)
        part = (acc_scr[...] / total).T.astype(jnp.bfloat16)
        lse = m_scr[...] * SCALE + jnp.log2(total)
        high = lse.astype(jnp.bfloat16).astype(jnp.float32)
        mid = (lse - high).astype(jnp.bfloat16).astype(jnp.float32)
        stats = (high, mid, lse - high - mid)
        xl4 = (tile // 2) * 4
        half = tile % 2
        rows = pl.multiple_of(half * HALF, 16)
        for d in range(4):
            out_ref[xl4 + d, pl.ds(rows, HALF), :] = part[d * HALF : (d + 1) * HALF]
            for n, stat in enumerate(stats):
                if d % 2:
                    stat = pltpu.roll(
                        jnp.broadcast_to(stat, (8, TILE)), TILE - 64, 1
                    )[:1]
                base = d * HALF - (d % 2) * 64
                for w in range(2):
                    st_scr[xl4 + d, pl.ds(half * 6 + n * 2 + w, 1), :] = stat[
                        :, base + w * 128 : base + (w + 1) * 128
                    ]
        return carry

    lax.fori_loop(0, 4, one_tile, 0)
    for dest in range(TEAM_SIZE):
        out_ref[dest, TOK:, :] = st_scr[dest].astype(jnp.bfloat16)


def project_kernel(at_ref, got_ref, w0_ref, w1_ref, out_ref, att_scr):
    for half in range(2):
        sides = []
        for w in range(2):
            lse = []
            for k in range(TEAM_SIZE):
                stat = got_ref[k, TOK:, :].astype(jnp.float32)
                row = half * 6 + w
                lse.append(
                    stat[row : row + 1] + stat[row + 2 : row + 3] + stat[row + 4 : row + 5]
                )
            lse = jnp.concatenate(lse, axis=0)
            weight = jnp.exp2(lse - jnp.max(lse, axis=0, keepdims=True))
            weight = weight / jnp.sum(weight, axis=0, keepdims=True)
            sides.append(weight.T)
        weight = jnp.concatenate([sides[0], sides[1][:64]], axis=0)
        total = jnp.zeros((HALF, HD), jnp.float32)
        for k in range(TEAM_SIZE):
            total += weight[:, k : k + 1] * got_ref[
                k, half * HALF : (half + 1) * HALF, :
            ].astype(jnp.float32)
        att_scr[half] = total.astype(jnp.bfloat16)
    own = at_ref[0]
    out = None
    for n, (w_ref, part, flip) in enumerate(
        ((w0_ref, 0, 0), (w0_ref, 1, 2), (w1_ref, 0, 1), (w1_ref, 1, 3))
    ):
        rows = pl.multiple_of((own ^ flip) * QUART, 16)
        att = jnp.concatenate(
            [att_scr[half, pl.ds(rows, QUART), :] for half in range(2)], axis=0
        )
        term = jnp.dot(att, w_ref[part], preferred_element_type=jnp.float32)
        out = term if out is None else out + term
    out_ref[...] = out.astype(jnp.bfloat16)


def doc_start(pos, bounds):
    start = jnp.zeros_like(pos)
    for n in range(bounds.shape[0]):
        start = jnp.where(pos >= bounds[n], jnp.maximum(start, bounds[n]), start)
    return start


def per_device(queries, keys, values, block_of_slot, doc_lengths, out_weight):
    zl, core = lax.axis_index("zl"), lax.axis_index("core")
    own = zl * 2 + core
    at = jnp.stack([own, lax.axis_index("zh")]).astype(jnp.int32)
    any_spec = pl.BlockSpec(memory_space=pl.ANY)
    smem = pl.BlockSpec(memory_space=pltpu.SMEM)
    vmem = pl.BlockSpec(memory_space=pltpu.VMEM)
    spread = pl.pallas_call(
        spread_kernel,
        out_shape=jax.ShapeDtypeStruct((SRC, 4 * QUART, HD), jnp.bfloat16),
        in_specs=[smem, any_spec, any_spec],
        out_specs=any_spec,
        scratch_shapes=[
            pltpu.VMEM((4 * QUART, HD), jnp.bfloat16),
            pltpu.SemaphoreType.DMA((4,)),
            pltpu.SemaphoreType.DMA((SRC,)),
        ],
        name="spread",
    )(at, keys, values)
    kv = lax.all_to_all(spread, KV_AXES, 0, 0, tiled=True)
    q = lax.all_gather(queries, TEAM, axis=0)
    flip = [(0, 1), (1, 0)]
    w_side = lax.ppermute(out_weight, "zl", flip)
    w0 = jnp.stack([out_weight, w_side])
    w1 = lax.ppermute(w0, "core", flip)

    table = block_of_slot.reshape(8, 2, 2, 2)
    xl = lax.axis_index("xl")
    blocks = jnp.where(xl == 0, table[:, :, 0], table[:, :, 1]).reshape(PIECES)
    rank = jnp.sum((blocks[None, :] < blocks[:, None]).astype(jnp.int32), axis=1)
    slots = jnp.arange(PIECES, dtype=jnp.int32)
    in_order = jnp.sum(
        jnp.where(rank[None, :] == slots[:, None], blocks[None, :], 0), axis=1
    )
    bounds = jnp.cumsum(doc_lengths)[:-1]
    key_pos = (
        in_order[:, None] * HALF + own * QUART + jnp.arange(QUART, dtype=jnp.int32)
    ).reshape(KEYS, 1)
    key_pos = jnp.concatenate([key_pos, jnp.full((PAD - KEYS, 1), FAR, jnp.int32)])
    in_order_pad = jnp.concatenate(
        [in_order, jnp.full(((PAD - KEYS) // QUART + 1,), FAR // HALF, jnp.int32)]
    )
    here = lax.axis_index("y") * 2 + lax.axis_index("xh")
    q_block = jnp.sum(
        jnp.where(
            jnp.arange(SRC, dtype=jnp.int32)[:, None] == here,
            block_of_slot.reshape(SRC, 4),
            0,
        ),
        axis=0,
    )
    lane = jnp.arange(TILE, dtype=jnp.int32)
    in_half = (lane % QUART) // 16 * 64 + lane // HALF * 16 + lane % 16
    q_pos = q_block[:, None] * HALF + in_half[None, :]
    q_start = doc_start(q_pos, bounds)
    first_start = doc_start(q_block * HALF, bounds)
    last_start = doc_start(q_block * HALF + HALF - 1, bounds)
    low = jnp.sum(
        (blocks[None, :] < first_start[:, None] // HALF).astype(jnp.int32), axis=1
    )
    high = jnp.sum((blocks[None, :] <= q_block[:, None]).astype(jnp.int32), axis=1)
    steps = ((high - low) * QUART + CHUNK - 1) // CHUNK
    tiles = jnp.stack([low, steps, q_block * HALF, last_start], axis=1)

    sent = pl.pallas_call(
        attend_kernel,
        out_shape=jax.ShapeDtypeStruct((TEAM_SIZE, SEND, HD), jnp.bfloat16),
        in_specs=[smem, smem, smem, vmem, vmem, vmem, vmem, vmem],
        out_specs=vmem,
        scratch_shapes=[
            pltpu.VMEM((PAD, HD), jnp.bfloat16),
            pltpu.VMEM((PAD, HD), jnp.bfloat16),
            pltpu.VMEM((4, TILE, HD), jnp.bfloat16),
            pltpu.VMEM((CHUNK, TILE), jnp.float32),
            pltpu.VMEM((1, TILE), jnp.float32),
            pltpu.VMEM((1, TILE), jnp.float32),
            pltpu.VMEM((HD, TILE), jnp.float32),
            pltpu.VMEM((TEAM_SIZE, STAT, HD), jnp.float32),
        ],
        compiler_params=pltpu.CompilerParams(vmem_limit_bytes=32 << 20),
        cost_estimate=pl.CostEstimate(
            flops=4 * 4 * TILE * KEYS * HD,
            transcendentals=4 * TILE * KEYS,
            bytes_accessed=4 << 20,
        ),
        name="attend",
    )(rank, in_order_pad, tiles, kv, q, key_pos, q_pos, q_start)
    got = lax.all_to_all(sent, TEAM, 0, 0, tiled=True)
    terms = pl.pallas_call(
        project_kernel,
        out_shape=jax.ShapeDtypeStruct((TOK // 4, out_weight.shape[1]), jnp.bfloat16),
        in_specs=[smem, vmem, vmem, vmem],
        out_specs=vmem,
        scratch_shapes=[pltpu.VMEM((2, HALF, HD), jnp.bfloat16)],
        compiler_params=pltpu.CompilerParams(vmem_limit_bytes=32 << 20),
        name="project",
    )(at, got, w0, w1)
    parts = lax.all_to_all(terms.reshape(6, 16, -1), Z6, 0, 0, tiled=True)
    return jnp.sum(parts.astype(jnp.float32), axis=0).astype(jnp.bfloat16)


def solution(mesh):
    fine = Mesh(mesh.devices.reshape(SIZES), AXES)
    return jax.shard_map(
        per_device,
        mesh=fine,
        in_specs=(P(DP, HEAD), P(DP, None), P(DP, None), P(), P(), P(HEAD, None)),
        out_specs=P(DP + HEAD, None),
        check_vma=False,
    )
```

time: 363 us -> 115 us (0.32)
  waiting for transfers between devices: 274 us -> 22 us
  blocking collectives: 0 us -> 47.9 us
  matrix products: 40.4 us -> 0 us
  starting transfers between devices: 0.09 us -> 20.5 us
  other arithmetic: 26 us -> 7.94 us
  between operations: 13.2 us -> 0.73 us
  Pallas kernels: 0 us -> 12.1 us
  local copies, waits for them, and re-layouts: 7.88 us -> 2.35 us
    all_gather x2 -> x0, waiting for transfers between devices: 186 us -> none  [the longest x1 94.7 us: per_device(): key_piece = lax.all_gather(own_keys, 'dp', axis=0, tiled=True)]
    reduce_scatter x1 -> x0, waiting for transfers between devices: 87.7 us -> none  [per_device(): lax.psum_scatter(partial_terms.astype(jnp.bfloat16), 'head', scatter_dime...]
    dot_general x17 -> x0, matrix products: 40.4 us -> none  [the longest x8 21.7 us: attend(): jnp.einsum('qd,kd->qk', queries, key_block, preferred_element_type=jnp.fl...]
    all_to_all x0 -> x1, blocking collectives: none -> 31.2 us  [per_device(): parts = lax.all_to_all(terms.reshape(6, 16, -1), Z6, 0, 0, tiled=True)]
    ppermute x0 -> x2, waiting for transfers between devices: none -> 22 us  [the longest x1 19.3 us: per_device(): w_side = lax.ppermute(out_weight, 'zl', flip)]
    all_gather x0 -> x1, blocking collectives: none -> 16.8 us  [per_device(): q = lax.all_gather(queries, TEAM, axis=0)]
    all_to_all x0 -> x2, starting transfers between devices: none -> 15.2 us  [the longest x1 10.1 us: per_device(): kv = lax.all_to_all(spread, KV_AXES, 0, 0, tiled=True)]
    reduce_sum x26 -> x5, other arithmetic: 15.5 us -> 1.28 us  [the longest x1 0.69 us: per_device(): return jnp.sum(parts.astype(jnp.float32), axis=0).astype(jnp.bfloat16)]
  transfers between devices with their start and end apart: 3 -> 4, of which waited for: 3 -> 2; matrix products, arithmetic and copies ran while one was open for 1% -> 7% of each run, Pallas kernels for 0% -> 0%
where the time goes in v1:
time: 115 us; the launch traced here: 114 us
  blocking collectives  47.9 us (42%)
  waiting for transfers between devices  22 us (19%)
  starting transfers between devices  20.5 us (18%)
  Pallas kernels  12.1 us (11%)
  other arithmetic  7.94 us (7%)
  local copies, waits for them, and re-layouts  2.35 us (2%)
    all_to_all x1, blocking collectives, per_device(): parts = lax.all_to_all(terms.reshape(6, 16, -1), Z6, 0, 0, tiled=True)  31.2 us
    ppermute x1, waiting for transfers between devices, per_device(): w_side = lax.ppermute(out_weight, 'zl', flip)  19.3 us
    all_gather x1, blocking collectives, per_device(): q = lax.all_gather(queries, TEAM, axis=0)  16.8 us
    all_to_all x1, starting transfers between devices, per_device(): kv = lax.all_to_all(spread, KV_AXES, 0, 0, tiled=True)  10.1 us
    pallas_call x1, Pallas kernels, per_device(): pl.pallas_call(attend_kernel, out_shape=jax.ShapeDtypeStruct((TEAM_SIZE,...  7.78 us
    all_to_all x1, starting transfers between devices, per_device(): got = lax.all_to_all(sent, TEAM, 0, 0, tiled=True)  5.13 us
    select_n x2, other arithmetic, doc_start(): start = jnp.where(pos >= bounds[n], jnp.maximum(start, bounds[n]), start)  3.72 us
    ppermute x1, starting transfers between devices, per_device(): w_side = lax.ppermute(out_weight, 'zl', flip)  3.37 us
  transfers between devices with their start and end apart: 4, of which 2 were waited for; matrix products, arithmetic and copies ran while one was open for 7% of the time, Pallas kernels for 0%

profile of v1, /device:TPU:6, one launch (start us, length us, event | category | flops | bytes accessed | tf_op | source)
XLA Modules:
  0.0 113.5 jit_solution(1891256695146320844)
XLA Ops:
  0.0 0.6 pad_add_fusion.1.at_ref
  0.6 2.5 %spread.1 = bf16[16,192,128]{2,1,0:T(8,128)(2,1)} custom-call(s32[2]{0:T(128)} %pad_add_fusion.1.at_ref, bf16[384,384]{1,0:T(8,128)(2,1)} %k_hbm.1, bf16[384,384]{1,0:T(8,128)(2,1)} %v_hbm.1), custom_call_target="tpu_custom_call" | custom-call | tf_op jit(solution)/shard_map/spread/pallas_call | solution.py:220
  3.1 0.0 copy-start.3
  3.1 10.1 %all-to-all-start = ((bf16[16,192,128]{2,1,0:T(8,128)(2,1)}), bf16[16,192,128]{2,1,0:T(8,128)(2,1)S(1)}, u32[]{:S(2)}, u32[]{:S(2)}) async-start(bf16[16,192,128]{2,1,0:T(8,128)(2,1)} %spread.1), calls=%async_computation | async-start | bytes 1572864 | tf_op jit(solution)/shard_map/all_to_all | solution.py:232
  13.2 0.0 copy-done.3
  13.2 0.1 reshape.253
  13.3 0.1 reshape.252
  13.4 0.0 copy-start.4
  13.4 0.6 copy-done.4
  14.1 0.2 reduce-window.4
  14.3 0.7 fusion.26
  15.5 0.1 select_n.147
  15.6 0.2 convert_reduce_fusion.rank_ref
  15.8 0.1 select_reduce_fusion.1
  15.9 1.8 %broadcast_multiply_fusion = (s32[4]{0:T(128)S(1)}, s32[4]{0:T(128)S(1)}, s32[4,1]{0,1:T(1,128)S(1)}) fusion(s32[4]{0:T(128)S(1)} %select_reduce_fusion.1, s32[]{:T(128)S(6)} %max_broadcast_in_dim.7, s32[]{:T(128)} %bitcast.5, s32[]{:T(128)} %bitcast.4, s32[]{:T(128)} %bitcast.3), kind=kLoop, calls=%fused_computation.66 | loop fusion | flops 68 | bytes 80 | tf_op jit(solution)/shard_map/mul | solution.py:268
  17.7 0.2 convert_reduce_fusion.2
  17.9 0.1 select_reduce_fusion
  18.1 0.1 copy.21
  18.2 0.1 copy.18
  18.3 0.1 copy.22
  18.4 0.1 iota_add_fusion
  18.4 0.4 add.152
  18.8 0.0 copy-start.2
  18.8 0.1 concatenate.7.kpos_ref
  18.9 1.8 %maximum_select_fusion.2 = (s32[4,1]{1,0:T(4,128)S(1)}, s32[4,1]{1,0:T(4,128)S(1)}) fusion(s32[4,1]{1,0:T(4,128)S(1)} %copy.22, s32[]{:T(128)S(6)} %max_broadcast_in_dim.7, s32[]{:T(128)} %bitcast.5, s32[]{:T(128)} %bitcast.4, s32[]{:T(128)} %bitcast.3, s32[4,1]{1,0:T(4,128)S(1)} %copy.18, s32[4,1]{1,0:T(4,128)S(1)} %copy.21), kind=kLoop, calls=%fused_computation.46 | loop fusion | flops 108 | bytes 96 | tf_op jit(solution)/shard_map/jit(_where)/select_n | solution.py:209
  20.7 0.1 pad_add_fusion.tile_ref
  20.8 1.9 %maximum_select_fusion = (s32[4,768]{1,0:T(4,128)S(1)}, s32[4,768]{1,0:T(4,128)S(1)}) fusion(s32[]{:T(128)S(6)} %max_broadcast_in_dim.7, s32[]{:T(128)} %bitcast.5, s32[]{:T(128)} %bitcast.4, s32[]{:T(128)} %bitcast.3, s32[768]{0:T(1024)S(1)} %fusion.11, s32[4]{0:T(128)S(1)} %get-tuple-element.9), kind=kLoop, calls=%fused_computation.1 | loop fusion | flops 27648 | bytes 27680 | tf_op jit(solution)/shard_map/jit(_where)/select_n | solution.py:209
  22.7 0.0 copy-done.2
  22.8 16.8 %all-gather = bf16[3072,128]{1,0:T(8,128)(2,1)S(1)} all-gather(bf16[384,128]{1,0:T(8,128)(2,1)S(1)} %copy-done.2), channel_id=2, replica_groups=mesh['y'=8,'xh'=2,'xl'=2,'zh'=3,'zm'=2,'zl'=2,'core'=2] {'xl','zl','core'}, dimensions={0}, use_global_device_ids=true | all-gather | bytes 884736 | tf_op jit(solution)/shard_map/all_gather | solution.py:233
  39.5 0.0 all-to-all-done.kv_ref
  39.5 7.8 %attend.1 = bf16[8,400,128]{2,1,0:T(8,128)(2,1)} custom-call(s32[32]{0:T(128)S(1)} %convert_reduce_fusion.rank_ref, s32[38]{0:T(128)S(1)} %concatenate.6.sorted_ref, s32[4,4]{1,0:T(4,128)S(1)} %pad_add_fusion.tile_ref, bf16[16,192,128]{2,1,0:T(8,128)(2,1)S(1)} %all-to-all-done.kv_ref, bf16[8,384,128]{2,1,0:T(8,128)(2,1)S(1)} %bitcast.15, ...), custom_call_target="tpu_custom_call" | custom-call | flops 2415919104 | bytes 4194304 | tf_op jit(solution)/shard_map/attend/pallas_call | solution.py:277
  47.3 0.0 copy-start.1
  47.3 5.1 %all-to-all-start.1 = ((bf16[8,400,128]{2,1,0:T(8,128)(2,1)}), bf16[8,400,128]{2,1,0:T(8,128)(2,1)S(1)}, u32[]{:S(2)}, u32[]{:S(2)}) async-start(bf16[8,400,128]{2,1,0:T(8,128)(2,1)} %attend.1), calls=%async_computation.1 | async-start | bytes 1638400 | tf_op jit(solution)/shard_map/all_to_all | solution.py:300
  52.4 0.0 copy-done.1
  52.4 3.4 %collective-permute-start = (bf16[128,2048]{1,0:T(8,128)(2,1)S(1)}, bf16[128,2048]{1,0:T(8,128)(2,1)S(1)}, u32[]{:S(2)}, u32[]{:S(2)}) collective-permute-start(bf16[128,2048]{1,0:T(8,128)(2,1)S(1)} %copy-done.1), channel_id=1, source_target_pairs={{0,2},{2,0},{1,3},{3,1},{4,6},{6,4},{5,7},{7,5},{8,10},{10,8},{9,1... | collective-permute-start | bytes 1572872 | tf_op jit(solution)/shard_map/ppermute | solution.py:235
  55.8 19.3 %collective-permute-done = bf16[128,2048]{1,0:T(8,128)(2,1)S(1)} collective-permute-done((bf16[128,2048]{1,0:T(8,128)(2,1)S(1)}, bf16[128,2048]{1,0:T(8,128)(2,1)S(1)}, u32[]{:S(2)}, u32[]{:S(2)}) %collective-permute-start) | collective-permute-done | bytes 524320 | tf_op jit(solution)/shard_map/ppermute | solution.py:235
  75.2 0.0 copy-start
  75.2 0.1 pad_maximum_fusion.w0_ref
  75.3 1.9 %collective-permute-start.1 = (bf16[2,128,2048]{2,1,0:T(8,128)(2,1)S(1)}, bf16[2,128,2048]{2,1,0:T(8,128)(2,1)S(1)}, u32[]{:S(2)}, u32[]{:S(2)}) collective-permute-start(bf16[2,128,2048]{2,1,0:T(8,128)(2,1)S(1)} %pad_maximum_fusion.w0_ref), channel_id=1, source_target_pairs={{0,1},{1,0},{2,3},{3,2},{4,5},{5,4},{6,7},{7,6},{8,9},{9,8},{10,11... | collective-permute-start | bytes 3145736 | tf_op jit(solution)/shard_map/ppermute | solution.py:237
  77.2 2.6 %collective-permute-done.1.w1_ref = bf16[2,128,2048]{2,1,0:T(8,128)(2,1)S(1)} collective-permute-done((bf16[2,128,2048]{2,1,0:T(8,128)(2,1)S(1)}, bf16[2,128,2048]{2,1,0:T(8,128)(2,1)S(1)}, u32[]{:S(2)}, u32[]{:S(2)}) %collective-permute-start.1) | collective-permute-done | bytes 1048608 | tf_op jit(solution)/shard_map/ppermute | solution.py:237
  79.8 0.0 all-to-all-done.1.got_ref
  79.8 0.0 copy-done
  79.8 1.8 %project.1 = bf16[96,2048]{1,0:T(8,128)(2,1)S(1)} custom-call(s32[2]{0:T(128)S(1)} %copy-done, bf16[8,400,128]{2,1,0:T(8,128)(2,1)S(1)} %all-to-all-done.1.got_ref, bf16[2,128,2048]{2,1,0:T(8,128)(2,1)S(1)} %pad_maximum_fusion.w0_ref, bf16[2,128,2048]{2,1,0:T(8,128)(2,1)S(1)} %collective-permute-done.1.w1_ref), custom_call_target="tpu_custom_call" | custom-call | tf_op jit(solution)/shard_map/project/pallas_call | solution.py:301
  81.7 31.2 %all_to_all.15 = bf16[6,16,2048]{2,1,0:T(8,128)(2,1)S(1)} all-to-all(bf16[6,16,2048]{2,1,0:T(8,128)(2,1)S(1)} %bitcast.14), channel_id=1, replica_groups=mesh['y'=8,'xh'=2,'xl'=2,'zh'=3,'zm'=2,'zl'=2,'core'=2] {'zh','zm'}, dimensions={0} | all-to-all | bytes 786432 | tf_op jit(solution)/shard_map/all_to_all | solution.py:310
  112.8 0.7 reduce_sum.65
  (5 shorter events, 0.1 us)
Async XLA Ops:
  3.1 10.1 %copy-start.3 = (s32[64]{0:T(128)S(1)}, s32[64]{0:T(128)}, u32[]{:S(2)}) copy-start(s32[64]{0:T(128)} %param.9) | copy-start | bytes 772
  3.1 36.4 %all-to-all-start = ((bf16[16,192,128]{2,1,0:T(8,128)(2,1)}), bf16[16,192,128]{2,1,0:T(8,128)(2,1)S(1)}, u32[]{:S(2)}, u32[]{:S(2)}) async-start(bf16[16,192,128]{2,1,0:T(8,128)(2,1)} %spread.1), calls=%async_computation | async-start | bytes 1572864 | tf_op jit(solution)/shard_map/all_to_all | solution.py:232
  13.4 0.7 copy-start.4
  18.8 3.9 %copy-start.2 = (bf16[384,128]{1,0:T(8,128)(2,1)S(1)}, bf16[384,128]{1,0:T(8,128)(2,1)}, u32[]{:S(2)}) copy-start(bf16[384,128]{1,0:T(8,128)(2,1)} %param.6) | copy-start | bytes 294916
  47.3 5.1 %copy-start.1 = (bf16[128,2048]{1,0:T(8,128)(2,1)S(1)}, bf16[128,2048]{1,0:T(8,128)(2,1)}, u32[]{:S(2)}) copy-start(bf16[128,2048]{1,0:T(8,128)(2,1)} %param.11) | copy-start | bytes 1572868
  47.3 32.5 %all-to-all-start.1 = ((bf16[8,400,128]{2,1,0:T(8,128)(2,1)}), bf16[8,400,128]{2,1,0:T(8,128)(2,1)S(1)}, u32[]{:S(2)}, u32[]{:S(2)}) async-start(bf16[8,400,128]{2,1,0:T(8,128)(2,1)} %attend.1), calls=%async_computation.1 | async-start | bytes 1638400 | tf_op jit(solution)/shard_map/all_to_all | solution.py:300
  52.4 22.7 %collective-permute-start = (bf16[128,2048]{1,0:T(8,128)(2,1)S(1)}, bf16[128,2048]{1,0:T(8,128)(2,1)S(1)}, u32[]{:S(2)}, u32[]{:S(2)}) collective-permute-start(bf16[128,2048]{1,0:T(8,128)(2,1)S(1)} %copy-done.1), channel_id=1, source_target_pairs={{0,2},{2,0},{1,3},{3,1},{4,6},{6,4},{5,7},{7,5},{8,10},{10,8},{9,1... | collective-permute-start | bytes 1572872 | tf_op jit(solution)/shard_map/ppermute | solution.py:235
  75.2 4.7 %copy-start = (s32[2]{0:T(128)S(1)}, s32[2]{0:T(128)}, u32[]{:S(2)}) copy-start(s32[2]{0:T(128)} %pad_add_fusion.1.at_ref) | copy-start | bytes 28
  75.3 4.6 %collective-permute-start.1 = (bf16[2,128,2048]{2,1,0:T(8,128)(2,1)S(1)}, bf16[2,128,2048]{2,1,0:T(8,128)(2,1)S(1)}, u32[]{:S(2)}, u32[]{:S(2)}) collective-permute-start(bf16[2,128,2048]{2,1,0:T(8,128)(2,1)S(1)} %pad_maximum_fusion.w0_ref), channel_id=1, source_target_pairs={{0,1},{1,0},{2,3},{3,2},{4,5},{5,4},{6,7},{7,6},{8,9},{9,8},{10,11... | collective-permute-start | bytes 3145736 | tf_op jit(solution)/shard_map/ppermute | solution.py:237

commit v2 on v1

v2 whole, which is shorter than its diff:
```python
import math

import jax
import jax.numpy as jnp
import numpy as np
from jax import lax
from jax.experimental import pallas as pl
from jax.experimental.pallas import tpu as pltpu
from jax.sharding import Mesh, PartitionSpec as P

AXES = ("y", "xh", "xl", "zh", "zm", "zl", "core")
SIZES = (8, 2, 2, 3, 2, 2, 2)
DP = ("y", "xh", "xl")
HEAD = ("zh", "zm", "zl", "core")
KV_AXES = ("y", "xh")
TEAM = ("xl", "zl", "core")
Z6 = ("zh", "zm")

TOK = 384
HALF = 192
HD = 128
QUART = 48
SRC = 16
PIECES = 2 * SRC
CHUNK = 256
KEYS = PIECES * QUART
PAD = KEYS + CHUNK
SLOTS = PIECES + CHUNK // QUART + 2
TILE = 4 * HALF
TEAM_SIZE = 8
STAT = 16
SEND = TOK + STAT
LOW = -1e30
FAR = 1 << 20
SCALE = math.log2(math.e) / math.sqrt(HD)


def spread_kernel(k_hbm, v_hbm, out_hbm, buf, in_sem, out_sem):
    own = lax.axis_index("zl") * 2 + lax.axis_index("core")
    row = pl.multiple_of(own * QUART, 16)
    col = pl.multiple_of(lax.axis_index("zh") * HD, HD)
    loads = []
    for n, src in enumerate((k_hbm, v_hbm)):
        for half in range(2):
            loads.append(
                pltpu.make_async_copy(
                    src.at[pl.ds(half * HALF + row, QUART), pl.ds(col, HD)],
                    buf.at[pl.ds((2 * n + half) * QUART, QUART), :],
                    in_sem.at[2 * n + half],
                )
            )
    for copy in loads:
        copy.start()
    for copy in loads:
        copy.wait()
    stores = [
        pltpu.make_async_copy(buf, out_hbm.at[n], out_sem.at[n]) for n in range(SRC)
    ]
    for copy in stores:
        copy.start()
    for copy in stores:
        copy.wait()


def start_of(pos, bounds):
    start = jnp.zeros_like(pos)
    for bound in bounds:
        start = jnp.where(pos >= bound, jnp.maximum(start, bound), start)
    return start


def table_kernel(
    slot_ref,
    len_ref,
    lane_ref,
    q_ref,
    rank_ref,
    sorted_ref,
    tile_ref,
    qpos_ref,
    qstart_ref,
    tiles_ref,
    where_scr,
    before_scr,
):
    xl = lax.axis_index("xl")
    here = lax.axis_index("y") * 2 + lax.axis_index("xh")

    def clear(n, carry):
        where_scr[n] = PIECES
        return carry

    lax.fori_loop(0, 2 * PIECES, clear, 0)
    for piece in range(PIECES):
        src, half = divmod(piece, 2)
        where_scr[slot_ref[4 * src + 2 * xl + half]] = piece

    def walk(block, count):
        before_scr[block] = count
        piece = where_scr[block]
        rank_ref[piece] = count
        sorted_ref[count] = block
        return count + (piece < PIECES).astype(jnp.int32)

    before_scr[2 * PIECES] = lax.fori_loop(0, 2 * PIECES, walk, jnp.int32(0))
    for n in range(PIECES, SLOTS):
        sorted_ref[n] = FAR // HALF
    bounds = [len_ref[0]]
    for n in range(1, len_ref.shape[0] - 1):
        bounds.append(bounds[-1] + len_ref[n])
    lane = lane_ref[...]
    for tile in range(4):
        rel, half = divmod(tile, 2)
        block = slot_ref[4 * here + 2 * (xl ^ rel) + half]
        base = block * HALF
        low = before_scr[lax.div(start_of(base, bounds), HALF)]
        high = before_scr[block + 1]
        tile_ref[tile, 0] = low
        tile_ref[tile, 1] = lax.div((high - low) * QUART + CHUNK - 1, CHUNK)
        tile_ref[tile, 2] = base
        tile_ref[tile, 3] = start_of(base + HALF - 1, bounds)
        pos = lane + base
        qpos_ref[tile : tile + 1, :] = pos
        qstart_ref[tile : tile + 1, :] = start_of(pos, bounds)
        for d in range(4):
            for j in range(4):
                for z3 in range(3):
                    to = d * HALF + j * QUART + z3 * 16
                    of = half * HALF + z3 * 64 + d * 16
                    tiles_ref[tile, to : to + 16, :] = q_ref[j, rel, of : of + 16, :]


def attend_kernel(
    rank_ref,
    sorted_ref,
    tile_ref,
    kv_ref,
    q_ref,
    qpos_ref,
    qstart_ref,
    out_ref,
    kpos_scr,
    k_scr,
    v_scr,
    s_scr,
    m_scr,
    l_scr,
    acc_scr,
    st_scr,
):
    for piece in range(PIECES):
        src, half = divmod(piece, 2)
        at = pl.multiple_of(rank_ref[piece] * QUART, 16)
        k_scr[pl.ds(at, QUART), :] = kv_ref[src, half * QUART : (half + 1) * QUART, :]
        v_scr[pl.ds(at, QUART), :] = kv_ref[
            src, (2 + half) * QUART : (3 + half) * QUART, :
        ]
    k_scr[KEYS:, :] = jnp.zeros((CHUNK, HD), jnp.bfloat16)
    v_scr[KEYS:, :] = jnp.zeros((CHUNK, HD), jnp.bfloat16)
    st_scr[...] = jnp.zeros_like(st_scr)
    own = lax.axis_index("zl") * 2 + lax.axis_index("core")
    row = lax.broadcasted_iota(jnp.int32, (QUART, HD), 0) + own * QUART
    for n in range(PIECES):
        kpos_scr[n * QUART : (n + 1) * QUART, :] = row + sorted_ref[n] * HALF
    kpos_scr[KEYS:, :] = jnp.full((PAD - KEYS, HD), FAR, jnp.int32)

    def one_tile(tile, carry):
        low, steps, q_first, start_last = (tile_ref[tile, n] for n in range(4))
        m_scr[...] = jnp.full_like(m_scr, LOW)
        l_scr[...] = jnp.zeros_like(l_scr)
        acc_scr[...] = jnp.zeros_like(acc_scr)

        def one_step(step, carry):
            first = low * QUART + step * CHUNK
            at = pl.multiple_of(first, 16)
            s_scr[...] = lax.dot_general(
                k_scr[pl.ds(at, CHUNK), :],
                q_ref[tile],
                (((1,), (1,)), ((), ())),
                preferred_element_type=jnp.float32,
            )
            first_pos = sorted_ref[lax.div(first, QUART)] * HALF
            last_pos = sorted_ref[lax.div(first + CHUNK - 1, QUART)] * HALF + HALF - 1

            @pl.when((last_pos > q_first) | (first_pos < start_last))
            def _():
                key_pos = kpos_scr[pl.ds(at, CHUNK), :]
                key_pos = jnp.concatenate([key_pos] * (TILE // HD), axis=1)
                allowed = (key_pos <= qpos_ref[pl.ds(tile, 1), :]) & (
                    key_pos >= qstart_ref[pl.ds(tile, 1), :]
                )
                s_scr[...] = jnp.where(allowed, s_scr[...], LOW)

            scores = s_scr[...]
            old = m_scr[...]
            new = jnp.maximum(old, jnp.max(scores, axis=0, keepdims=True))
            m_scr[...] = new
            probs = jnp.exp2((scores - new) * SCALE)
            factor = jnp.exp2((old - new) * SCALE)
            l_scr[...] = l_scr[...] * factor + jnp.sum(probs, axis=0, keepdims=True)
            acc_scr[...] = acc_scr[...] * factor + lax.dot_general(
                v_scr[pl.ds(at, CHUNK), :],
                probs.astype(jnp.bfloat16),
                (((0,), (0,)), ((), ())),
                preferred_element_type=jnp.float32,
            )
            return carry

        lax.fori_loop(0, steps, one_step, 0)
        total = jnp.where(l_scr[...] > 0, l_scr[...], 1.0)
        part = (acc_scr[...] / total).T.astype(jnp.bfloat16)
        lse = m_scr[...] * SCALE + jnp.log2(total)
        high = lse.astype(jnp.bfloat16).astype(jnp.float32)
        mid = (lse - high).astype(jnp.bfloat16).astype(jnp.float32)
        stats = (high, mid, lse - high - mid)
        xl4 = ((tile >> 1) ^ lax.axis_index("xl")) * 4
        half = tile & 1
        rows = pl.multiple_of(half * HALF, 16)
        for d in range(4):
            out_ref[xl4 + d, pl.ds(rows, HALF), :] = part[d * HALF : (d + 1) * HALF]
            for n, stat in enumerate(stats):
                if d % 2:
                    stat = pltpu.roll(
                        jnp.broadcast_to(stat, (8, TILE)), TILE - 64, 1
                    )[:1]
                base = d * HALF - (d % 2) * 64
                for w in range(2):
                    st_scr[xl4 + d, pl.ds(half * 6 + n * 2 + w, 1), :] = stat[
                        :, base + w * 128 : base + (w + 1) * 128
                    ]
        return carry

    lax.fori_loop(0, 4, one_tile, 0)
    for dest in range(TEAM_SIZE):
        out_ref[dest, TOK:, :] = st_scr[dest].astype(jnp.bfloat16)


def project_kernel(got_ref, w0_ref, w1_ref, out_ref, att_scr):
    for half in range(2):
        sides = []
        for w in range(2):
            lse = []
            for k in range(TEAM_SIZE):
                stat = got_ref[k, TOK:, :].astype(jnp.float32)
                row = half * 6 + w
                lse.append(
                    stat[row : row + 1] + stat[row + 2 : row + 3] + stat[row + 4 : row + 5]
                )
            lse = jnp.concatenate(lse, axis=0)
            weight = jnp.exp2(lse - jnp.max(lse, axis=0, keepdims=True))
            weight = weight / jnp.sum(weight, axis=0, keepdims=True)
            sides.append(weight.T)
        weight = jnp.concatenate([sides[0], sides[1][:64]], axis=0)
        total = jnp.zeros((HALF, HD), jnp.float32)
        for k in range(TEAM_SIZE):
            total += weight[:, k : k + 1] * got_ref[
                k, half * HALF : (half + 1) * HALF, :
            ].astype(jnp.float32)
        att_scr[half] = total.astype(jnp.bfloat16)
    own = lax.axis_index("zl") * 2 + lax.axis_index("core")
    out = None
    for w_ref, part, flip in ((w0_ref, 0, 0), (w0_ref, 1, 2), (w1_ref, 0, 1), (w1_ref, 1, 3)):
        rows = pl.multiple_of((own ^ flip) * QUART, 16)
        att = jnp.concatenate(
            [att_scr[half, pl.ds(rows, QUART), :] for half in range(2)], axis=0
        )
        term = jnp.dot(att, w_ref[part], preferred_element_type=jnp.float32)
        out = term if out is None else out + term
    out_ref[...] = out.astype(jnp.bfloat16)


def per_device(queries, keys, values, block_of_slot, doc_lengths, out_weight):
    hbm = pl.BlockSpec(memory_space=pltpu.HBM)
    smem = pl.BlockSpec(memory_space=pltpu.SMEM)
    vmem = pl.BlockSpec(memory_space=pltpu.VMEM)
    spread = pl.pallas_call(
        spread_kernel,
        out_shape=jax.ShapeDtypeStruct((SRC, 4 * QUART, HD), jnp.bfloat16),
        in_specs=[hbm, hbm],
        out_specs=hbm,
        scratch_shapes=[
            pltpu.VMEM((4 * QUART, HD), jnp.bfloat16),
            pltpu.SemaphoreType.DMA((4,)),
            pltpu.SemaphoreType.DMA((SRC,)),
        ],
        name="spread",
    )(keys, values)
    spread, queries, out_weight = lax.optimization_barrier(
        (spread, queries, out_weight)
    )
    kv = lax.all_to_all(spread, KV_AXES, 0, 0, tiled=True)
    flip = [(0, 1), (1, 0)]
    q_side = lax.ppermute(queries, "xl", flip)
    w_side = lax.ppermute(out_weight, "zl", flip)
    q = jnp.concatenate([queries, q_side])
    q = lax.all_gather(q, ("zl", "core"), axis=0, tiled=True)
    q = q.reshape(4, 2, TOK, HD)
    w0 = jnp.stack([out_weight, w_side])
    w1 = lax.ppermute(w0, "core", flip)

    lane = np.arange(TILE)
    in_half = (lane % QUART) // 16 * 64 + lane // HALF * 16 + lane % 16
    i32 = jnp.int32
    rank, in_order, tiles, q_pos, q_start, q = pl.pallas_call(
        table_kernel,
        out_shape=(
            jax.ShapeDtypeStruct((PIECES + 1,), i32),
            jax.ShapeDtypeStruct((SLOTS,), i32),
            jax.ShapeDtypeStruct((4, 4), i32),
            jax.ShapeDtypeStruct((4, TILE), i32),
            jax.ShapeDtypeStruct((4, TILE), i32),
            jax.ShapeDtypeStruct((4, TILE, HD), jnp.bfloat16),
        ),
        in_specs=[smem, smem, vmem, vmem],
        out_specs=(smem, smem, smem, vmem, vmem, vmem),
        scratch_shapes=[
            pltpu.SMEM((2 * PIECES,), i32),
            pltpu.SMEM((2 * PIECES + 1,), i32),
        ],
        compiler_params=pltpu.CompilerParams(vmem_limit_bytes=8 << 20),
        name="tables",
    )(block_of_slot, doc_lengths, jnp.asarray(in_half[None, :], i32), q)
    kv, w1 = lax.optimization_barrier((kv, w1))

    sent = pl.pallas_call(
        attend_kernel,
        out_shape=jax.ShapeDtypeStruct((TEAM_SIZE, SEND, HD), jnp.bfloat16),
        in_specs=[smem, smem, smem, vmem, vmem, vmem, vmem],
        out_specs=vmem,
        scratch_shapes=[
            pltpu.VMEM((PAD, HD), jnp.int32),
            pltpu.VMEM((PAD, HD), jnp.bfloat16),
            pltpu.VMEM((PAD, HD), jnp.bfloat16),
            pltpu.VMEM((CHUNK, TILE), jnp.float32),
            pltpu.VMEM((1, TILE), jnp.float32),
            pltpu.VMEM((1, TILE), jnp.float32),
            pltpu.VMEM((HD, TILE), jnp.float32),
            pltpu.VMEM((TEAM_SIZE, STAT, HD), jnp.float32),
        ],
        compiler_params=pltpu.CompilerParams(vmem_limit_bytes=16 << 20),
        cost_estimate=pl.CostEstimate(
            flops=4 * 4 * TILE * KEYS * HD,
            transcendentals=4 * TILE * KEYS,
            bytes_accessed=4 << 20,
        ),
        name="attend",
    )(rank, in_order, tiles, kv, q, q_pos, q_start)
    got = lax.all_to_all(sent, TEAM, 0, 0, tiled=True)
    terms = pl.pallas_call(
        project_kernel,
        out_shape=jax.ShapeDtypeStruct((TOK // 4, out_weight.shape[1]), jnp.bfloat16),
        in_specs=[vmem, vmem, vmem],
        out_specs=vmem,
        scratch_shapes=[pltpu.VMEM((2, HALF, HD), jnp.bfloat16)],
        compiler_params=pltpu.CompilerParams(vmem_limit_bytes=16 << 20),
        name="project",
    )(got, w0, w1)
    parts = lax.all_to_all(terms.reshape(6, 16, -1), Z6, 0, 0, tiled=True)
    return jnp.sum(parts.astype(jnp.float32), axis=0).astype(jnp.bfloat16)


def solution(mesh):
    fine = Mesh(mesh.devices.reshape(SIZES), AXES)
    return jax.shard_map(
        per_device,
        mesh=fine,
        in_specs=(P(DP, HEAD), P(DP, None), P(DP, None), P(), P(), P(HEAD, None)),
        out_specs=P(DP + HEAD, None),
        check_vma=False,
    )
```

time: 115 us -> 105 us (0.913)
  the two profiles are of different devices: /device:TPU:6 before, /device:TPU:52 now
where the time goes in v2:
time: 105 us; the launch traced here: 104 us
  blocking collectives  61.1 us (58%)
  starting transfers between devices  19.2 us (18%)
  Pallas kernels  11.8 us (11%)
  waiting for transfers between devices  8.48 us (8%)
  local copies, waits for them, and re-layouts  2.73 us (3%)
    all_to_all x1, blocking collectives, per_device(): parts = lax.all_to_all(terms.reshape(6, 16, -1), Z6, 0, 0, tiled=True)  33.2 us
    all_to_all x1, blocking collectives, per_device(): got = lax.all_to_all(sent, TEAM, 0, 0, tiled=True)  15.3 us
    all_gather x1, blocking collectives, per_device(): q = lax.all_gather(q, ('zl', 'core'), axis=0, tiled=True)  12.7 us
    all_to_all x1, starting transfers between devices, per_device(): kv = lax.all_to_all(spread, KV_AXES, 0, 0, tiled=True)  9.94 us
    ppermute x1, waiting for transfers between devices, per_device(): q_side = lax.ppermute(queries, 'xl', flip)  6.51 us
    pallas_call x1, Pallas kernels, per_device(): pl.pallas_call(attend_kernel, out_shape=jax.ShapeDtypeStruct((TEAM_SIZE,...  6.44 us
    ppermute x1, starting transfers between devices, per_device(): w_side = lax.ppermute(out_weight, 'zl', flip)  4.28 us
    ppermute x1, starting transfers between devices, per_device(): q_side = lax.ppermute(queries, 'xl', flip)  3.11 us
  transfers between devices with their start and end apart: 4, of which 2 were waited for; matrix products, arithmetic and copies ran while one was open for 0% of the time, Pallas kernels for 2%

profile of v2, /device:TPU:52, one launch (start us, length us, event | category | flops | bytes accessed | tf_op | source)
XLA Modules:
  0.0 104.3 jit_solution(8334212192677036956)
XLA Ops:
  0.0 0.0 copy-start.5
  0.0 1.9 %spread.1 = bf16[16,192,128]{2,1,0:T(8,128)(2,1)} custom-call(bf16[384,384]{1,0:T(8,128)(2,1)} %k_hbm.1, bf16[384,384]{1,0:T(8,128)(2,1)} %v_hbm.1), custom_call_target="tpu_custom_call" | custom-call | tf_op jit(solution)/shard_map/spread/pallas_call | solution.py:276
  1.9 0.0 copy-done.5
  1.9 4.3 %collective-permute-start.1 = (bf16[128,2048]{1,0:T(8,128)(2,1)S(1)}, bf16[128,2048]{1,0:T(8,128)(2,1)S(1)}, u32[]{:S(2)}, u32[]{:S(2)}) collective-permute-start(bf16[128,2048]{1,0:T(8,128)(2,1)S(1)} %copy-done.5), channel_id=1, source_target_pairs={{0,2},{2,0},{1,3},{3,1},{4,6},{6,4},{5,7},{7,5},{8,10},{10,8},{9,1... | collective-permute-start | bytes 1572872 | tf_op jit(solution)/shard_map/ppermute | solution.py:294
  6.2 9.9 %all-to-all-start = ((bf16[16,192,128]{2,1,0:T(8,128)(2,1)}), bf16[16,192,128]{2,1,0:T(8,128)(2,1)S(1)}, u32[]{:S(2)}, u32[]{:S(2)}) async-start(bf16[16,192,128]{2,1,0:T(8,128)(2,1)} %spread.1), calls=%async_computation | async-start | bytes 1572864 | tf_op jit(solution)/shard_map/all_to_all | solution.py:291
  16.1 2.0 %collective-permute-done.1 = bf16[128,2048]{1,0:T(8,128)(2,1)S(1)} collective-permute-done((bf16[128,2048]{1,0:T(8,128)(2,1)S(1)}, bf16[128,2048]{1,0:T(8,128)(2,1)S(1)}, u32[]{:S(2)}, u32[]{:S(2)}) %collective-permute-start.1) | collective-permute-done | bytes 524320 | tf_op jit(solution)/shard_map/ppermute | solution.py:294
  18.1 0.0 copy-start.6
  18.1 0.1 pad_maximum_fusion.w0_ref
  18.2 1.9 %collective-permute-start.2 = (bf16[2,128,2048]{2,1,0:T(8,128)(2,1)S(1)}, bf16[2,128,2048]{2,1,0:T(8,128)(2,1)S(1)}, u32[]{:S(2)}, u32[]{:S(2)}) collective-permute-start(bf16[2,128,2048]{2,1,0:T(8,128)(2,1)S(1)} %pad_maximum_fusion.w0_ref), channel_id=1, source_target_pairs={{0,1},{1,0},{2,3},{3,2},{4,5},{5,4},{6,7},{7,6},{8,9},{9,8},{10,11... | collective-permute-start | bytes 3145736 | tf_op jit(solution)/shard_map/ppermute | solution.py:299
  20.1 0.0 copy-done.6
  20.1 3.1 %collective-permute-start = (bf16[384,128]{1,0:T(8,128)(2,1)S(1)}, bf16[384,128]{1,0:T(8,128)(2,1)S(1)}, u32[]{:S(2)}, u32[]{:S(2)}) collective-permute-start(bf16[384,128]{1,0:T(8,128)(2,1)S(1)} %copy-done.6), channel_id=1, source_target_pairs={{0,24},{24,0},{1,25},{25,1},{2,26},{26,2},{3,27},{27,3},{4,28},{28... | collective-permute-start | bytes 294920 | tf_op jit(solution)/shard_map/ppermute | solution.py:293
  23.2 6.5 %collective-permute-done = bf16[384,128]{1,0:T(8,128)(2,1)S(1)} collective-permute-done((bf16[384,128]{1,0:T(8,128)(2,1)S(1)}, bf16[384,128]{1,0:T(8,128)(2,1)S(1)}, u32[]{:S(2)}, u32[]{:S(2)}) %collective-permute-start) | collective-permute-done | bytes 98336 | tf_op jit(solution)/shard_map/ppermute | solution.py:293
  29.8 0.0 copy-start
  29.8 12.7 %all_gather.3 = bf16[3072,128]{1,0:T(8,128)(2,1)S(1)} all-gather(bf16[768,128]{1,0:T(8,128)(2,1)S(1)} %pad_maximum_fusion.1), channel_id=1, replica_groups=mesh['y'=8,'xh'=2,'xl'=2,'zh'=3,'zm'=2,'zl'=2,'core'=2] {'zl','core'}, dimensions={0}, use_global_device_ids=true | all-gather | bytes 983040 | tf_op jit(solution)/shard_map/all_gather | solution.py:296
  42.5 0.0 copy-start.1
  42.5 0.0 copy-start.2
  42.5 0.0 copy-done
  42.5 0.6 copy-done.1
  43.1 0.0 copy-done.2
  43.1 2.2 %tables.1 = (s32[33]{0:T(128)S(1)}, s32[39]{0:T(128)S(1)}, s32[4,4]{1,0:T(4,128)S(1)}, s32[4,768]{1,0:T(4,128)S(1)}, s32[4,768]{1,0:T(4,128)S(1)}, /*index=5*/bf16[4,768,128]{2,1,0:T(8,128)(2,1)S(1)}) custom-call(s32[64]{0:T(128)S(1)} %copy-done.1, s32[4]{0:T(128)S(1)} %copy-done.2, s32[1,768]{1,0:T(1,128)S(1)} %copy-done, bf16[4,2,384,128]{3,2,1,0:T(8,128)(2,1)S(1)} %bitcast.4), custom_call_target="tpu_custom_call" | custom-call | tf_op jit(solution)/shard_map/tables/pallas_call | solution.py:304
  45.3 0.0 copy-start.3
  45.4 0.9 copy-done.3
  46.3 0.0 all-to-all-done.kv_ref
  46.3 0.0 collective-permute-done.2.w1_ref
  46.3 0.0 copy-start.4
  46.3 1.1 %copy-done.4 = bf16[4,768,128]{2,1,0:T(8,128)(2,1)S(1)} copy-done((bf16[4,768,128]{2,1,0:T(8,128)(2,1)S(1)}, bf16[4,768,128]{2,1,0:T(8,128)(2,1)}, u32[]{:S(2)}) %copy-start.4) | copy-done | bytes 786456
  47.4 6.4 %attend.1 = bf16[8,400,128]{2,1,0:T(8,128)(2,1)S(1)} custom-call(s32[33]{0:T(128)S(1)} %get-tuple-element.17.rank_ref, s32[39]{0:T(128)S(1)} %get-tuple-element.18.sorted_ref, s32[4,4]{1,0:T(4,128)S(1)} %get-tuple-element.19.tile_ref, bf16[16,192,128]{2,1,0:T(8,128)(2,1)S(1)} %all-to-all-done.kv_ref, bf16[4,768,128]{2,1,0:T(8,128)(2,1)S(1)} %copy-done.4, ...), custom_call_target="tpu_custom_call" | custom-call | flops 2415919104 | bytes 4194304 | tf_op jit(solution)/shard_map/attend/pallas_call | solution.py:325
  53.8 15.3 %all_to_all.15.got_ref = bf16[8,400,128]{2,1,0:T(8,128)(2,1)S(1)} all-to-all(bf16[8,400,128]{2,1,0:T(8,128)(2,1)S(1)} %attend.1), channel_id=1, replica_groups=mesh['y'=8,'xh'=2,'xl'=2,'zh'=3,'zm'=2,'zl'=2,'core'=2] {'xl','zl','core'}, dimensions={0} | all-to-all | bytes 1638400 | tf_op jit(solution)/shard_map/all_to_all | solution.py:348
  69.1 1.3 %project.1 = bf16[96,2048]{1,0:T(8,128)(2,1)S(1)} custom-call(bf16[8,400,128]{2,1,0:T(8,128)(2,1)S(1)} %all_to_all.15.got_ref, bf16[2,128,2048]{2,1,0:T(8,128)(2,1)S(1)} %pad_maximum_fusion.w0_ref, bf16[2,128,2048]{2,1,0:T(8,128)(2,1)S(1)} %collective-permute-done.2.w1_ref), custom_call_target="tpu_custom_call" | custom-call | tf_op jit(solution)/shard_map/project/pallas_call | solution.py:349
  70.4 33.2 %all_to_all.16 = bf16[6,16,2048]{2,1,0:T(8,128)(2,1)S(1)} all-to-all(bf16[6,16,2048]{2,1,0:T(8,128)(2,1)S(1)} %bitcast.5), channel_id=1, replica_groups=mesh['y'=8,'xh'=2,'xl'=2,'zh'=3,'zm'=2,'zl'=2,'core'=2] {'zh','zm'}, dimensions={0} | all-to-all | bytes 786432 | tf_op jit(solution)/shard_map/all_to_all | solution.py:358
  103.6 0.7 reduce_sum.12
  (1 shorter events, 0.0 us)
Async XLA Ops:
  0.0 1.9 %copy-start.5 = (bf16[128,2048]{1,0:T(8,128)(2,1)S(1)}, bf16[128,2048]{1,0:T(8,128)(2,1)}, u32[]{:S(2)}) copy-start(bf16[128,2048]{1,0:T(8,128)(2,1)} %param.12) | copy-start | bytes 1572868
  1.9 16.2 %collective-permute-start.1 = (bf16[128,2048]{1,0:T(8,128)(2,1)S(1)}, bf16[128,2048]{1,0:T(8,128)(2,1)S(1)}, u32[]{:S(2)}, u32[]{:S(2)}) collective-permute-start(bf16[128,2048]{1,0:T(8,128)(2,1)S(1)} %copy-done.5), channel_id=1, source_target_pairs={{0,2},{2,0},{1,3},{3,1},{4,6},{6,4},{5,7},{7,5},{8,10},{10,8},{9,1... | collective-permute-start | bytes 1572872 | tf_op jit(solution)/shard_map/ppermute | solution.py:294
  6.2 40.1 %all-to-all-start = ((bf16[16,192,128]{2,1,0:T(8,128)(2,1)}), bf16[16,192,128]{2,1,0:T(8,128)(2,1)S(1)}, u32[]{:S(2)}, u32[]{:S(2)}) async-start(bf16[16,192,128]{2,1,0:T(8,128)(2,1)} %spread.1), calls=%async_computation | async-start | bytes 1572864 | tf_op jit(solution)/shard_map/all_to_all | solution.py:291
  18.1 2.0 %copy-start.6 = (bf16[384,128]{1,0:T(8,128)(2,1)S(1)}, bf16[384,128]{1,0:T(8,128)(2,1)}, u32[]{:S(2)}) copy-start(bf16[384,128]{1,0:T(8,128)(2,1)} %param.7) | copy-start | bytes 294916
  18.2 28.1 %collective-permute-start.2 = (bf16[2,128,2048]{2,1,0:T(8,128)(2,1)S(1)}, bf16[2,128,2048]{2,1,0:T(8,128)(2,1)S(1)}, u32[]{:S(2)}, u32[]{:S(2)}) collective-permute-start(bf16[2,128,2048]{2,1,0:T(8,128)(2,1)S(1)} %pad_maximum_fusion.w0_ref), channel_id=1, source_target_pairs={{0,1},{1,0},{2,3},{3,2},{4,5},{5,4},{6,7},{7,6},{8,9},{9,8},{10,11... | collective-permute-start | bytes 3145736 | tf_op jit(solution)/shard_map/ppermute | solution.py:299
  20.1 9.6 %collective-permute-start = (bf16[384,128]{1,0:T(8,128)(2,1)S(1)}, bf16[384,128]{1,0:T(8,128)(2,1)S(1)}, u32[]{:S(2)}, u32[]{:S(2)}) collective-permute-start(bf16[384,128]{1,0:T(8,128)(2,1)S(1)} %copy-done.6), channel_id=1, source_target_pairs={{0,24},{24,0},{1,25},{25,1},{2,26},{26,2},{3,27},{27,3},{4,28},{28... | collective-permute-start | bytes 294920 | tf_op jit(solution)/shard_map/ppermute | solution.py:293
  29.8 12.7 %copy-start = (s32[1,768]{1,0:T(1,128)S(1)}, s32[1,768]{1,0:T(1,128)}, u32[]{:S(2)}) copy-start(s32[1,768]{1,0:T(1,128)} %constant.5.clone.lane_ref) | copy-start | bytes 9220
  42.5 0.7 copy-start.1
  42.5 0.7 copy-start.2
  45.3 0.9 copy-start.3
  46.3 1.1 %copy-start.4 = (bf16[4,768,128]{2,1,0:T(8,128)(2,1)S(1)}, bf16[4,768,128]{2,1,0:T(8,128)(2,1)}, u32[]{:S(2)}) copy-start(bf16[4,768,128]{2,1,0:T(8,128)(2,1)} %copy-done.3) | copy-start | bytes 2359300

commit v3 on v2

--- a/solution.py
+++ b/solution.py
@@ -73,13 +73,11 @@
     slot_ref,
     len_ref,
     lane_ref,
-    q_ref,
     rank_ref,
     sorted_ref,
     tile_ref,
     qpos_ref,
     qstart_ref,
-    tiles_ref,
     where_scr,
     before_scr,
 ):
@@ -122,12 +120,6 @@
         pos = lane + base
         qpos_ref[tile : tile + 1, :] = pos
         qstart_ref[tile : tile + 1, :] = start_of(pos, bounds)
-        for d in range(4):
-            for j in range(4):
-                for z3 in range(3):
-                    to = d * HALF + j * QUART + z3 * 16
-                    of = half * HALF + z3 * 64 + d * 16
-                    tiles_ref[tile, to : to + 16, :] = q_ref[j, rel, of : of + 16, :]
 
 
 def attend_kernel(
@@ -135,13 +127,15 @@
     sorted_ref,
     tile_ref,
     kv_ref,
-    q_ref,
+    q_own_ref,
+    q_side_ref,
     qpos_ref,
     qstart_ref,
     out_ref,
     kpos_scr,
     k_scr,
     v_scr,
+    q_scr,
     s_scr,
     m_scr,
     l_scr,
@@ -164,6 +158,16 @@
         kpos_scr[n * QUART : (n + 1) * QUART, :] = row + sorted_ref[n] * HALF
     kpos_scr[KEYS:, :] = jnp.full((PAD - KEYS, HD), FAR, jnp.int32)
 
+    for tile in range(4):
+        q_ref = (q_own_ref, q_side_ref)[tile // 2]
+        half = tile % 2
+        for d in range(4):
+            for j in range(4):
+                for z3 in range(3):
+                    to = d * HALF + j * QUART + z3 * 16
+                    of = j * TOK + half * HALF + z3 * 64 + d * 16
+                    q_scr[tile, to : to + 16, :] = q_ref[of : of + 16, :]
+
     def one_tile(tile, carry):
         low, steps, q_first, start_last = (tile_ref[tile, n] for n in range(4))
         m_scr[...] = jnp.full_like(m_scr, LOW)
@@ -175,7 +179,7 @@
             at = pl.multiple_of(first, 16)
             s_scr[...] = lax.dot_general(
                 k_scr[pl.ds(at, CHUNK), :],
-                q_ref[tile],
+                q_scr[tile],
                 (((1,), (1,)), ((), ())),
                 preferred_element_type=jnp.float32,
             )
@@ -290,18 +294,16 @@
     )
     kv = lax.all_to_all(spread, KV_AXES, 0, 0, tiled=True)
     flip = [(0, 1), (1, 0)]
-    q_side = lax.ppermute(queries, "xl", flip)
+    q = lax.all_gather(queries, ("zl", "core"), axis=0, tiled=True)
+    q_side = lax.ppermute(q, "xl", flip)
     w_side = lax.ppermute(out_weight, "zl", flip)
-    q = jnp.concatenate([queries, q_side])
-    q = lax.all_gather(q, ("zl", "core"), axis=0, tiled=True)
-    q = q.reshape(4, 2, TOK, HD)
     w0 = jnp.stack([out_weight, w_side])
     w1 = lax.ppermute(w0, "core", flip)
 
     lane = np.arange(TILE)
     in_half = (lane % QUART) // 16 * 64 + lane // HALF * 16 + lane % 16
     i32 = jnp.int32
-    rank, in_order, tiles, q_pos, q_start, q = pl.pallas_call(
+    rank, in_order, tiles, q_pos, q_start = pl.pallas_call(
         table_kernel,
         out_shape=(
             jax.ShapeDtypeStruct((PIECES + 1,), i32),
@@ -309,28 +311,28 @@
             jax.ShapeDtypeStruct((4, 4), i32),
             jax.ShapeDtypeStruct((4, TILE), i32),
             jax.ShapeDtypeStruct((4, TILE), i32),
-            jax.ShapeDtypeStruct((4, TILE, HD), jnp.bfloat16),
         ),
-        in_specs=[smem, smem, vmem, vmem],
-        out_specs=(smem, smem, smem, vmem, vmem, vmem),
+        in_specs=[smem, smem, vmem],
+        out_specs=(smem, smem, smem, vmem, vmem),
         scratch_shapes=[
             pltpu.SMEM((2 * PIECES,), i32),
             pltpu.SMEM((2 * PIECES + 1,), i32),
         ],
         compiler_params=pltpu.CompilerParams(vmem_limit_bytes=8 << 20),
         name="tables",
-    )(block_of_slot, doc_lengths, jnp.asarray(in_half[None, :], i32), q)
+    )(block_of_slot, doc_lengths, jnp.asarray(in_half[None, :], i32))
     kv, w1 = lax.optimization_barrier((kv, w1))
 
     sent = pl.pallas_call(
         attend_kernel,
         out_shape=jax.ShapeDtypeStruct((TEAM_SIZE, SEND, HD), jnp.bfloat16),
-        in_specs=[smem, smem, smem, vmem, vmem, vmem, vmem],
+        in_specs=[smem, smem, smem, vmem, vmem, vmem, vmem, vmem],
         out_specs=vmem,
         scratch_shapes=[
             pltpu.VMEM((PAD, HD), jnp.int32),
             pltpu.VMEM((PAD, HD), jnp.bfloat16),
             pltpu.VMEM((PAD, HD), jnp.bfloat16),
+            pltpu.VMEM((4, TILE, HD), jnp.bfloat16),
             pltpu.VMEM((CHUNK, TILE), jnp.float32),
             pltpu.VMEM((1, TILE), jnp.float32),
             pltpu.VMEM((1, TILE), jnp.float32),
@@ -344,7 +346,7 @@
             bytes_accessed=4 << 20,
         ),
         name="attend",
-    )(rank, in_order, tiles, kv, q, q_pos, q_start)
+    )(rank, in_order, tiles, kv, q, q_side, q_pos, q_start)
     got = lax.all_to_all(sent, TEAM, 0, 0, tiled=True)
     terms = pl.pallas_call(
         project_kernel,

time: 105 us -> 102 us (0.971)
  the two profiles are of different devices: /device:TPU:52 before, /device:TPU:6 now
where the time goes in v3:
time: 102 us; the launch traced here: 100 us
  blocking collectives  54 us (53%)
  starting transfers between devices  19.1 us (19%)
  waiting for transfers between devices  14 us (14%)
  Pallas kernels  12.3 us (12%)
    all_to_all x1, blocking collectives, per_device(): parts = lax.all_to_all(terms.reshape(6, 16, -1), Z6, 0, 0, tiled=True)  32.6 us
    all_to_all x1, blocking collectives, per_device(): got = lax.all_to_all(sent, TEAM, 0, 0, tiled=True)  14.7 us
    all_to_all x1, starting transfers between devices, per_device(): kv = lax.all_to_all(spread, KV_AXES, 0, 0, tiled=True)  10.1 us
    pallas_call x1, Pallas kernels, per_device(): pl.pallas_call(attend_kernel, out_shape=jax.ShapeDtypeStruct((TEAM_SIZE,...  7.02 us
    all_gather x1, blocking collectives, per_device(): q = lax.all_gather(queries, ('zl', 'core'), axis=0, tiled=True)  6.72 us
    ppermute x1, waiting for transfers between devices, per_device(): q_side = lax.ppermute(q, 'xl', flip)  6.31 us
    all_to_all x1, waiting for transfers between devices, per_device(): kv = lax.all_to_all(spread, KV_AXES, 0, 0, tiled=True)  5.88 us
    ppermute x1, starting transfers between devices, per_device(): w_side = lax.ppermute(out_weight, 'zl', flip)  4.28 us
  transfers between devices with their start and end apart: 4, of which 3 were waited for; matrix products, arithmetic and copies ran while one was open for 0% of the time, Pallas kernels for 2%

profile of v3, /device:TPU:6, one launch (start us, length us, event | category | flops | bytes accessed | tf_op | source)
XLA Modules:
  0.0 100.4 jit_solution(3434420135305373715)
XLA Ops:
  0.0 0.0 copy-start.3
  0.0 1.9 %spread.1 = bf16[16,192,128]{2,1,0:T(8,128)(2,1)} custom-call(bf16[384,384]{1,0:T(8,128)(2,1)} %k_hbm.1, bf16[384,384]{1,0:T(8,128)(2,1)} %v_hbm.1), custom_call_target="tpu_custom_call" | custom-call | tf_op jit(solution)/shard_map/spread/pallas_call | solution.py:280
  1.9 0.0 copy-done.3
  1.9 4.3 %collective-permute-start = (bf16[128,2048]{1,0:T(8,128)(2,1)S(1)}, bf16[128,2048]{1,0:T(8,128)(2,1)S(1)}, u32[]{:S(2)}, u32[]{:S(2)}) collective-permute-start(bf16[128,2048]{1,0:T(8,128)(2,1)S(1)} %copy-done.3), channel_id=1, source_target_pairs={{0,2},{2,0},{1,3},{3,1},{4,6},{6,4},{5,7},{7,5},{8,10},{10,8},{9,1... | collective-permute-start | bytes 1572872 | tf_op jit(solution)/shard_map/ppermute | solution.py:299
  6.2 10.1 %all-to-all-start = ((bf16[16,192,128]{2,1,0:T(8,128)(2,1)}), bf16[16,192,128]{2,1,0:T(8,128)(2,1)S(1)}, u32[]{:S(2)}, u32[]{:S(2)}) async-start(bf16[16,192,128]{2,1,0:T(8,128)(2,1)} %spread.1), calls=%async_computation | async-start | bytes 1572864 | tf_op jit(solution)/shard_map/all_to_all | solution.py:295
  16.3 1.8 %collective-permute-done = bf16[128,2048]{1,0:T(8,128)(2,1)S(1)} collective-permute-done((bf16[128,2048]{1,0:T(8,128)(2,1)S(1)}, bf16[128,2048]{1,0:T(8,128)(2,1)S(1)}, u32[]{:S(2)}, u32[]{:S(2)}) %collective-permute-start) | collective-permute-done | bytes 524320 | tf_op jit(solution)/shard_map/ppermute | solution.py:299
  18.1 0.0 copy-start.4
  18.1 0.1 pad_maximum_fusion.w0_ref
  18.2 0.0 copy-start
  18.2 0.0 copy-start.1
  18.2 0.0 copy-start.2
  18.2 2.1 %collective-permute-start.1 = (bf16[2,128,2048]{2,1,0:T(8,128)(2,1)S(1)}, bf16[2,128,2048]{2,1,0:T(8,128)(2,1)S(1)}, u32[]{:S(2)}, u32[]{:S(2)}) collective-permute-start(bf16[2,128,2048]{2,1,0:T(8,128)(2,1)S(1)} %pad_maximum_fusion.w0_ref), channel_id=1, source_target_pairs={{0,1},{1,0},{2,3},{3,2},{4,5},{5,4},{6,7},{7,6},{8,9},{9,8},{10,11... | collective-permute-start | bytes 3145736 | tf_op jit(solution)/shard_map/ppermute | solution.py:301
  20.3 0.0 copy-done.4
  20.3 6.7 %all_gather.3.q_own_ref = bf16[1536,128]{1,0:T(8,128)(2,1)S(1)} all-gather(bf16[384,128]{1,0:T(8,128)(2,1)S(1)} %copy-done.4), channel_id=1, replica_groups=mesh['y'=8,'xh'=2,'xl'=2,'zh'=3,'zm'=2,'zl'=2,'core'=2] {'zl','core'}, dimensions={0}, use_global_device_ids=true | all-gather | bytes 491520 | tf_op jit(solution)/shard_map/all_gather | solution.py:297
  27.0 2.7 %collective-permute-start.2 = (bf16[1536,128]{1,0:T(8,128)(2,1)S(1)}, bf16[1536,128]{1,0:T(8,128)(2,1)}, u32[]{:S(2)}, u32[]{:S(2)}) collective-permute-start(bf16[1536,128]{1,0:T(8,128)(2,1)S(1)} %all_gather.3.q_own_ref), channel_id=1, source_target_pairs={{0,24},{24,0},{1,25},{25,1},{2,26},{26,2},{3,27},{27,3},{4,28},{28... | collective-permute-start | bytes 1179656 | tf_op jit(solution)/shard_map/ppermute | solution.py:298
  29.8 0.0 copy-done
  29.8 0.0 copy-done.1
  29.8 0.0 copy-done.2
  29.8 2.1 %tables.1 = (s32[33]{0:T(128)S(1)}, s32[39]{0:T(128)S(1)}, s32[4,4]{1,0:T(4,128)S(1)}, s32[4,768]{1,0:T(4,128)S(1)}, s32[4,768]{1,0:T(4,128)S(1)}) custom-call(s32[64]{0:T(128)S(1)} %copy-done.1, s32[4]{0:T(128)S(1)} %copy-done.2, s32[1,768]{1,0:T(1,128)S(1)} %copy-done), custom_call_target="tpu_custom_call" | custom-call | tf_op jit(solution)/shard_map/tables/pallas_call | solution.py:306
  31.9 5.9 %all-to-all-done.kv_ref = bf16[16,192,128]{2,1,0:T(8,128)(2,1)S(1)} async-done(((bf16[16,192,128]{2,1,0:T(8,128)(2,1)}), bf16[16,192,128]{2,1,0:T(8,128)(2,1)S(1)}, u32[]{:S(2)}, u32[]{:S(2)}) %all-to-all-start) | async-done | bytes 786464 | tf_op jit(solution)/shard_map/all_to_all | solution.py:295
  37.8 0.0 collective-permute-done.1.w1_ref
  37.8 6.3 %collective-permute-done.2.q_side_ref = bf16[1536,128]{1,0:T(8,128)(2,1)} collective-permute-done((bf16[1536,128]{1,0:T(8,128)(2,1)S(1)}, bf16[1536,128]{1,0:T(8,128)(2,1)}, u32[]{:S(2)}, u32[]{:S(2)}) %collective-permute-start.2) | collective-permute-done | bytes 393248 | tf_op jit(solution)/shard_map/ppermute | solution.py:298
  44.1 7.0 %attend.1 = bf16[8,400,128]{2,1,0:T(8,128)(2,1)S(1)} custom-call(s32[33]{0:T(128)S(1)} %get-tuple-element.15.rank_ref, s32[39]{0:T(128)S(1)} %get-tuple-element.16.sorted_ref, s32[4,4]{1,0:T(4,128)S(1)} %get-tuple-element.17.tile_ref, bf16[16,192,128]{2,1,0:T(8,128)(2,1)S(1)} %all-to-all-done.kv_ref, bf16[1536,128]{1,0:T(8,128)(2,1)S(1)} %all_gather.3.q_own_ref, ...), custom_call_target="tpu_custom_call" | custom-call | flops 2415919104 | bytes 4194304 | tf_op jit(solution)/shard_map/attend/pallas_call | solution.py:326
  51.1 14.7 %all_to_all.15.got_ref = bf16[8,400,128]{2,1,0:T(8,128)(2,1)S(1)} all-to-all(bf16[8,400,128]{2,1,0:T(8,128)(2,1)S(1)} %attend.1), channel_id=1, replica_groups=mesh['y'=8,'xh'=2,'xl'=2,'zh'=3,'zm'=2,'zl'=2,'core'=2] {'xl','zl','core'}, dimensions={0} | all-to-all | bytes 1638400 | tf_op jit(solution)/shard_map/all_to_all | solution.py:350
  65.8 1.3 %project.1 = bf16[96,2048]{1,0:T(8,128)(2,1)S(1)} custom-call(bf16[8,400,128]{2,1,0:T(8,128)(2,1)S(1)} %all_to_all.15.got_ref, bf16[2,128,2048]{2,1,0:T(8,128)(2,1)S(1)} %pad_maximum_fusion.w0_ref, bf16[2,128,2048]{2,1,0:T(8,128)(2,1)S(1)} %collective-permute-done.1.w1_ref), custom_call_target="tpu_custom_call" | custom-call | tf_op jit(solution)/shard_map/project/pallas_call | solution.py:351
  67.1 32.6 %all_to_all.16 = bf16[6,16,2048]{2,1,0:T(8,128)(2,1)S(1)} all-to-all(bf16[6,16,2048]{2,1,0:T(8,128)(2,1)S(1)} %bitcast.3), channel_id=1, replica_groups=mesh['y'=8,'xh'=2,'xl'=2,'zh'=3,'zm'=2,'zl'=2,'core'=2] {'zh','zm'}, dimensions={0} | all-to-all | bytes 786432 | tf_op jit(solution)/shard_map/all_to_all | solution.py:360
  99.7 0.7 reduce_sum.12
Async XLA Ops:
  0.0 1.9 %copy-start.3 = (bf16[128,2048]{1,0:T(8,128)(2,1)S(1)}, bf16[128,2048]{1,0:T(8,128)(2,1)}, u32[]{:S(2)}) copy-start(bf16[128,2048]{1,0:T(8,128)(2,1)} %param.12) | copy-start | bytes 1572868
  1.9 16.2 %collective-permute-start = (bf16[128,2048]{1,0:T(8,128)(2,1)S(1)}, bf16[128,2048]{1,0:T(8,128)(2,1)S(1)}, u32[]{:S(2)}, u32[]{:S(2)}) collective-permute-start(bf16[128,2048]{1,0:T(8,128)(2,1)S(1)} %copy-done.3), channel_id=1, source_target_pairs={{0,2},{2,0},{1,3},{3,1},{4,6},{6,4},{5,7},{7,5},{8,10},{10,8},{9,1... | collective-permute-start | bytes 1572872 | tf_op jit(solution)/shard_map/ppermute | solution.py:299
  6.2 31.6 %all-to-all-start = ((bf16[16,192,128]{2,1,0:T(8,128)(2,1)}), bf16[16,192,128]{2,1,0:T(8,128)(2,1)S(1)}, u32[]{:S(2)}, u32[]{:S(2)}) async-start(bf16[16,192,128]{2,1,0:T(8,128)(2,1)} %spread.1), calls=%async_computation | async-start | bytes 1572864 | tf_op jit(solution)/shard_map/all_to_all | solution.py:295
  18.1 2.2 %copy-start.4 = (bf16[384,128]{1,0:T(8,128)(2,1)S(1)}, bf16[384,128]{1,0:T(8,128)(2,1)}, u32[]{:S(2)}) copy-start(bf16[384,128]{1,0:T(8,128)(2,1)} %param.7) | copy-start | bytes 294916
  18.2 11.6 %copy-start = (s32[1,768]{1,0:T(1,128)S(1)}, s32[1,768]{1,0:T(1,128)}, u32[]{:S(2)}) copy-start(s32[1,768]{1,0:T(1,128)} %constant.5.clone.lane_ref) | copy-start | bytes 9220
  18.2 11.6 %copy-start.1 = (s32[64]{0:T(128)S(1)}, s32[64]{0:T(128)}, u32[]{:S(2)}) copy-start(s32[64]{0:T(128)} %slot_ref.1) | copy-start | bytes 772
  18.2 11.6 %copy-start.2 = (s32[4]{0:T(128)S(1)}, s32[4]{0:T(128)}, u32[]{:S(2)}) copy-start(s32[4]{0:T(128)} %len_ref.1) | copy-start | bytes 52
  18.2 19.6 %collective-permute-start.1 = (bf16[2,128,2048]{2,1,0:T(8,128)(2,1)S(1)}, bf16[2,128,2048]{2,1,0:T(8,128)(2,1)S(1)}, u32[]{:S(2)}, u32[]{:S(2)}) collective-permute-start(bf16[2,128,2048]{2,1,0:T(8,128)(2,1)S(1)} %pad_maximum_fusion.w0_ref), channel_id=1, source_target_pairs={{0,1},{1,0},{2,3},{3,2},{4,5},{5,4},{6,7},{7,6},{8,9},{9,8},{10,11... | collective-permute-start | bytes 3145736 | tf_op jit(solution)/shard_map/ppermute | solution.py:301
  27.0 17.1 %collective-permute-start.2 = (bf16[1536,128]{1,0:T(8,128)(2,1)S(1)}, bf16[1536,128]{1,0:T(8,128)(2,1)}, u32[]{:S(2)}, u32[]{:S(2)}) collective-permute-start(bf16[1536,128]{1,0:T(8,128)(2,1)S(1)} %all_gather.3.q_own_ref), channel_id=1, source_target_pairs={{0,24},{24,0},{1,25},{25,1},{2,26},{26,2},{3,27},{27,3},{4,28},{28... | collective-permute-start | bytes 1179656 | tf_op jit(solution)/shard_map/ppermute | solution.py:298

commit v4 on v3

--- a/solution.py
+++ b/solution.py
@@ -294,11 +294,10 @@
     )
     kv = lax.all_to_all(spread, KV_AXES, 0, 0, tiled=True)
     flip = [(0, 1), (1, 0)]
+    q_side = lax.ppermute(queries, "xl", flip)
     q = lax.all_gather(queries, ("zl", "core"), axis=0, tiled=True)
-    q_side = lax.ppermute(q, "xl", flip)
+    q_side = lax.all_gather(q_side, ("zl", "core"), axis=0, tiled=True)
     w_side = lax.ppermute(out_weight, "zl", flip)
-    w0 = jnp.stack([out_weight, w_side])
-    w1 = lax.ppermute(w0, "core", flip)
 
     lane = np.arange(TILE)
     in_half = (lane % QUART) // 16 * 64 + lane // HALF * 16 + lane % 16
@@ -321,7 +320,6 @@
         compiler_params=pltpu.CompilerParams(vmem_limit_bytes=8 << 20),
         name="tables",
     )(block_of_slot, doc_lengths, jnp.asarray(in_half[None, :], i32))
-    kv, w1 = lax.optimization_barrier((kv, w1))
 
     sent = pl.pallas_call(
         attend_kernel,
@@ -347,7 +345,10 @@
         ),
         name="attend",
     )(rank, in_order, tiles, kv, q, q_side, q_pos, q_start)
+    sent, w_side = lax.optimization_barrier((sent, w_side))
     got = lax.all_to_all(sent, TEAM, 0, 0, tiled=True)
+    w0 = jnp.stack([out_weight, w_side])
+    w1 = lax.ppermute(w0, "core", flip)
     terms = pl.pallas_call(
         project_kernel,
         out_shape=jax.ShapeDtypeStruct((TOK // 4, out_weight.shape[1]), jnp.bfloat16),

time: 102 us -> 95 us (0.931)
  blocking collectives: 54 us -> 47 us
  starting transfers between devices: 19.1 us -> 24.1 us
  waiting for transfers between devices: 14 us -> 9.33 us
    all_to_all x1 -> x0, blocking collectives: 14.7 us -> none  [per_device(): got = lax.all_to_all(sent, TEAM, 0, 0, tiled=True)]
    all_to_all x0 -> x1, waiting for transfers between devices: none -> 6.8 us  [per_device(): got = lax.all_to_all(sent, TEAM, 0, 0, tiled=True)]
    all_gather x0 -> x1, blocking collectives: none -> 6.69 us  [per_device(): q_side = lax.all_gather(q_side, ('zl', 'core'), axis=0, tiled=True)]
    ppermute x1, waiting for transfers between devices: 6.31 us -> 0.01 us  [per_device(): q_side = lax.ppermute(queries, 'xl', flip)]
    all_to_all x1, waiting for transfers between devices: 5.88 us -> 0.01 us  [per_device(): kv = lax.all_to_all(spread, KV_AXES, 0, 0, tiled=True)]
    all_to_all x0 -> x1, starting transfers between devices: none -> 4.34 us  [per_device(): got = lax.all_to_all(sent, TEAM, 0, 0, tiled=True)]
    ppermute x1, waiting for transfers between devices: 0.01 us -> 2.52 us  [per_device(): w1 = lax.ppermute(w0, 'core', flip)]
    all_gather x1, blocking collectives: 6.72 us -> 8.93 us  [per_device(): q = lax.all_gather(queries, ('zl', 'core'), axis=0, tiled=True)]
  transfers between devices with their start and end apart: 4 -> 5, of which waited for: 3 -> 2; matrix products, arithmetic and copies ran while one was open for 0% -> 0% of each run, Pallas kernels for 2% -> 10%
where the time goes in v4:
time: 95 us; the launch traced here: 94.1 us
  blocking collectives  47 us (49%)
  starting transfers between devices  24.1 us (25%)
  Pallas kernels  12.7 us (13%)
  waiting for transfers between devices  9.33 us (10%)
    all_to_all x1, blocking collectives, per_device(): parts = lax.all_to_all(terms.reshape(6, 16, -1), Z6, 0, 0, tiled=True)  31.4 us
    all_to_all x1, starting transfers between devices, per_device(): kv = lax.all_to_all(spread, KV_AXES, 0, 0, tiled=True)  10.2 us
    all_gather x1, blocking collectives, per_device(): q = lax.all_gather(queries, ('zl', 'core'), axis=0, tiled=True)  8.93 us
    pallas_call x1, Pallas kernels, per_device(): pl.pallas_call(attend_kernel, out_shape=jax.ShapeDtypeStruct((TEAM_SIZE,...  7.49 us
    all_to_all x1, waiting for transfers between devices, per_device(): got = lax.all_to_all(sent, TEAM, 0, 0, tiled=True)  6.8 us
    all_gather x1, blocking collectives, per_device(): q_side = lax.all_gather(q_side, ('zl', 'core'), axis=0, tiled=True)  6.69 us
    all_to_all x1, starting transfers between devices, per_device(): got = lax.all_to_all(sent, TEAM, 0, 0, tiled=True)  4.34 us
    ppermute x1, starting transfers between devices, per_device(): w_side = lax.ppermute(out_weight, 'zl', flip)  4.28 us
  transfers between devices with their start and end apart: 5, of which 2 were waited for; matrix products, arithmetic and copies ran while one was open for 0% of the time, Pallas kernels for 10%

profile of v4, /device:TPU:6, one launch (start us, length us, event | category | flops | bytes accessed | tf_op | source)
XLA Modules:
  0.0 94.1 jit_solution(1944069548491870999)
XLA Ops:
  0.0 1.8 %spread.1 = bf16[16,192,128]{2,1,0:T(8,128)(2,1)} custom-call(bf16[384,384]{1,0:T(8,128)(2,1)} %k_hbm.1, bf16[384,384]{1,0:T(8,128)(2,1)} %v_hbm.1), custom_call_target="tpu_custom_call" | custom-call | tf_op jit(solution)/shard_map/spread/pallas_call | solution.py:280
  1.8 0.0 copy-start.3
  1.8 0.0 copy-start.4
  1.8 0.0 copy-start
  1.9 0.0 copy-start.1
  1.9 0.0 copy-start.2
  1.9 10.2 %all-to-all-start = ((bf16[16,192,128]{2,1,0:T(8,128)(2,1)}), bf16[16,192,128]{2,1,0:T(8,128)(2,1)S(1)}, u32[]{:S(2)}, u32[]{:S(2)}) async-start(bf16[16,192,128]{2,1,0:T(8,128)(2,1)} %spread.1), calls=%async_computation | async-start | bytes 1572864 | tf_op jit(solution)/shard_map/all_to_all | solution.py:295
  12.1 0.0 copy-done.3
  12.1 4.3 %collective-permute-start.1 = (bf16[128,2048]{1,0:T(8,128)(2,1)S(1)}, bf16[128,2048]{1,0:T(8,128)(2,1)S(1)}, u32[]{:S(2)}, u32[]{:S(2)}) collective-permute-start(bf16[128,2048]{1,0:T(8,128)(2,1)S(1)} %copy-done.3), channel_id=1, source_target_pairs={{0,2},{2,0},{1,3},{3,1},{4,6},{6,4},{5,7},{7,5},{8,10},{10,8},{9,1... | collective-permute-start | bytes 1572872 | tf_op jit(solution)/shard_map/ppermute | solution.py:300
  16.4 0.0 copy-done.4
  16.4 3.2 %collective-permute-start = (bf16[384,128]{1,0:T(8,128)(2,1)S(1)}, bf16[384,128]{1,0:T(8,128)(2,1)S(1)}, u32[]{:S(2)}, u32[]{:S(2)}) collective-permute-start(bf16[384,128]{1,0:T(8,128)(2,1)S(1)} %copy-done.4), channel_id=1, source_target_pairs={{0,24},{24,0},{1,25},{25,1},{2,26},{26,2},{3,27},{27,3},{4,28},{28... | collective-permute-start | bytes 294920 | tf_op jit(solution)/shard_map/ppermute | solution.py:297
  19.6 0.0 copy-done
  19.6 0.0 copy-done.1
  19.6 0.0 copy-done.2
  19.6 2.1 %tables.1 = (s32[33]{0:T(128)S(1)}, s32[39]{0:T(128)S(1)}, s32[4,4]{1,0:T(4,128)S(1)}, s32[4,768]{1,0:T(4,128)S(1)}, s32[4,768]{1,0:T(4,128)S(1)}) custom-call(s32[64]{0:T(128)S(1)} %copy-done.1, s32[4]{0:T(128)S(1)} %copy-done.2, s32[1,768]{1,0:T(1,128)S(1)} %copy-done), custom_call_target="tpu_custom_call" | custom-call | tf_op jit(solution)/shard_map/tables/pallas_call | solution.py:305
  21.8 8.9 %all_gather.6.q_own_ref = bf16[1536,128]{1,0:T(8,128)(2,1)S(1)} all-gather(bf16[384,128]{1,0:T(8,128)(2,1)S(1)} %copy-done.4), channel_id=1, replica_groups=mesh['y'=8,'xh'=2,'xl'=2,'zh'=3,'zm'=2,'zl'=2,'core'=2] {'zl','core'}, dimensions={0}, use_global_device_ids=true | all-gather | bytes 491520 | tf_op jit(solution)/shard_map/all_gather | solution.py:298
  30.7 0.0 collective-permute-done
  30.7 6.7 %all_gather.7.q_side_ref = bf16[1536,128]{1,0:T(8,128)(2,1)S(1)} all-gather(bf16[384,128]{1,0:T(8,128)(2,1)S(1)} %collective-permute-done), channel_id=1, replica_groups=mesh['y'=8,'xh'=2,'xl'=2,'zh'=3,'zm'=2,'zl'=2,'core'=2] {'zl','core'}, dimensions={0}, use_global_device_ids=true | all-gather | bytes 491520 | tf_op jit(solution)/shard_map/all_gather | solution.py:299
  37.4 0.0 all-to-all-done.kv_ref
  37.4 7.5 %attend.1 = bf16[8,400,128]{2,1,0:T(8,128)(2,1)} custom-call(s32[33]{0:T(128)S(1)} %get-tuple-element.15.rank_ref, s32[39]{0:T(128)S(1)} %get-tuple-element.16.sorted_ref, s32[4,4]{1,0:T(4,128)S(1)} %get-tuple-element.17.tile_ref, bf16[16,192,128]{2,1,0:T(8,128)(2,1)S(1)} %all-to-all-done.kv_ref, bf16[1536,128]{1,0:T(8,128)(2,1)S(1)} %all_gather.6.q_own_ref, ...), custom_call_target="tpu_custom_call" | custom-call | flops 2415919104 | bytes 4194304 | tf_op jit(solution)/shard_map/attend/pallas_call | solution.py:324
  44.9 0.0 collective-permute-done.1
  44.9 4.3 %all-to-all-start.1 = ((bf16[8,400,128]{2,1,0:T(8,128)(2,1)}), bf16[8,400,128]{2,1,0:T(8,128)(2,1)S(1)}, u32[]{:S(2)}, u32[]{:S(2)}) async-start(bf16[8,400,128]{2,1,0:T(8,128)(2,1)} %attend.1), calls=%async_computation.1 | async-start | bytes 1638400 | tf_op jit(solution)/shard_map/all_to_all | solution.py:349
  49.2 0.1 pad_maximum_fusion.w0_ref
  49.3 2.0 %collective-permute-start.2 = (bf16[2,128,2048]{2,1,0:T(8,128)(2,1)S(1)}, bf16[2,128,2048]{2,1,0:T(8,128)(2,1)S(1)}, u32[]{:S(2)}, u32[]{:S(2)}) collective-permute-start(bf16[2,128,2048]{2,1,0:T(8,128)(2,1)S(1)} %pad_maximum_fusion.w0_ref), channel_id=1, source_target_pairs={{0,1},{1,0},{2,3},{3,2},{4,5},{5,4},{6,7},{7,6},{8,9},{9,8},{10,11... | collective-permute-start | bytes 3145736 | tf_op jit(solution)/shard_map/ppermute | solution.py:351
  51.4 2.5 %collective-permute-done.2.w1_ref = bf16[2,128,2048]{2,1,0:T(8,128)(2,1)S(1)} collective-permute-done((bf16[2,128,2048]{2,1,0:T(8,128)(2,1)S(1)}, bf16[2,128,2048]{2,1,0:T(8,128)(2,1)S(1)}, u32[]{:S(2)}, u32[]{:S(2)}) %collective-permute-start.2) | collective-permute-done | bytes 1048608 | tf_op jit(solution)/shard_map/ppermute | solution.py:351
  53.9 6.8 %all-to-all-done.1.got_ref = bf16[8,400,128]{2,1,0:T(8,128)(2,1)S(1)} async-done(((bf16[8,400,128]{2,1,0:T(8,128)(2,1)}), bf16[8,400,128]{2,1,0:T(8,128)(2,1)S(1)}, u32[]{:S(2)}, u32[]{:S(2)}) %all-to-all-start.1) | async-done | bytes 819232 | tf_op jit(solution)/shard_map/all_to_all | solution.py:349
  60.7 1.3 %project.1 = bf16[96,2048]{1,0:T(8,128)(2,1)S(1)} custom-call(bf16[8,400,128]{2,1,0:T(8,128)(2,1)S(1)} %all-to-all-done.1.got_ref, bf16[2,128,2048]{2,1,0:T(8,128)(2,1)S(1)} %pad_maximum_fusion.w0_ref, bf16[2,128,2048]{2,1,0:T(8,128)(2,1)S(1)} %collective-permute-done.2.w1_ref), custom_call_target="tpu_custom_call" | custom-call | tf_op jit(solution)/shard_map/project/pallas_call | solution.py:352
  62.0 31.4 %all_to_all.15 = bf16[6,16,2048]{2,1,0:T(8,128)(2,1)S(1)} all-to-all(bf16[6,16,2048]{2,1,0:T(8,128)(2,1)S(1)} %bitcast.3), channel_id=1, replica_groups=mesh['y'=8,'xh'=2,'xl'=2,'zh'=3,'zm'=2,'zl'=2,'core'=2] {'zh','zm'}, dimensions={0} | all-to-all | bytes 786432 | tf_op jit(solution)/shard_map/all_to_all | solution.py:361
  93.4 0.7 reduce_sum.12
Async XLA Ops:
  1.8 10.3 %copy-start.3 = (bf16[128,2048]{1,0:T(8,128)(2,1)S(1)}, bf16[128,2048]{1,0:T(8,128)(2,1)}, u32[]{:S(2)}) copy-start(bf16[128,2048]{1,0:T(8,128)(2,1)} %param.12) | copy-start | bytes 1572868
  1.8 14.6 %copy-start.4 = (bf16[384,128]{1,0:T(8,128)(2,1)S(1)}, bf16[384,128]{1,0:T(8,128)(2,1)}, u32[]{:S(2)}) copy-start(bf16[384,128]{1,0:T(8,128)(2,1)} %param.7) | copy-start | bytes 294916
  1.8 17.8 %copy-start = (s32[1,768]{1,0:T(1,128)S(1)}, s32[1,768]{1,0:T(1,128)}, u32[]{:S(2)}) copy-start(s32[1,768]{1,0:T(1,128)} %constant.5.clone.lane_ref) | copy-start | bytes 9220
  1.9 17.8 %copy-start.1 = (s32[64]{0:T(128)S(1)}, s32[64]{0:T(128)}, u32[]{:S(2)}) copy-start(s32[64]{0:T(128)} %slot_ref.1) | copy-start | bytes 772
  1.9 17.8 %copy-start.2 = (s32[4]{0:T(128)S(1)}, s32[4]{0:T(128)}, u32[]{:S(2)}) copy-start(s32[4]{0:T(128)} %len_ref.1) | copy-start | bytes 52
  1.9 35.5 %all-to-all-start = ((bf16[16,192,128]{2,1,0:T(8,128)(2,1)}), bf16[16,192,128]{2,1,0:T(8,128)(2,1)S(1)}, u32[]{:S(2)}, u32[]{:S(2)}) async-start(bf16[16,192,128]{2,1,0:T(8,128)(2,1)} %spread.1), calls=%async_computation | async-start | bytes 1572864 | tf_op jit(solution)/shard_map/all_to_all | solution.py:295
  12.1 32.8 %collective-permute-start.1 = (bf16[128,2048]{1,0:T(8,128)(2,1)S(1)}, bf16[128,2048]{1,0:T(8,128)(2,1)S(1)}, u32[]{:S(2)}, u32[]{:S(2)}) collective-permute-start(bf16[128,2048]{1,0:T(8,128)(2,1)S(1)} %copy-done.3), channel_id=1, source_target_pairs={{0,2},{2,0},{1,3},{3,1},{4,6},{6,4},{5,7},{7,5},{8,10},{10,8},{9,1... | collective-permute-start | bytes 1572872 | tf_op jit(solution)/shard_map/ppermute | solution.py:300
  16.4 14.3 %collective-permute-start = (bf16[384,128]{1,0:T(8,128)(2,1)S(1)}, bf16[384,128]{1,0:T(8,128)(2,1)S(1)}, u32[]{:S(2)}, u32[]{:S(2)}) collective-permute-start(bf16[384,128]{1,0:T(8,128)(2,1)S(1)} %copy-done.4), channel_id=1, source_target_pairs={{0,24},{24,0},{1,25},{25,1},{2,26},{26,2},{3,27},{27,3},{4,28},{28... | collective-permute-start | bytes 294920 | tf_op jit(solution)/shard_map/ppermute | solution.py:297
  44.9 15.8 %all-to-all-start.1 = ((bf16[8,400,128]{2,1,0:T(8,128)(2,1)}), bf16[8,400,128]{2,1,0:T(8,128)(2,1)S(1)}, u32[]{:S(2)}, u32[]{:S(2)}) async-start(bf16[8,400,128]{2,1,0:T(8,128)(2,1)} %attend.1), calls=%async_computation.1 | async-start | bytes 1638400 | tf_op jit(solution)/shard_map/all_to_all | solution.py:349
  49.3 4.6 %collective-permute-start.2 = (bf16[2,128,2048]{2,1,0:T(8,128)(2,1)S(1)}, bf16[2,128,2048]{2,1,0:T(8,128)(2,1)S(1)}, u32[]{:S(2)}, u32[]{:S(2)}) collective-permute-start(bf16[2,128,2048]{2,1,0:T(8,128)(2,1)S(1)} %pad_maximum_fusion.w0_ref), channel_id=1, source_target_pairs={{0,1},{1,0},{2,3},{3,2},{4,5},{5,4},{6,7},{7,6},{8,9},{9,8},{10,11... | collective-permute-start | bytes 3145736 | tf_op jit(solution)/shard_map/ppermute | solution.py:351

commit v5 on v4

--- a/solution.py
+++ b/solution.py
@@ -27,6 +27,7 @@
 PAD = KEYS + CHUNK
 SLOTS = PIECES + CHUNK // QUART + 2
 TILE = 4 * HALF
+LANES = 384
 TEAM_SIZE = 8
 STAT = 16
 SEND = TOK + STAT
@@ -136,7 +137,6 @@
     k_scr,
     v_scr,
     q_scr,
-    s_scr,
     m_scr,
     l_scr,
     acc_scr,
@@ -177,37 +177,45 @@
         def one_step(step, carry):
             first = low * QUART + step * CHUNK
             at = pl.multiple_of(first, 16)
-            s_scr[...] = lax.dot_general(
-                k_scr[pl.ds(at, CHUNK), :],
-                q_scr[tile],
-                (((1,), (1,)), ((), ())),
-                preferred_element_type=jnp.float32,
-            )
             first_pos = sorted_ref[lax.div(first, QUART)] * HALF
             last_pos = sorted_ref[lax.div(first + CHUNK - 1, QUART)] * HALF + HALF - 1
-
-            @pl.when((last_pos > q_first) | (first_pos < start_last))
-            def _():
-                key_pos = kpos_scr[pl.ds(at, CHUNK), :]
-                key_pos = jnp.concatenate([key_pos] * (TILE // HD), axis=1)
-                allowed = (key_pos <= qpos_ref[pl.ds(tile, 1), :]) & (
-                    key_pos >= qstart_ref[pl.ds(tile, 1), :]
-                )
-                s_scr[...] = jnp.where(allowed, s_scr[...], LOW)
-
-            scores = s_scr[...]
-            old = m_scr[...]
-            new = jnp.maximum(old, jnp.max(scores, axis=0, keepdims=True))
-            m_scr[...] = new
-            probs = jnp.exp2((scores - new) * SCALE)
-            factor = jnp.exp2((old - new) * SCALE)
-            l_scr[...] = l_scr[...] * factor + jnp.sum(probs, axis=0, keepdims=True)
-            acc_scr[...] = acc_scr[...] * factor + lax.dot_general(
-                v_scr[pl.ds(at, CHUNK), :],
-                probs.astype(jnp.bfloat16),
-                (((0,), (0,)), ((), ())),
-                preferred_element_type=jnp.float32,
-            )
+            edge = (last_pos > q_first) | (first_pos < start_last)
+
+            def block(masked):
+                keys = k_scr[pl.ds(at, CHUNK), :]
+                vals = v_scr[pl.ds(at, CHUNK), :]
+                for part in range(TILE // LANES):
+                    cols = slice(part * LANES, (part + 1) * LANES)
+                    scores = lax.dot_general(
+                        keys,
+                        q_scr[tile, cols, :],
+                        (((1,), (1,)), ((), ())),
+                        preferred_element_type=jnp.float32,
+                    )
+                    if masked:
+                        key_pos = kpos_scr[pl.ds(at, CHUNK), :]
+                        key_pos = jnp.concatenate([key_pos] * (LANES // HD), axis=1)
+                        allowed = (key_pos <= qpos_ref[pl.ds(tile, 1), cols]) & (
+                            key_pos >= qstart_ref[pl.ds(tile, 1), cols]
+                        )
+                        scores = jnp.where(allowed, scores, LOW)
+                    old = m_scr[:, cols]
+                    new = jnp.maximum(old, jnp.max(scores, axis=0, keepdims=True))
+                    m_scr[:, cols] = new
+                    probs = jnp.exp2((scores - new) * SCALE)
+                    factor = jnp.exp2((old - new) * SCALE)
+                    l_scr[:, cols] = l_scr[:, cols] * factor + jnp.sum(
+                        probs, axis=0, keepdims=True
+                    )
+                    acc_scr[:, cols] = acc_scr[:, cols] * factor + lax.dot_general(
+                        vals,
+                        probs.astype(jnp.bfloat16),
+                        (((0,), (0,)), ((), ())),
+                        preferred_element_type=jnp.float32,
+                    )
+
+            pl.when(edge)(lambda: block(True))
+            pl.when(jnp.logical_not(edge))(lambda: block(False))
             return carry
 
         lax.fori_loop(0, steps, one_step, 0)
@@ -321,7 +329,7 @@
         name="tables",
     )(block_of_slot, doc_lengths, jnp.asarray(in_half[None, :], i32))
 
-    sent = pl.pallas_call(
+    attend = pl.pallas_call(
         attend_kernel,
         out_shape=jax.ShapeDtypeStruct((TEAM_SIZE, SEND, HD), jnp.bfloat16),
         in_specs=[smem, smem, smem, vmem, vmem, vmem, vmem, vmem],
@@ -331,7 +339,6 @@
             pltpu.VMEM((PAD, HD), jnp.bfloat16),
             pltpu.VMEM((PAD, HD), jnp.bfloat16),
             pltpu.VMEM((4, TILE, HD), jnp.bfloat16),
-            pltpu.VMEM((CHUNK, TILE), jnp.float32),
             pltpu.VMEM((1, TILE), jnp.float32),
             pltpu.VMEM((1, TILE), jnp.float32),
             pltpu.VMEM((HD, TILE), jnp.float32),
@@ -344,8 +351,9 @@
             bytes_accessed=4 << 20,
         ),
         name="attend",
-    )(rank, in_order, tiles, kv, q, q_side, q_pos, q_start)
-    sent, w_side = lax.optimization_barrier((sent, w_side))
+    )
+    sent = attend(rank, in_order, tiles, kv, q, q_side, q_pos, q_start)
+    _, w_side = lax.optimization_barrier((sent, w_side))
     got = lax.all_to_all(sent, TEAM, 0, 0, tiled=True)
     w0 = jnp.stack([out_weight, w_side])
     w1 = lax.ppermute(w0, "core", flip)

time: 95 us -> 111 us (1.17)
  waiting for transfers between devices: 9.33 us -> 23.4 us
  starting transfers between devices: 24.1 us -> 26.3 us
  blocking collectives: 47 us -> 45.5 us
    ppermute x1, waiting for transfers between devices: 0.01 us -> 19.3 us  [per_device(): w_side = lax.ppermute(out_weight, 'zl', flip)]
    all_to_all x1, waiting for transfers between devices: 6.8 us -> 0.01 us  [per_device(): got = lax.all_to_all(sent, TEAM, 0, 0, tiled=True)]
    all_gather x1, blocking collectives: 8.93 us -> 6.14 us  [per_device(): q = lax.all_gather(queries, ('zl', 'core'), axis=0, tiled=True)]
    ppermute x1, starting transfers between devices: 3.19 us -> 5.55 us  [per_device(): q_side = lax.ppermute(queries, 'xl', flip)]
    all_to_all x1, blocking collectives: 31.4 us -> 32.8 us  [per_device(): parts = lax.all_to_all(terms.reshape(6, 16, -1), Z6, 0, 0, tiled=True)]
    all_to_all x1, waiting for transfers between devices: 0.01 us -> 1.44 us  [per_device(): kv = lax.all_to_all(spread, KV_AXES, 0, 0, tiled=True)]
  transfers between devices with their start and end apart: 5 -> 5, of which waited for: 2 -> 3; matrix products, arithmetic and copies ran while one was open for 0% -> 0% of each run, Pallas kernels for 10% -> 2%
where the time goes in v5:
time: 111 us; the launch traced here: 109 us
  blocking collectives  45.5 us (41%)
  starting transfers between devices  26.3 us (24%)
  waiting for transfers between devices  23.4 us (21%)
  Pallas kernels  13.3 us (12%)
    all_to_all x1, blocking collectives, per_device(): parts = lax.all_to_all(terms.reshape(6, 16, -1), Z6, 0, 0, tiled=True)  32.8 us
    ppermute x1, waiting for transfers between devices, per_device(): w_side = lax.ppermute(out_weight, 'zl', flip)  19.3 us
    all_to_all x1, starting transfers between devices, per_device(): kv = lax.all_to_all(spread, KV_AXES, 0, 0, tiled=True)  10.2 us
    pallas_call x1, Pallas kernels, per_device(): sent = attend(rank, in_order, tiles, kv, q, q_side, q_pos, q_start)  8.08 us
    all_gather x1, blocking collectives, per_device(): q_side = lax.all_gather(q_side, ('zl', 'core'), axis=0, tiled=True)  6.55 us
    all_gather x1, blocking collectives, per_device(): q = lax.all_gather(queries, ('zl', 'core'), axis=0, tiled=True)  6.14 us
    ppermute x1, starting transfers between devices, per_device(): q_side = lax.ppermute(queries, 'xl', flip)  5.55 us
    all_to_all x1, starting transfers between devices, per_device(): got = lax.all_to_all(sent, TEAM, 0, 0, tiled=True)  5.24 us
  transfers between devices with their start and end apart: 5, of which 3 were waited for; matrix products, arithmetic and copies ran while one was open for 0% of the time, Pallas kernels for 2%

profile of v5, /device:TPU:6, one launch (start us, length us, event | category | flops | bytes accessed | tf_op | source)
XLA Modules:
  0.0 109.5 jit_solution(10616162266151999062)
XLA Ops:
  0.0 1.8 %spread.1 = bf16[16,192,128]{2,1,0:T(8,128)(2,1)} custom-call(bf16[384,384]{1,0:T(8,128)(2,1)} %k_hbm.1, bf16[384,384]{1,0:T(8,128)(2,1)} %v_hbm.1), custom_call_target="tpu_custom_call" | custom-call | tf_op jit(solution)/shard_map/spread/pallas_call | solution.py:288
  1.8 0.0 copy-start.4
  1.8 0.0 copy-start
  1.8 0.0 copy-start.1
  1.9 0.0 copy-start.2
  1.9 10.2 %all-to-all-start = ((bf16[16,192,128]{2,1,0:T(8,128)(2,1)}), bf16[16,192,128]{2,1,0:T(8,128)(2,1)S(1)}, u32[]{:S(2)}, u32[]{:S(2)}) async-start(bf16[16,192,128]{2,1,0:T(8,128)(2,1)} %spread.1), calls=%async_computation | async-start | bytes 1572864 | tf_op jit(solution)/shard_map/all_to_all | solution.py:303
  12.1 0.0 copy-done.4
  12.1 5.5 %collective-permute-start = (bf16[384,128]{1,0:T(8,128)(2,1)S(1)}, bf16[384,128]{1,0:T(8,128)(2,1)S(1)}, u32[]{:S(2)}, u32[]{:S(2)}) collective-permute-start(bf16[384,128]{1,0:T(8,128)(2,1)S(1)} %copy-done.4), channel_id=1, source_target_pairs={{0,24},{24,0},{1,25},{25,1},{2,26},{26,2},{3,27},{27,3},{4,28},{28... | collective-permute-start | bytes 294920 | tf_op jit(solution)/shard_map/ppermute | solution.py:305
  17.6 0.0 copy-done
  17.7 0.0 copy-done.1
  17.7 0.0 copy-done.2
  17.7 2.1 %tables.1 = (s32[33]{0:T(128)S(1)}, s32[39]{0:T(128)S(1)}, s32[4,4]{1,0:T(4,128)S(1)}, s32[4,768]{1,0:T(4,128)S(1)}, s32[4,768]{1,0:T(4,128)S(1)}) custom-call(s32[64]{0:T(128)S(1)} %copy-done.1, s32[4]{0:T(128)S(1)} %copy-done.2, s32[1,768]{1,0:T(1,128)S(1)} %copy-done), custom_call_target="tpu_custom_call" | custom-call | tf_op jit(solution)/shard_map/tables/pallas_call | solution.py:313
  19.8 6.1 %all_gather.6.q_own_ref = bf16[1536,128]{1,0:T(8,128)(2,1)S(1)} all-gather(bf16[384,128]{1,0:T(8,128)(2,1)S(1)} %copy-done.4), channel_id=1, replica_groups=mesh['y'=8,'xh'=2,'xl'=2,'zh'=3,'zm'=2,'zl'=2,'core'=2] {'zl','core'}, dimensions={0}, use_global_device_ids=true | all-gather | bytes 491520 | tf_op jit(solution)/shard_map/all_gather | solution.py:306
  26.0 0.0 collective-permute-done
  26.0 6.6 %all_gather.7.q_side_ref = bf16[1536,128]{1,0:T(8,128)(2,1)S(1)} all-gather(bf16[384,128]{1,0:T(8,128)(2,1)S(1)} %collective-permute-done), channel_id=1, replica_groups=mesh['y'=8,'xh'=2,'xl'=2,'zh'=3,'zm'=2,'zl'=2,'core'=2] {'zl','core'}, dimensions={0}, use_global_device_ids=true | all-gather | bytes 491520 | tf_op jit(solution)/shard_map/all_gather | solution.py:307
  32.5 1.4 %all-to-all-done.kv_ref = bf16[16,192,128]{2,1,0:T(8,128)(2,1)S(1)} async-done(((bf16[16,192,128]{2,1,0:T(8,128)(2,1)}), bf16[16,192,128]{2,1,0:T(8,128)(2,1)S(1)}, u32[]{:S(2)}, u32[]{:S(2)}) %all-to-all-start) | async-done | bytes 786464 | tf_op jit(solution)/shard_map/all_to_all | solution.py:303
  34.0 8.1 %attend.1 = bf16[8,400,128]{2,1,0:T(8,128)(2,1)} custom-call(s32[33]{0:T(128)S(1)} %get-tuple-element.14.rank_ref, s32[39]{0:T(128)S(1)} %get-tuple-element.15.sorted_ref, s32[4,4]{1,0:T(4,128)S(1)} %get-tuple-element.16.tile_ref, bf16[16,192,128]{2,1,0:T(8,128)(2,1)S(1)} %all-to-all-done.kv_ref, bf16[1536,128]{1,0:T(8,128)(2,1)S(1)} %all_gather.6.q_own_ref, ...), custom_call_target="tpu_custom_call" | custom-call | flops 2415919104 | bytes 4194304 | tf_op jit(solution)/shard_map/attend/pallas_call | solution.py:355
  42.0 0.0 copy-start.3
  42.0 5.2 %all-to-all-start.1 = ((bf16[8,400,128]{2,1,0:T(8,128)(2,1)}), bf16[8,400,128]{2,1,0:T(8,128)(2,1)S(1)}, u32[]{:S(2)}, u32[]{:S(2)}) async-start(bf16[8,400,128]{2,1,0:T(8,128)(2,1)} %attend.1), calls=%async_computation.1 | async-start | bytes 1638400 | tf_op jit(solution)/shard_map/all_to_all | solution.py:357
  47.3 0.0 copy-done.3
  47.3 3.4 %collective-permute-start.1 = (bf16[128,2048]{1,0:T(8,128)(2,1)S(1)}, bf16[128,2048]{1,0:T(8,128)(2,1)S(1)}, u32[]{:S(2)}, u32[]{:S(2)}) collective-permute-start(bf16[128,2048]{1,0:T(8,128)(2,1)S(1)} %copy-done.3), channel_id=1, source_target_pairs={{0,2},{2,0},{1,3},{3,1},{4,6},{6,4},{5,7},{7,5},{8,10},{10,8},{9,1... | collective-permute-start | bytes 1572872 | tf_op jit(solution)/shard_map/ppermute | solution.py:308
  50.7 19.3 %collective-permute-done.1 = bf16[128,2048]{1,0:T(8,128)(2,1)S(1)} collective-permute-done((bf16[128,2048]{1,0:T(8,128)(2,1)S(1)}, bf16[128,2048]{1,0:T(8,128)(2,1)S(1)}, u32[]{:S(2)}, u32[]{:S(2)}) %collective-permute-start.1) | collective-permute-done | bytes 524320 | tf_op jit(solution)/shard_map/ppermute | solution.py:308
  70.0 0.1 pad_maximum_fusion.w0_ref
  70.1 1.9 %collective-permute-start.2 = (bf16[2,128,2048]{2,1,0:T(8,128)(2,1)S(1)}, bf16[2,128,2048]{2,1,0:T(8,128)(2,1)S(1)}, u32[]{:S(2)}, u32[]{:S(2)}) collective-permute-start(bf16[2,128,2048]{2,1,0:T(8,128)(2,1)S(1)} %pad_maximum_fusion.w0_ref), channel_id=1, source_target_pairs={{0,1},{1,0},{2,3},{3,2},{4,5},{5,4},{6,7},{7,6},{8,9},{9,8},{10,11... | collective-permute-start | bytes 3145736 | tf_op jit(solution)/shard_map/ppermute | solution.py:359
  72.0 2.6 %collective-permute-done.2.w1_ref = bf16[2,128,2048]{2,1,0:T(8,128)(2,1)S(1)} collective-permute-done((bf16[2,128,2048]{2,1,0:T(8,128)(2,1)S(1)}, bf16[2,128,2048]{2,1,0:T(8,128)(2,1)S(1)}, u32[]{:S(2)}, u32[]{:S(2)}) %collective-permute-start.2) | collective-permute-done | bytes 1048608 | tf_op jit(solution)/shard_map/ppermute | solution.py:359
  74.6 0.0 all-to-all-done.1.got_ref
  74.6 1.3 %project.1 = bf16[96,2048]{1,0:T(8,128)(2,1)S(1)} custom-call(bf16[8,400,128]{2,1,0:T(8,128)(2,1)S(1)} %all-to-all-done.1.got_ref, bf16[2,128,2048]{2,1,0:T(8,128)(2,1)S(1)} %pad_maximum_fusion.w0_ref, bf16[2,128,2048]{2,1,0:T(8,128)(2,1)S(1)} %collective-permute-done.2.w1_ref), custom_call_target="tpu_custom_call" | custom-call | tf_op jit(solution)/shard_map/project/pallas_call | solution.py:360
  76.0 32.8 %all_to_all.15 = bf16[6,16,2048]{2,1,0:T(8,128)(2,1)S(1)} all-to-all(bf16[6,16,2048]{2,1,0:T(8,128)(2,1)S(1)} %bitcast.3), channel_id=1, replica_groups=mesh['y'=8,'xh'=2,'xl'=2,'zh'=3,'zm'=2,'zl'=2,'core'=2] {'zh','zm'}, dimensions={0} | all-to-all | bytes 786432 | tf_op jit(solution)/shard_map/all_to_all | solution.py:369
  108.8 0.7 reduce_sum.12
Async XLA Ops:
  1.8 10.3 %copy-start.4 = (bf16[384,128]{1,0:T(8,128)(2,1)S(1)}, bf16[384,128]{1,0:T(8,128)(2,1)}, u32[]{:S(2)}) copy-start(bf16[384,128]{1,0:T(8,128)(2,1)} %param.7) | copy-start | bytes 294916
  1.8 15.8 %copy-start = (s32[1,768]{1,0:T(1,128)S(1)}, s32[1,768]{1,0:T(1,128)}, u32[]{:S(2)}) copy-start(s32[1,768]{1,0:T(1,128)} %constant.5.clone.lane_ref) | copy-start | bytes 9220
  1.8 15.8 %copy-start.1 = (s32[64]{0:T(128)S(1)}, s32[64]{0:T(128)}, u32[]{:S(2)}) copy-start(s32[64]{0:T(128)} %slot_ref.1) | copy-start | bytes 772
  1.9 15.8 %copy-start.2 = (s32[4]{0:T(128)S(1)}, s32[4]{0:T(128)}, u32[]{:S(2)}) copy-start(s32[4]{0:T(128)} %len_ref.1) | copy-start | bytes 52
  1.9 32.1 %all-to-all-start = ((bf16[16,192,128]{2,1,0:T(8,128)(2,1)}), bf16[16,192,128]{2,1,0:T(8,128)(2,1)S(1)}, u32[]{:S(2)}, u32[]{:S(2)}) async-start(bf16[16,192,128]{2,1,0:T(8,128)(2,1)} %spread.1), calls=%async_computation | async-start | bytes 1572864 | tf_op jit(solution)/shard_map/all_to_all | solution.py:303
  12.1 13.9 %collective-permute-start = (bf16[384,128]{1,0:T(8,128)(2,1)S(1)}, bf16[384,128]{1,0:T(8,128)(2,1)S(1)}, u32[]{:S(2)}, u32[]{:S(2)}) collective-permute-start(bf16[384,128]{1,0:T(8,128)(2,1)S(1)} %copy-done.4), channel_id=1, source_target_pairs={{0,24},{24,0},{1,25},{25,1},{2,26},{26,2},{3,27},{27,3},{4,28},{28... | collective-permute-start | bytes 294920 | tf_op jit(solution)/shard_map/ppermute | solution.py:305
  42.0 5.2 %copy-start.3 = (bf16[128,2048]{1,0:T(8,128)(2,1)S(1)}, bf16[128,2048]{1,0:T(8,128)(2,1)}, u32[]{:S(2)}) copy-start(bf16[128,2048]{1,0:T(8,128)(2,1)} %param.12) | copy-start | bytes 1572868
  42.0 32.6 %all-to-all-start.1 = ((bf16[8,400,128]{2,1,0:T(8,128)(2,1)}), bf16[8,400,128]{2,1,0:T(8,128)(2,1)S(1)}, u32[]{:S(2)}, u32[]{:S(2)}) async-start(bf16[8,400,128]{2,1,0:T(8,128)(2,1)} %attend.1), calls=%async_computation.1 | async-start | bytes 1638400 | tf_op jit(solution)/shard_map/all_to_all | solution.py:357
  47.3 22.7 %collective-permute-start.1 = (bf16[128,2048]{1,0:T(8,128)(2,1)S(1)}, bf16[128,2048]{1,0:T(8,128)(2,1)S(1)}, u32[]{:S(2)}, u32[]{:S(2)}) collective-permute-start(bf16[128,2048]{1,0:T(8,128)(2,1)S(1)} %copy-done.3), channel_id=1, source_target_pairs={{0,2},{2,0},{1,3},{3,1},{4,6},{6,4},{5,7},{7,5},{8,10},{10,8},{9,1... | collective-permute-start | bytes 1572872 | tf_op jit(solution)/shard_map/ppermute | solution.py:308
  70.1 4.6 %collective-permute-start.2 = (bf16[2,128,2048]{2,1,0:T(8,128)(2,1)S(1)}, bf16[2,128,2048]{2,1,0:T(8,128)(2,1)S(1)}, u32[]{:S(2)}, u32[]{:S(2)}) collective-permute-start(bf16[2,128,2048]{2,1,0:T(8,128)(2,1)S(1)} %pad_maximum_fusion.w0_ref), channel_id=1, source_target_pairs={{0,1},{1,0},{2,3},{3,2},{4,5},{5,4},{6,7},{7,6},{8,9},{9,8},{10,11... | collective-permute-start | bytes 3145736 | tf_op jit(solution)/shard_map/ppermute | solution.py:359

commit v6 on v5

--- a/solution.py
+++ b/solution.py
@@ -12,9 +12,16 @@
 SIZES = (8, 2, 2, 3, 2, 2, 2)
 DP = ("y", "xh", "xl")
 HEAD = ("zh", "zm", "zl", "core")
-KV_AXES = ("y", "xh")
 TEAM = ("xl", "zl", "core")
-Z6 = ("zh", "zm")
+KV_GROUPS = [
+    [y * 4 + xh * 2 + (kind ^ xh) for y in range(8) for xh in range(2)]
+    for kind in range(2)
+]
+SUM_GROUPS = [
+    [p * 4 + (kind ^ p % 2) * 2 + core for p in range(6)]
+    for kind in range(2)
+    for core in range(2)
+]
 
 TOK = 384
 HALF = 192
@@ -27,7 +34,8 @@
 PAD = KEYS + CHUNK
 SLOTS = PIECES + CHUNK // QUART + 2
 TILE = 4 * HALF
-LANES = 384
+LANES = 256
+ROWS = 128
 TEAM_SIZE = 8
 STAT = 16
 SEND = TOK + STAT
@@ -84,6 +92,7 @@
 ):
     xl = lax.axis_index("xl")
     here = lax.axis_index("y") * 2 + lax.axis_index("xh")
+    kind = xl ^ lax.axis_index("xh")
 
     def clear(n, carry):
         where_scr[n] = PIECES
@@ -92,7 +101,8 @@
     lax.fori_loop(0, 2 * PIECES, clear, 0)
     for piece in range(PIECES):
         src, half = divmod(piece, 2)
-        where_scr[slot_ref[4 * src + 2 * xl + half]] = piece
+        side = 2 * (kind ^ (src % 2))
+        where_scr[slot_ref[4 * src + side + half]] = piece
 
     def walk(block, count):
         before_scr[block] = count
@@ -107,7 +117,6 @@
     bounds = [len_ref[0]]
     for n in range(1, len_ref.shape[0] - 1):
         bounds.append(bounds[-1] + len_ref[n])
-    lane = lane_ref[...]
     for tile in range(4):
         rel, half = divmod(tile, 2)
         block = slot_ref[4 * here + 2 * (xl ^ rel) + half]
@@ -118,7 +127,7 @@
         tile_ref[tile, 1] = lax.div((high - low) * QUART + CHUNK - 1, CHUNK)
         tile_ref[tile, 2] = base
         tile_ref[tile, 3] = start_of(base + HALF - 1, bounds)
-        pos = lane + base
+        pos = lane_ref[pl.ds(lax.axis_index("zm") ^ half, 1), :] + base
         qpos_ref[tile : tile + 1, :] = pos
         qstart_ref[tile : tile + 1, :] = start_of(pos, bounds)
 
@@ -158,6 +167,8 @@
         kpos_scr[n * QUART : (n + 1) * QUART, :] = row + sorted_ref[n] * HALF
     kpos_scr[KEYS:, :] = jnp.full((PAD - KEYS, HD), FAR, jnp.int32)
 
+    zm = lax.axis_index("zm")
+    flips = (zm * 32, (1 - zm) * 32)
     for tile in range(4):
         q_ref = (q_own_ref, q_side_ref)[tile // 2]
         half = tile % 2
@@ -165,8 +176,10 @@
             for j in range(4):
                 for z3 in range(3):
                     to = d * HALF + j * QUART + z3 * 16
-                    of = j * TOK + half * HALF + z3 * 64 + d * 16
-                    q_scr[tile, to : to + 16, :] = q_ref[of : of + 16, :]
+                    of = j * TOK + half * HALF + z3 * 64
+                    of = of + ((d * 16) ^ flips[(half * 3 + z3) % 2])
+                    rows = pl.ds(pl.multiple_of(of, 16), 16)
+                    q_scr[tile, to : to + 16, :] = q_ref[rows, :]
 
     def one_tile(tile, carry):
         low, steps, q_first, start_last = (tile_ref[tile, n] for n in range(4))
@@ -182,34 +195,53 @@
             edge = (last_pos > q_first) | (first_pos < start_last)
 
             def block(masked):
-                keys = k_scr[pl.ds(at, CHUNK), :]
+                parts = TILE // LANES
+                keys = [
+                    k_scr[pl.ds(at + r * ROWS, ROWS), :] for r in range(CHUNK // ROWS)
+                ]
                 vals = v_scr[pl.ds(at, CHUNK), :]
-                for part in range(TILE // LANES):
+
+                def score(part, r):
                     cols = slice(part * LANES, (part + 1) * LANES)
                     scores = lax.dot_general(
-                        keys,
+                        keys[r],
                         q_scr[tile, cols, :],
                         (((1,), (1,)), ((), ())),
                         preferred_element_type=jnp.float32,
                     )
                     if masked:
-                        key_pos = kpos_scr[pl.ds(at, CHUNK), :]
+                        key_pos = kpos_scr[pl.ds(at + r * ROWS, ROWS), :]
                         key_pos = jnp.concatenate([key_pos] * (LANES // HD), axis=1)
                         allowed = (key_pos <= qpos_ref[pl.ds(tile, 1), cols]) & (
                             key_pos >= qstart_ref[pl.ds(tile, 1), cols]
                         )
                         scores = jnp.where(allowed, scores, LOW)
+                    return scores
+
+                ahead = [score(0, r) for r in range(CHUNK // ROWS)]
+                for part in range(parts):
+                    cols = slice(part * LANES, (part + 1) * LANES)
+                    now, ahead = ahead, []
+                    high = now[0]
+                    for scores in now[1:]:
+                        high = jnp.maximum(high, scores)
                     old = m_scr[:, cols]
-                    new = jnp.maximum(old, jnp.max(scores, axis=0, keepdims=True))
+                    new = jnp.maximum(old, jnp.max(high, axis=0, keepdims=True))
                     m_scr[:, cols] = new
-                    probs = jnp.exp2((scores - new) * SCALE)
                     factor = jnp.exp2((old - new) * SCALE)
+                    probs, total = [], None
+                    for r, scores in enumerate(now):
+                        if part + 1 < parts:
+                            ahead.append(score(part + 1, r))
+                        prob = jnp.exp2((scores - new) * SCALE)
+                        total = prob if total is None else total + prob
+                        probs.append(prob.astype(jnp.bfloat16))
                     l_scr[:, cols] = l_scr[:, cols] * factor + jnp.sum(
-                        probs, axis=0, keepdims=True
+                        total, axis=0, keepdims=True
                     )
                     acc_scr[:, cols] = acc_scr[:, cols] * factor + lax.dot_general(
                         vals,
-                        probs.astype(jnp.bfloat16),
+                        jnp.concatenate(probs, axis=0),
                         (((0,), (0,)), ((), ())),
                         preferred_element_type=jnp.float32,
                     )
@@ -300,7 +332,9 @@
     spread, queries, out_weight = lax.optimization_barrier(
         (spread, queries, out_weight)
     )
-    kv = lax.all_to_all(spread, KV_AXES, 0, 0, tiled=True)
+    kv = lax.all_to_all(
+        spread, DP, 0, 0, axis_index_groups=KV_GROUPS, tiled=True
+    )
     flip = [(0, 1), (1, 0)]
     q_side = lax.ppermute(queries, "xl", flip)
     q = lax.all_gather(queries, ("zl", "core"), axis=0, tiled=True)
@@ -308,7 +342,13 @@
     w_side = lax.ppermute(out_weight, "zl", flip)
 
     lane = np.arange(TILE)
-    in_half = (lane % QUART) // 16 * 64 + lane // HALF * 16 + lane % 16
+    third = lane % QUART // 16
+    in_half = np.stack(
+        [
+            third * 64 + (lane // HALF * 16 ^ (n ^ third % 2) * 32) + lane % 16
+            for n in range(2)
+        ]
+    )
     i32 = jnp.int32
     rank, in_order, tiles, q_pos, q_start = pl.pallas_call(
         table_kernel,
@@ -327,7 +367,7 @@
         ],
         compiler_params=pltpu.CompilerParams(vmem_limit_bytes=8 << 20),
         name="tables",
-    )(block_of_slot, doc_lengths, jnp.asarray(in_half[None, :], i32))
+    )(block_of_slot, doc_lengths, jnp.asarray(in_half, i32))
 
     attend = pl.pallas_call(
         attend_kernel,
@@ -366,7 +406,9 @@
         compiler_params=pltpu.CompilerParams(vmem_limit_bytes=16 << 20),
         name="project",
     )(got, w0, w1)
-    parts = lax.all_to_all(terms.reshape(6, 16, -1), Z6, 0, 0, tiled=True)
+    parts = lax.all_to_all(
+        terms.reshape(6, 16, -1), HEAD, 0, 0, axis_index_groups=SUM_GROUPS, tiled=True
+    )
     return jnp.sum(parts.astype(jnp.float32), axis=0).astype(jnp.bfloat16)
 
 

time: 111 us -> 111 us (level)
    ppermute x1, starting transfers between devices: 5.55 us -> 1.92 us  [per_device(): q_side = lax.ppermute(queries, 'xl', flip)]
    all_to_all x1, starting transfers between devices: 10.2 us -> 13 us  [per_device(): lax.all_to_all(spread, DP, 0, 0, axis_index_groups=KV_GROUPS, tiled=True)]
where the time goes in v6:
time: 111 us; the launch traced here: 109 us
  blocking collectives  46.1 us (42%)
  starting transfers between devices  26.3 us (24%)
  waiting for transfers between devices  23.1 us (21%)
  Pallas kernels  12.7 us (11%)
    all_to_all x1, blocking collectives, per_device(): lax.all_to_all(terms.reshape(6, 16, -1), HEAD, 0, 0, axis_index_groups=SU...  33.4 us
    ppermute x1, waiting for transfers between devices, per_device(): w_side = lax.ppermute(out_weight, 'zl', flip)  19.3 us
    all_to_all x1, starting transfers between devices, per_device(): lax.all_to_all(spread, DP, 0, 0, axis_index_groups=KV_GROUPS, tiled=True)  13 us
    pallas_call x1, Pallas kernels, per_device(): sent = attend(rank, in_order, tiles, kv, q, q_side, q_pos, q_start)  7.49 us
    all_gather x1, blocking collectives, per_device(): q_side = lax.all_gather(q_side, ('zl', 'core'), axis=0, tiled=True)  6.55 us
    all_gather x1, blocking collectives, per_device(): q = lax.all_gather(queries, ('zl', 'core'), axis=0, tiled=True)  6.14 us
    all_to_all x1, starting transfers between devices, per_device(): got = lax.all_to_all(sent, TEAM, 0, 0, tiled=True)  6.14 us
    ppermute x1, starting transfers between devices, per_device(): w_side = lax.ppermute(out_weight, 'zl', flip)  3.36 us
  transfers between devices with their start and end apart: 5, of which 3 were waited for; matrix products, arithmetic and copies ran while one was open for 0% of the time, Pallas kernels for 2%

profile of v6, /device:TPU:6, one launch (start us, length us, event | category | flops | bytes accessed | tf_op | source)
XLA Modules:
  0.0 109.1 jit_solution(12243696162479963935)
XLA Ops:
  0.0 1.8 %spread.1 = bf16[16,192,128]{2,1,0:T(8,128)(2,1)} custom-call(bf16[384,384]{1,0:T(8,128)(2,1)} %k_hbm.1, bf16[384,384]{1,0:T(8,128)(2,1)} %v_hbm.1), custom_call_target="tpu_custom_call" | custom-call | tf_op jit(solution)/shard_map/spread/pallas_call | solution.py:320
  1.8 0.0 copy-start.4
  1.8 0.0 copy-start
  1.8 0.0 copy-start.1
  1.9 0.0 copy-start.2
  1.9 13.0 %all-to-all-start = ((bf16[16,192,128]{2,1,0:T(8,128)(2,1)}), bf16[16,192,128]{2,1,0:T(8,128)(2,1)S(1)}, u32[]{:S(2)}, u32[]{:S(2)}) async-start(bf16[16,192,128]{2,1,0:T(8,128)(2,1)} %spread.1), calls=%async_computation | async-start | bytes 1572864 | tf_op jit(solution)/shard_map/all_to_all | solution.py:335
  14.9 0.0 copy-done.4
  14.9 1.9 %collective-permute-start = (bf16[384,128]{1,0:T(8,128)(2,1)S(1)}, bf16[384,128]{1,0:T(8,128)(2,1)S(1)}, u32[]{:S(2)}, u32[]{:S(2)}) collective-permute-start(bf16[384,128]{1,0:T(8,128)(2,1)S(1)} %copy-done.4), channel_id=1, source_target_pairs={{0,24},{24,0},{1,25},{25,1},{2,26},{26,2},{3,27},{27,3},{4,28},{28... | collective-permute-start | bytes 294920 | tf_op jit(solution)/shard_map/ppermute | solution.py:339
  16.8 0.0 copy-done
  16.8 0.0 copy-done.1
  16.8 0.0 copy-done.2
  16.8 2.1 %tables.1 = (s32[33]{0:T(128)S(1)}, s32[39]{0:T(128)S(1)}, s32[4,4]{1,0:T(4,128)S(1)}, s32[4,768]{1,0:T(4,128)S(1)}, s32[4,768]{1,0:T(4,128)S(1)}) custom-call(s32[64]{0:T(128)S(1)} %copy-done.1, s32[4]{0:T(128)S(1)} %copy-done.2, s32[2,768]{1,0:T(2,128)S(1)} %copy-done), custom_call_target="tpu_custom_call" | custom-call | tf_op jit(solution)/shard_map/tables/pallas_call | solution.py:353
  19.0 6.1 %all_gather.6.q_own_ref = bf16[1536,128]{1,0:T(8,128)(2,1)S(1)} all-gather(bf16[384,128]{1,0:T(8,128)(2,1)S(1)} %copy-done.4), channel_id=1, replica_groups=mesh['y'=8,'xh'=2,'xl'=2,'zh'=3,'zm'=2,'zl'=2,'core'=2] {'zl','core'}, dimensions={0}, use_global_device_ids=true | all-gather | bytes 491520 | tf_op jit(solution)/shard_map/all_gather | solution.py:340
  25.1 0.0 collective-permute-done
  25.1 6.6 %all_gather.7.q_side_ref = bf16[1536,128]{1,0:T(8,128)(2,1)S(1)} all-gather(bf16[384,128]{1,0:T(8,128)(2,1)S(1)} %collective-permute-done), channel_id=1, replica_groups=mesh['y'=8,'xh'=2,'xl'=2,'zh'=3,'zm'=2,'zl'=2,'core'=2] {'zl','core'}, dimensions={0}, use_global_device_ids=true | all-gather | bytes 491520 | tf_op jit(solution)/shard_map/all_gather | solution.py:341
  31.7 1.1 %all-to-all-done.kv_ref = bf16[16,192,128]{2,1,0:T(8,128)(2,1)S(1)} async-done(((bf16[16,192,128]{2,1,0:T(8,128)(2,1)}), bf16[16,192,128]{2,1,0:T(8,128)(2,1)S(1)}, u32[]{:S(2)}, u32[]{:S(2)}) %all-to-all-start) | async-done | bytes 786464 | tf_op jit(solution)/shard_map/all_to_all | solution.py:335
  32.8 7.5 %attend.1 = bf16[8,400,128]{2,1,0:T(8,128)(2,1)} custom-call(s32[33]{0:T(128)S(1)} %get-tuple-element.14.rank_ref, s32[39]{0:T(128)S(1)} %get-tuple-element.15.sorted_ref, s32[4,4]{1,0:T(4,128)S(1)} %get-tuple-element.16.tile_ref, bf16[16,192,128]{2,1,0:T(8,128)(2,1)S(1)} %all-to-all-done.kv_ref, bf16[1536,128]{1,0:T(8,128)(2,1)S(1)} %all_gather.6.q_own_ref, ...), custom_call_target="tpu_custom_call" | custom-call | flops 2415919104 | bytes 4194304 | tf_op jit(solution)/shard_map/attend/pallas_call | solution.py:395
  40.3 0.0 copy-start.3
  40.3 6.1 %all-to-all-start.1 = ((bf16[8,400,128]{2,1,0:T(8,128)(2,1)}), bf16[8,400,128]{2,1,0:T(8,128)(2,1)S(1)}, u32[]{:S(2)}, u32[]{:S(2)}) async-start(bf16[8,400,128]{2,1,0:T(8,128)(2,1)} %attend.1), calls=%async_computation.1 | async-start | bytes 1638400 | tf_op jit(solution)/shard_map/all_to_all | solution.py:397
  46.4 0.0 copy-done.3
  46.4 3.4 %collective-permute-start.1 = (bf16[128,2048]{1,0:T(8,128)(2,1)S(1)}, bf16[128,2048]{1,0:T(8,128)(2,1)S(1)}, u32[]{:S(2)}, u32[]{:S(2)}) collective-permute-start(bf16[128,2048]{1,0:T(8,128)(2,1)S(1)} %copy-done.3), channel_id=1, source_target_pairs={{0,2},{2,0},{1,3},{3,1},{4,6},{6,4},{5,7},{7,5},{8,10},{10,8},{9,1... | collective-permute-start | bytes 1572872 | tf_op jit(solution)/shard_map/ppermute | solution.py:342
  49.8 19.3 %collective-permute-done.1 = bf16[128,2048]{1,0:T(8,128)(2,1)S(1)} collective-permute-done((bf16[128,2048]{1,0:T(8,128)(2,1)S(1)}, bf16[128,2048]{1,0:T(8,128)(2,1)S(1)}, u32[]{:S(2)}, u32[]{:S(2)}) %collective-permute-start.1) | collective-permute-done | bytes 524320 | tf_op jit(solution)/shard_map/ppermute | solution.py:342
  69.1 0.1 pad_maximum_fusion.w0_ref
  69.2 1.9 %collective-permute-start.2 = (bf16[2,128,2048]{2,1,0:T(8,128)(2,1)S(1)}, bf16[2,128,2048]{2,1,0:T(8,128)(2,1)S(1)}, u32[]{:S(2)}, u32[]{:S(2)}) collective-permute-start(bf16[2,128,2048]{2,1,0:T(8,128)(2,1)S(1)} %pad_maximum_fusion.w0_ref), channel_id=1, source_target_pairs={{0,1},{1,0},{2,3},{3,2},{4,5},{5,4},{6,7},{7,6},{8,9},{9,8},{10,11... | collective-permute-start | bytes 3145736 | tf_op jit(solution)/shard_map/ppermute | solution.py:399
  71.1 2.6 %collective-permute-done.2.w1_ref = bf16[2,128,2048]{2,1,0:T(8,128)(2,1)S(1)} collective-permute-done((bf16[2,128,2048]{2,1,0:T(8,128)(2,1)S(1)}, bf16[2,128,2048]{2,1,0:T(8,128)(2,1)S(1)}, u32[]{:S(2)}, u32[]{:S(2)}) %collective-permute-start.2) | collective-permute-done | bytes 1048608 | tf_op jit(solution)/shard_map/ppermute | solution.py:399
  73.7 0.0 all-to-all-done.1.got_ref
  73.8 1.3 %project.1 = bf16[96,2048]{1,0:T(8,128)(2,1)S(1)} custom-call(bf16[8,400,128]{2,1,0:T(8,128)(2,1)S(1)} %all-to-all-done.1.got_ref, bf16[2,128,2048]{2,1,0:T(8,128)(2,1)S(1)} %pad_maximum_fusion.w0_ref, bf16[2,128,2048]{2,1,0:T(8,128)(2,1)S(1)} %collective-permute-done.2.w1_ref), custom_call_target="tpu_custom_call" | custom-call | tf_op jit(solution)/shard_map/project/pallas_call | solution.py:400
  75.1 33.4 %all_to_all.15 = bf16[6,16,2048]{2,1,0:T(8,128)(2,1)S(1)} all-to-all(bf16[6,16,2048]{2,1,0:T(8,128)(2,1)S(1)} %bitcast.3), channel_id=1, replica_groups={{0,6,8,14,16,22},{1,7,9,15,17,23},{2,4,10,12,18,20},{3,5,11,13,19,21},{..., dimensions={0} | all-to-all | bytes 786432 | tf_op jit(solution)/shard_map/all_to_all | solution.py:409
  108.4 0.7 reduce_sum.12
Async XLA Ops:
  1.8 13.1 %copy-start.4 = (bf16[384,128]{1,0:T(8,128)(2,1)S(1)}, bf16[384,128]{1,0:T(8,128)(2,1)}, u32[]{:S(2)}) copy-start(bf16[384,128]{1,0:T(8,128)(2,1)} %param.7) | copy-start | bytes 294916
  1.8 15.0 %copy-start = (s32[2,768]{1,0:T(2,128)S(1)}, s32[2,768]{1,0:T(2,128)}, u32[]{:S(2)}) copy-start(s32[2,768]{1,0:T(2,128)} %constant.5.clone.lane_ref) | copy-start | bytes 18436
  1.8 15.0 %copy-start.1 = (s32[64]{0:T(128)S(1)}, s32[64]{0:T(128)}, u32[]{:S(2)}) copy-start(s32[64]{0:T(128)} %slot_ref.1) | copy-start | bytes 772
  1.9 15.0 %copy-start.2 = (s32[4]{0:T(128)S(1)}, s32[4]{0:T(128)}, u32[]{:S(2)}) copy-start(s32[4]{0:T(128)} %len_ref.1) | copy-start | bytes 52
  1.9 30.9 %all-to-all-start = ((bf16[16,192,128]{2,1,0:T(8,128)(2,1)}), bf16[16,192,128]{2,1,0:T(8,128)(2,1)S(1)}, u32[]{:S(2)}, u32[]{:S(2)}) async-start(bf16[16,192,128]{2,1,0:T(8,128)(2,1)} %spread.1), calls=%async_computation | async-start | bytes 1572864 | tf_op jit(solution)/shard_map/all_to_all | solution.py:335
  14.9 10.2 %collective-permute-start = (bf16[384,128]{1,0:T(8,128)(2,1)S(1)}, bf16[384,128]{1,0:T(8,128)(2,1)S(1)}, u32[]{:S(2)}, u32[]{:S(2)}) collective-permute-start(bf16[384,128]{1,0:T(8,128)(2,1)S(1)} %copy-done.4), channel_id=1, source_target_pairs={{0,24},{24,0},{1,25},{25,1},{2,26},{26,2},{3,27},{27,3},{4,28},{28... | collective-permute-start | bytes 294920 | tf_op jit(solution)/shard_map/ppermute | solution.py:339
  40.3 6.1 %copy-start.3 = (bf16[128,2048]{1,0:T(8,128)(2,1)S(1)}, bf16[128,2048]{1,0:T(8,128)(2,1)}, u32[]{:S(2)}) copy-start(bf16[128,2048]{1,0:T(8,128)(2,1)} %param.12) | copy-start | bytes 1572868
  40.3 33.5 %all-to-all-start.1 = ((bf16[8,400,128]{2,1,0:T(8,128)(2,1)}), bf16[8,400,128]{2,1,0:T(8,128)(2,1)S(1)}, u32[]{:S(2)}, u32[]{:S(2)}) async-start(bf16[8,400,128]{2,1,0:T(8,128)(2,1)} %attend.1), calls=%async_computation.1 | async-start | bytes 1638400 | tf_op jit(solution)/shard_map/all_to_all | solution.py:397
  46.4 22.7 %collective-permute-start.1 = (bf16[128,2048]{1,0:T(8,128)(2,1)S(1)}, bf16[128,2048]{1,0:T(8,128)(2,1)S(1)}, u32[]{:S(2)}, u32[]{:S(2)}) collective-permute-start(bf16[128,2048]{1,0:T(8,128)(2,1)S(1)} %copy-done.3), channel_id=1, source_target_pairs={{0,2},{2,0},{1,3},{3,1},{4,6},{6,4},{5,7},{7,5},{8,10},{10,8},{9,1... | collective-permute-start | bytes 1572872 | tf_op jit(solution)/shard_map/ppermute | solution.py:342
  69.2 4.6 %collective-permute-start.2 = (bf16[2,128,2048]{2,1,0:T(8,128)(2,1)S(1)}, bf16[2,128,2048]{2,1,0:T(8,128)(2,1)S(1)}, u32[]{:S(2)}, u32[]{:S(2)}) collective-permute-start(bf16[2,128,2048]{2,1,0:T(8,128)(2,1)S(1)} %pad_maximum_fusion.w0_ref), channel_id=1, source_target_pairs={{0,1},{1,0},{2,3},{3,2},{4,5},{5,4},{6,7},{7,6},{8,9},{9,8},{10,11... | collective-permute-start | bytes 3145736 | tf_op jit(solution)/shard_map/ppermute | solution.py:399

commit v7 on v6

--- a/solution.py
+++ b/solution.py
@@ -17,11 +17,7 @@
     [y * 4 + xh * 2 + (kind ^ xh) for y in range(8) for xh in range(2)]
     for kind in range(2)
 ]
-SUM_GROUPS = [
-    [p * 4 + (kind ^ p % 2) * 2 + core for p in range(6)]
-    for kind in range(2)
-    for core in range(2)
-]
+Z6 = ("zh", "zm")
 
 TOK = 384
 HALF = 192
@@ -36,6 +32,7 @@
 TILE = 4 * HALF
 LANES = 256
 ROWS = 128
+GROUPS = CHUNK // ROWS
 TEAM_SIZE = 8
 STAT = 16
 SEND = TOK + STAT
@@ -127,7 +124,7 @@
         tile_ref[tile, 1] = lax.div((high - low) * QUART + CHUNK - 1, CHUNK)
         tile_ref[tile, 2] = base
         tile_ref[tile, 3] = start_of(base + HALF - 1, bounds)
-        pos = lane_ref[pl.ds(lax.axis_index("zm") ^ half, 1), :] + base
+        pos = lane_ref[...] + base
         qpos_ref[tile : tile + 1, :] = pos
         qstart_ref[tile : tile + 1, :] = start_of(pos, bounds)
 
@@ -146,6 +143,7 @@
     k_scr,
     v_scr,
     q_scr,
+    s_scr,
     m_scr,
     l_scr,
     acc_scr,
@@ -167,8 +165,6 @@
         kpos_scr[n * QUART : (n + 1) * QUART, :] = row + sorted_ref[n] * HALF
     kpos_scr[KEYS:, :] = jnp.full((PAD - KEYS, HD), FAR, jnp.int32)
 
-    zm = lax.axis_index("zm")
-    flips = (zm * 32, (1 - zm) * 32)
     for tile in range(4):
         q_ref = (q_own_ref, q_side_ref)[tile // 2]
         half = tile % 2
@@ -176,16 +172,26 @@
             for j in range(4):
                 for z3 in range(3):
                     to = d * HALF + j * QUART + z3 * 16
-                    of = j * TOK + half * HALF + z3 * 64
-                    of = of + ((d * 16) ^ flips[(half * 3 + z3) % 2])
-                    rows = pl.ds(pl.multiple_of(of, 16), 16)
-                    q_scr[tile, to : to + 16, :] = q_ref[rows, :]
+                    of = j * TOK + half * HALF + z3 * 64 + d * 16
+                    q_scr[tile, to : to + 16, :] = q_ref[of : of + 16, :]
+
+    def score(tile, at, part, r):
+        return lax.dot_general(
+            k_scr[pl.ds(at + r * ROWS, ROWS), :],
+            q_scr[tile, part * LANES : (part + 1) * LANES, :],
+            (((1,), (1,)), ((), ())),
+            preferred_element_type=jnp.float32,
+        )
 
     def one_tile(tile, carry):
         low, steps, q_first, start_last = (tile_ref[tile, n] for n in range(4))
         m_scr[...] = jnp.full_like(m_scr, LOW)
         l_scr[...] = jnp.zeros_like(l_scr)
         acc_scr[...] = jnp.zeros_like(acc_scr)
+
+        start = pl.multiple_of(low * QUART, 16)
+        for r in range(GROUPS):
+            s_scr[r * ROWS : (r + 1) * ROWS, :] = score(tile, start, 0, r)
 
         def one_step(step, carry):
             first = low * QUART + step * CHUNK
@@ -194,34 +200,34 @@
             last_pos = sorted_ref[lax.div(first + CHUNK - 1, QUART)] * HALF + HALF - 1
             edge = (last_pos > q_first) | (first_pos < start_last)
 
+            after = pl.multiple_of(jnp.minimum(first + CHUNK, KEYS), 16)
+
             def block(masked):
                 parts = TILE // LANES
-                keys = [
-                    k_scr[pl.ds(at + r * ROWS, ROWS), :] for r in range(CHUNK // ROWS)
-                ]
                 vals = v_scr[pl.ds(at, CHUNK), :]
-
-                def score(part, r):
-                    cols = slice(part * LANES, (part + 1) * LANES)
-                    scores = lax.dot_general(
-                        keys[r],
-                        q_scr[tile, cols, :],
-                        (((1,), (1,)), ((), ())),
+                waiting = []
+
+                def collect():
+                    cols, factor, probs = waiting.pop(0)
+                    acc_scr[:, cols] = acc_scr[:, cols] * factor + lax.dot_general(
+                        vals,
+                        probs,
+                        (((0,), (0,)), ((), ())),
                         preferred_element_type=jnp.float32,
                     )
-                    if masked:
-                        key_pos = kpos_scr[pl.ds(at + r * ROWS, ROWS), :]
-                        key_pos = jnp.concatenate([key_pos] * (LANES // HD), axis=1)
-                        allowed = (key_pos <= qpos_ref[pl.ds(tile, 1), cols]) & (
-                            key_pos >= qstart_ref[pl.ds(tile, 1), cols]
-                        )
-                        scores = jnp.where(allowed, scores, LOW)
-                    return scores
-
-                ahead = [score(0, r) for r in range(CHUNK // ROWS)]
+
+                ahead = [s_scr[r * ROWS : (r + 1) * ROWS, :] for r in range(GROUPS)]
                 for part in range(parts):
                     cols = slice(part * LANES, (part + 1) * LANES)
                     now, ahead = ahead, []
+                    if masked:
+                        for r in range(GROUPS):
+                            key_pos = kpos_scr[pl.ds(at + r * ROWS, ROWS), :]
+                            key_pos = jnp.concatenate([key_pos] * (LANES // HD), axis=1)
+                            allowed = (key_pos <= qpos_ref[pl.ds(tile, 1), cols]) & (
+                                key_pos >= qstart_ref[pl.ds(tile, 1), cols]
+                            )
+                            now[r] = jnp.where(allowed, now[r], LOW)
                     high = now[0]
                     for scores in now[1:]:
                         high = jnp.maximum(high, scores)
@@ -232,19 +238,21 @@
                     probs, total = [], None
                     for r, scores in enumerate(now):
                         if part + 1 < parts:
-                            ahead.append(score(part + 1, r))
+                            ahead.append(score(tile, at, part + 1, r))
+                        else:
+                            ahead.append(score(tile, after, 0, r))
                         prob = jnp.exp2((scores - new) * SCALE)
                         total = prob if total is None else total + prob
                         probs.append(prob.astype(jnp.bfloat16))
                     l_scr[:, cols] = l_scr[:, cols] * factor + jnp.sum(
                         total, axis=0, keepdims=True
                     )
-                    acc_scr[:, cols] = acc_scr[:, cols] * factor + lax.dot_general(
-                        vals,
-                        jnp.concatenate(probs, axis=0),
-                        (((0,), (0,)), ((), ())),
-                        preferred_element_type=jnp.float32,
-                    )
+                    waiting.append((cols, factor, jnp.concatenate(probs, axis=0)))
+                    if part:
+                        collect()
+                collect()
+                for r in range(GROUPS):
+                    s_scr[r * ROWS : (r + 1) * ROWS, :] = ahead[r]
 
             pl.when(edge)(lambda: block(True))
             pl.when(jnp.logical_not(edge))(lambda: block(False))
@@ -342,13 +350,7 @@
     w_side = lax.ppermute(out_weight, "zl", flip)
 
     lane = np.arange(TILE)
-    third = lane % QUART // 16
-    in_half = np.stack(
-        [
-            third * 64 + (lane // HALF * 16 ^ (n ^ third % 2) * 32) + lane % 16
-            for n in range(2)
-        ]
-    )
+    in_half = lane % QUART // 16 * 64 + lane // HALF * 16 + lane % 16
     i32 = jnp.int32
     rank, in_order, tiles, q_pos, q_start = pl.pallas_call(
         table_kernel,
@@ -367,7 +369,7 @@
         ],
         compiler_params=pltpu.CompilerParams(vmem_limit_bytes=8 << 20),
         name="tables",
-    )(block_of_slot, doc_lengths, jnp.asarray(in_half, i32))
+    )(block_of_slot, doc_lengths, jnp.asarray(in_half[None, :], i32))
 
     attend = pl.pallas_call(
         attend_kernel,
@@ -379,6 +381,7 @@
             pltpu.VMEM((PAD, HD), jnp.bfloat16),
             pltpu.VMEM((PAD, HD), jnp.bfloat16),
             pltpu.VMEM((4, TILE, HD), jnp.bfloat16),
+            pltpu.VMEM((CHUNK, LANES), jnp.float32),
             pltpu.VMEM((1, TILE), jnp.float32),
             pltpu.VMEM((1, TILE), jnp.float32),
             pltpu.VMEM((HD, TILE), jnp.float32),
@@ -407,7 +410,7 @@
         name="project",
     )(got, w0, w1)
     parts = lax.all_to_all(
-        terms.reshape(6, 16, -1), HEAD, 0, 0, axis_index_groups=SUM_GROUPS, tiled=True
+        terms.reshape(6, 16, -1), Z6, 0, 0, tiled=True
     )
     return jnp.sum(parts.astype(jnp.float32), axis=0).astype(jnp.bfloat16)
 

time: 111 us -> 110 us (level)
  no operation moved by 1% of the time
where the time goes in v7:
time: 110 us; the launch traced here: 108 us
  blocking collectives  45.5 us (41%)
  starting transfers between devices  26.3 us (24%)
  waiting for transfers between devices  23.1 us (21%)
  Pallas kernels  11.9 us (11%)
    all_to_all x1, blocking collectives, per_device(): parts = lax.all_to_all(terms.reshape(6, 16, -1), Z6, 0, 0, tiled=True)  32.8 us
    ppermute x1, waiting for transfers between devices, per_device(): w_side = lax.ppermute(out_weight, 'zl', flip)  19.3 us
    all_to_all x1, starting transfers between devices, per_device(): lax.all_to_all(spread, DP, 0, 0, axis_index_groups=KV_GROUPS, tiled=True)  13 us
    pallas_call x1, Pallas kernels, per_device(): sent = attend(rank, in_order, tiles, kv, q, q_side, q_pos, q_start)  6.68 us
    all_gather x1, blocking collectives, per_device(): q_side = lax.all_gather(q_side, ('zl', 'core'), axis=0, tiled=True)  6.55 us
    all_gather x1, blocking collectives, per_device(): q = lax.all_gather(queries, ('zl', 'core'), axis=0, tiled=True)  6.14 us
    all_to_all x1, starting transfers between devices, per_device(): got = lax.all_to_all(sent, TEAM, 0, 0, tiled=True)  6.14 us
    ppermute x1, starting transfers between devices, per_device(): w_side = lax.ppermute(out_weight, 'zl', flip)  3.36 us
  transfers between devices with their start and end apart: 5, of which 3 were waited for; matrix products, arithmetic and copies ran while one was open for 0% of the time, Pallas kernels for 2%

profile of v7, /device:TPU:6, one launch (start us, length us, event | category | flops | bytes accessed | tf_op | source)
XLA Modules:
  0.0 107.8 jit_solution(11471363523566817300)
XLA Ops:
  0.0 1.8 %spread.1 = bf16[16,192,128]{2,1,0:T(8,128)(2,1)} custom-call(bf16[384,384]{1,0:T(8,128)(2,1)} %k_hbm.1, bf16[384,384]{1,0:T(8,128)(2,1)} %v_hbm.1), custom_call_target="tpu_custom_call" | custom-call | tf_op jit(solution)/shard_map/spread/pallas_call | solution.py:328
  1.8 0.0 copy-start.4
  1.8 0.0 copy-start
  1.8 0.0 copy-start.1
  1.9 0.0 copy-start.2
  1.9 13.0 %all-to-all-start = ((bf16[16,192,128]{2,1,0:T(8,128)(2,1)}), bf16[16,192,128]{2,1,0:T(8,128)(2,1)S(1)}, u32[]{:S(2)}, u32[]{:S(2)}) async-start(bf16[16,192,128]{2,1,0:T(8,128)(2,1)} %spread.1), calls=%async_computation | async-start | bytes 1572864 | tf_op jit(solution)/shard_map/all_to_all | solution.py:343
  14.9 0.0 copy-done.4
  14.9 1.9 %collective-permute-start = (bf16[384,128]{1,0:T(8,128)(2,1)S(1)}, bf16[384,128]{1,0:T(8,128)(2,1)S(1)}, u32[]{:S(2)}, u32[]{:S(2)}) collective-permute-start(bf16[384,128]{1,0:T(8,128)(2,1)S(1)} %copy-done.4), channel_id=1, source_target_pairs={{0,24},{24,0},{1,25},{25,1},{2,26},{26,2},{3,27},{27,3},{4,28},{28... | collective-permute-start | bytes 294920 | tf_op jit(solution)/shard_map/ppermute | solution.py:347
  16.8 0.0 copy-done
  16.8 0.0 copy-done.1
  16.8 0.0 copy-done.2
  16.8 2.1 %tables.1 = (s32[33]{0:T(128)S(1)}, s32[39]{0:T(128)S(1)}, s32[4,4]{1,0:T(4,128)S(1)}, s32[4,768]{1,0:T(4,128)S(1)}, s32[4,768]{1,0:T(4,128)S(1)}) custom-call(s32[64]{0:T(128)S(1)} %copy-done.1, s32[4]{0:T(128)S(1)} %copy-done.2, s32[1,768]{1,0:T(1,128)S(1)} %copy-done), custom_call_target="tpu_custom_call" | custom-call | tf_op jit(solution)/shard_map/tables/pallas_call | solution.py:355
  19.0 6.1 %all_gather.6.q_own_ref = bf16[1536,128]{1,0:T(8,128)(2,1)S(1)} all-gather(bf16[384,128]{1,0:T(8,128)(2,1)S(1)} %copy-done.4), channel_id=1, replica_groups=mesh['y'=8,'xh'=2,'xl'=2,'zh'=3,'zm'=2,'zl'=2,'core'=2] {'zl','core'}, dimensions={0}, use_global_device_ids=true | all-gather | bytes 491520 | tf_op jit(solution)/shard_map/all_gather | solution.py:348
  25.1 0.0 collective-permute-done
  25.1 6.6 %all_gather.7.q_side_ref = bf16[1536,128]{1,0:T(8,128)(2,1)S(1)} all-gather(bf16[384,128]{1,0:T(8,128)(2,1)S(1)} %collective-permute-done), channel_id=1, replica_groups=mesh['y'=8,'xh'=2,'xl'=2,'zh'=3,'zm'=2,'zl'=2,'core'=2] {'zl','core'}, dimensions={0}, use_global_device_ids=true | all-gather | bytes 491520 | tf_op jit(solution)/shard_map/all_gather | solution.py:349
  31.7 1.1 %all-to-all-done.kv_ref = bf16[16,192,128]{2,1,0:T(8,128)(2,1)S(1)} async-done(((bf16[16,192,128]{2,1,0:T(8,128)(2,1)}), bf16[16,192,128]{2,1,0:T(8,128)(2,1)S(1)}, u32[]{:S(2)}, u32[]{:S(2)}) %all-to-all-start) | async-done | bytes 786464 | tf_op jit(solution)/shard_map/all_to_all | solution.py:343
  32.8 6.7 %attend.1 = bf16[8,400,128]{2,1,0:T(8,128)(2,1)} custom-call(s32[33]{0:T(128)S(1)} %get-tuple-element.14.rank_ref, s32[39]{0:T(128)S(1)} %get-tuple-element.15.sorted_ref, s32[4,4]{1,0:T(4,128)S(1)} %get-tuple-element.16.tile_ref, bf16[16,192,128]{2,1,0:T(8,128)(2,1)S(1)} %all-to-all-done.kv_ref, bf16[1536,128]{1,0:T(8,128)(2,1)S(1)} %all_gather.6.q_own_ref, ...), custom_call_target="tpu_custom_call" | custom-call | flops 2415919104 | bytes 4194304 | tf_op jit(solution)/shard_map/attend/pallas_call | solution.py:398
  39.5 0.0 copy-start.3
  39.5 6.1 %all-to-all-start.1 = ((bf16[8,400,128]{2,1,0:T(8,128)(2,1)}), bf16[8,400,128]{2,1,0:T(8,128)(2,1)S(1)}, u32[]{:S(2)}, u32[]{:S(2)}) async-start(bf16[8,400,128]{2,1,0:T(8,128)(2,1)} %attend.1), calls=%async_computation.1 | async-start | bytes 1638400 | tf_op jit(solution)/shard_map/all_to_all | solution.py:400
  45.6 0.0 copy-done.3
  45.6 3.4 %collective-permute-start.1 = (bf16[128,2048]{1,0:T(8,128)(2,1)S(1)}, bf16[128,2048]{1,0:T(8,128)(2,1)S(1)}, u32[]{:S(2)}, u32[]{:S(2)}) collective-permute-start(bf16[128,2048]{1,0:T(8,128)(2,1)S(1)} %copy-done.3), channel_id=1, source_target_pairs={{0,2},{2,0},{1,3},{3,1},{4,6},{6,4},{5,7},{7,5},{8,10},{10,8},{9,1... | collective-permute-start | bytes 1572872 | tf_op jit(solution)/shard_map/ppermute | solution.py:350
  49.0 19.3 %collective-permute-done.1 = bf16[128,2048]{1,0:T(8,128)(2,1)S(1)} collective-permute-done((bf16[128,2048]{1,0:T(8,128)(2,1)S(1)}, bf16[128,2048]{1,0:T(8,128)(2,1)S(1)}, u32[]{:S(2)}, u32[]{:S(2)}) %collective-permute-start.1) | collective-permute-done | bytes 524320 | tf_op jit(solution)/shard_map/ppermute | solution.py:350
  68.3 0.1 pad_maximum_fusion.w0_ref
  68.4 1.9 %collective-permute-start.2 = (bf16[2,128,2048]{2,1,0:T(8,128)(2,1)S(1)}, bf16[2,128,2048]{2,1,0:T(8,128)(2,1)S(1)}, u32[]{:S(2)}, u32[]{:S(2)}) collective-permute-start(bf16[2,128,2048]{2,1,0:T(8,128)(2,1)S(1)} %pad_maximum_fusion.w0_ref), channel_id=1, source_target_pairs={{0,1},{1,0},{2,3},{3,2},{4,5},{5,4},{6,7},{7,6},{8,9},{9,8},{10,11... | collective-permute-start | bytes 3145736 | tf_op jit(solution)/shard_map/ppermute | solution.py:402
  70.3 2.6 %collective-permute-done.2.w1_ref = bf16[2,128,2048]{2,1,0:T(8,128)(2,1)S(1)} collective-permute-done((bf16[2,128,2048]{2,1,0:T(8,128)(2,1)S(1)}, bf16[2,128,2048]{2,1,0:T(8,128)(2,1)S(1)}, u32[]{:S(2)}, u32[]{:S(2)}) %collective-permute-start.2) | collective-permute-done | bytes 1048608 | tf_op jit(solution)/shard_map/ppermute | solution.py:402
  72.9 0.0 all-to-all-done.1.got_ref
  72.9 1.3 %project.1 = bf16[96,2048]{1,0:T(8,128)(2,1)S(1)} custom-call(bf16[8,400,128]{2,1,0:T(8,128)(2,1)S(1)} %all-to-all-done.1.got_ref, bf16[2,128,2048]{2,1,0:T(8,128)(2,1)S(1)} %pad_maximum_fusion.w0_ref, bf16[2,128,2048]{2,1,0:T(8,128)(2,1)S(1)} %collective-permute-done.2.w1_ref), custom_call_target="tpu_custom_call" | custom-call | tf_op jit(solution)/shard_map/project/pallas_call | solution.py:403
  74.3 32.8 %all_to_all.15 = bf16[6,16,2048]{2,1,0:T(8,128)(2,1)S(1)} all-to-all(bf16[6,16,2048]{2,1,0:T(8,128)(2,1)S(1)} %bitcast.3), channel_id=1, replica_groups=mesh['y'=8,'xh'=2,'xl'=2,'zh'=3,'zm'=2,'zl'=2,'core'=2] {'zh','zm'}, dimensions={0} | all-to-all | bytes 786432 | tf_op jit(solution)/shard_map/all_to_all | solution.py:412
  107.1 0.7 reduce_sum.12
Async XLA Ops:
  1.8 13.1 %copy-start.4 = (bf16[384,128]{1,0:T(8,128)(2,1)S(1)}, bf16[384,128]{1,0:T(8,128)(2,1)}, u32[]{:S(2)}) copy-start(bf16[384,128]{1,0:T(8,128)(2,1)} %param.7) | copy-start | bytes 294916
  1.8 15.0 %copy-start = (s32[1,768]{1,0:T(1,128)S(1)}, s32[1,768]{1,0:T(1,128)}, u32[]{:S(2)}) copy-start(s32[1,768]{1,0:T(1,128)} %constant.5.clone.lane_ref) | copy-start | bytes 9220
  1.8 15.0 %copy-start.1 = (s32[64]{0:T(128)S(1)}, s32[64]{0:T(128)}, u32[]{:S(2)}) copy-start(s32[64]{0:T(128)} %slot_ref.1) | copy-start | bytes 772
  1.9 15.0 %copy-start.2 = (s32[4]{0:T(128)S(1)}, s32[4]{0:T(128)}, u32[]{:S(2)}) copy-start(s32[4]{0:T(128)} %len_ref.1) | copy-start | bytes 52
  1.9 30.9 %all-to-all-start = ((bf16[16,192,128]{2,1,0:T(8,128)(2,1)}), bf16[16,192,128]{2,1,0:T(8,128)(2,1)S(1)}, u32[]{:S(2)}, u32[]{:S(2)}) async-start(bf16[16,192,128]{2,1,0:T(8,128)(2,1)} %spread.1), calls=%async_computation | async-start | bytes 1572864 | tf_op jit(solution)/shard_map/all_to_all | solution.py:343
  14.9 10.2 %collective-permute-start = (bf16[384,128]{1,0:T(8,128)(2,1)S(1)}, bf16[384,128]{1,0:T(8,128)(2,1)S(1)}, u32[]{:S(2)}, u32[]{:S(2)}) collective-permute-start(bf16[384,128]{1,0:T(8,128)(2,1)S(1)} %copy-done.4), channel_id=1, source_target_pairs={{0,24},{24,0},{1,25},{25,1},{2,26},{26,2},{3,27},{27,3},{4,28},{28... | collective-permute-start | bytes 294920 | tf_op jit(solution)/shard_map/ppermute | solution.py:347
  39.5 6.1 %copy-start.3 = (bf16[128,2048]{1,0:T(8,128)(2,1)S(1)}, bf16[128,2048]{1,0:T(8,128)(2,1)}, u32[]{:S(2)}) copy-start(bf16[128,2048]{1,0:T(8,128)(2,1)} %param.12) | copy-start | bytes 1572868
  39.5 33.5 %all-to-all-start.1 = ((bf16[8,400,128]{2,1,0:T(8,128)(2,1)}), bf16[8,400,128]{2,1,0:T(8,128)(2,1)S(1)}, u32[]{:S(2)}, u32[]{:S(2)}) async-start(bf16[8,400,128]{2,1,0:T(8,128)(2,1)} %attend.1), calls=%async_computation.1 | async-start | bytes 1638400 | tf_op jit(solution)/shard_map/all_to_all | solution.py:400
  45.6 22.7 %collective-permute-start.1 = (bf16[128,2048]{1,0:T(8,128)(2,1)S(1)}, bf16[128,2048]{1,0:T(8,128)(2,1)S(1)}, u32[]{:S(2)}, u32[]{:S(2)}) collective-permute-start(bf16[128,2048]{1,0:T(8,128)(2,1)S(1)} %copy-done.3), channel_id=1, source_target_pairs={{0,2},{2,0},{1,3},{3,1},{4,6},{6,4},{5,7},{7,5},{8,10},{10,8},{9,1... | collective-permute-start | bytes 1572872 | tf_op jit(solution)/shard_map/ppermute | solution.py:350
  68.4 4.6 %collective-permute-start.2 = (bf16[2,128,2048]{2,1,0:T(8,128)(2,1)S(1)}, bf16[2,128,2048]{2,1,0:T(8,128)(2,1)S(1)}, u32[]{:S(2)}, u32[]{:S(2)}) collective-permute-start(bf16[2,128,2048]{2,1,0:T(8,128)(2,1)S(1)} %pad_maximum_fusion.w0_ref), channel_id=1, source_target_pairs={{0,1},{1,0},{2,3},{3,2},{4,5},{5,4},{6,7},{7,6},{8,9},{9,8},{10,11... | collective-permute-start | bytes 3145736 | tf_op jit(solution)/shard_map/ppermute | solution.py:402

commit v8 on v7

--- a/solution.py
+++ b/solution.py
@@ -13,22 +13,18 @@
 DP = ("y", "xh", "xl")
 HEAD = ("zh", "zm", "zl", "core")
 TEAM = ("xl", "zl", "core")
-KV_GROUPS = [
-    [y * 4 + xh * 2 + (kind ^ xh) for y in range(8) for xh in range(2)]
-    for kind in range(2)
-]
 Z6 = ("zh", "zm")
 
 TOK = 384
 HALF = 192
 HD = 128
 QUART = 48
-SRC = 16
+KROWS = 24
+SRC = 32
 PIECES = 2 * SRC
 CHUNK = 256
-KEYS = PIECES * QUART
+KEYS = PIECES * KROWS
 PAD = KEYS + CHUNK
-SLOTS = PIECES + CHUNK // QUART + 2
 TILE = 4 * HALF
 LANES = 256
 ROWS = 128
@@ -41,26 +37,32 @@
 SCALE = math.log2(math.e) / math.sqrt(HD)
 
 
+def team_index():
+    own = lax.axis_index("zl") * 2 + lax.axis_index("core")
+    return lax.axis_index("xl") * 4 + own
+
+
 def spread_kernel(k_hbm, v_hbm, out_hbm, buf, in_sem, out_sem):
     own = lax.axis_index("zl") * 2 + lax.axis_index("core")
-    row = pl.multiple_of(own * QUART, 16)
     col = pl.multiple_of(lax.axis_index("zh") * HD, HD)
     loads = []
-    for n, src in enumerate((k_hbm, v_hbm)):
-        for half in range(2):
-            loads.append(
-                pltpu.make_async_copy(
-                    src.at[pl.ds(half * HALF + row, QUART), pl.ds(col, HD)],
-                    buf.at[pl.ds((2 * n + half) * QUART, QUART), :],
-                    in_sem.at[2 * n + half],
+    for side in range(2):
+        row = pl.multiple_of((side * 4 + own) * KROWS, 8)
+        for n, src in enumerate((k_hbm, v_hbm)):
+            for half in range(2):
+                loads.append(
+                    pltpu.make_async_copy(
+                        src.at[pl.ds(half * HALF + row, KROWS), pl.ds(col, HD)],
+                        buf.at[side, pl.ds((2 * n + half) * KROWS, KROWS), :],
+                        in_sem.at[4 * side + 2 * n + half],
+                    )
                 )
-            )
     for copy in loads:
         copy.start()
     for copy in loads:
         copy.wait()
     stores = [
-        pltpu.make_async_copy(buf, out_hbm.at[n], out_sem.at[n]) for n in range(SRC)
+        pltpu.make_async_copy(buf.at[n % 2], out_hbm.at[n], out_sem.at[n]) for n in range(SRC)
     ]
     for copy in stores:
         copy.start()
@@ -75,53 +77,18 @@
     return start
 
 
-def table_kernel(
-    slot_ref,
-    len_ref,
-    lane_ref,
-    rank_ref,
-    sorted_ref,
-    tile_ref,
-    qpos_ref,
-    qstart_ref,
-    where_scr,
-    before_scr,
-):
-    xl = lax.axis_index("xl")
+def table_kernel(slot_ref, len_ref, lane_ref, tile_ref, qpos_ref, qstart_ref):
     here = lax.axis_index("y") * 2 + lax.axis_index("xh")
-    kind = xl ^ lax.axis_index("xh")
-
-    def clear(n, carry):
-        where_scr[n] = PIECES
-        return carry
-
-    lax.fori_loop(0, 2 * PIECES, clear, 0)
-    for piece in range(PIECES):
-        src, half = divmod(piece, 2)
-        side = 2 * (kind ^ (src % 2))
-        where_scr[slot_ref[4 * src + side + half]] = piece
-
-    def walk(block, count):
-        before_scr[block] = count
-        piece = where_scr[block]
-        rank_ref[piece] = count
-        sorted_ref[count] = block
-        return count + (piece < PIECES).astype(jnp.int32)
-
-    before_scr[2 * PIECES] = lax.fori_loop(0, 2 * PIECES, walk, jnp.int32(0))
-    for n in range(PIECES, SLOTS):
-        sorted_ref[n] = FAR // HALF
     bounds = [len_ref[0]]
     for n in range(1, len_ref.shape[0] - 1):
         bounds.append(bounds[-1] + len_ref[n])
     for tile in range(4):
         rel, half = divmod(tile, 2)
-        block = slot_ref[4 * here + 2 * (xl ^ rel) + half]
+        block = slot_ref[4 * here + 2 * (lax.axis_index("xl") ^ rel) + half]
         base = block * HALF
-        low = before_scr[lax.div(start_of(base, bounds), HALF)]
-        high = before_scr[block + 1]
+        low = lax.div(start_of(base, bounds), HALF)
         tile_ref[tile, 0] = low
-        tile_ref[tile, 1] = lax.div((high - low) * QUART + CHUNK - 1, CHUNK)
+        tile_ref[tile, 1] = lax.div((block + 1 - low) * KROWS + CHUNK - 1, CHUNK)
         tile_ref[tile, 2] = base
         tile_ref[tile, 3] = start_of(base + HALF - 1, bounds)
         pos = lane_ref[...] + base
@@ -130,8 +97,7 @@
 
 
 def attend_kernel(
-    rank_ref,
-    sorted_ref,
+    slot_ref,
     tile_ref,
     kv_ref,
     q_own_ref,
@@ -151,18 +117,16 @@
 ):
     for piece in range(PIECES):
         src, half = divmod(piece, 2)
-        at = pl.multiple_of(rank_ref[piece] * QUART, 16)
-        k_scr[pl.ds(at, QUART), :] = kv_ref[src, half * QUART : (half + 1) * QUART, :]
-        v_scr[pl.ds(at, QUART), :] = kv_ref[
-            src, (2 + half) * QUART : (3 + half) * QUART, :
-        ]
-    k_scr[KEYS:, :] = jnp.zeros((CHUNK, HD), jnp.bfloat16)
-    v_scr[KEYS:, :] = jnp.zeros((CHUNK, HD), jnp.bfloat16)
+        at = pl.multiple_of(slot_ref[piece] * KROWS, 8)
+        for n, scr in enumerate((k_scr, v_scr)):
+            rows = slice((2 * n + half) * KROWS, (2 * n + half + 1) * KROWS)
+            scr[pl.ds(at, KROWS), :] = kv_ref[src, rows, :].astype(jnp.float32)
+    k_scr[KEYS:, :] = jnp.zeros((CHUNK, HD), jnp.float32)
+    v_scr[KEYS:, :] = jnp.zeros((CHUNK, HD), jnp.float32)
     st_scr[...] = jnp.zeros_like(st_scr)
-    own = lax.axis_index("zl") * 2 + lax.axis_index("core")
-    row = lax.broadcasted_iota(jnp.int32, (QUART, HD), 0) + own * QUART
+    row = lax.broadcasted_iota(jnp.int32, (KROWS, HD), 0) + team_index() * KROWS
     for n in range(PIECES):
-        kpos_scr[n * QUART : (n + 1) * QUART, :] = row + sorted_ref[n] * HALF
+        kpos_scr[n * KROWS : (n + 1) * KROWS, :] = row + n * HALF
     kpos_scr[KEYS:, :] = jnp.full((PAD - KEYS, HD), FAR, jnp.int32)
 
     for tile in range(4):
@@ -177,7 +141,7 @@
 
     def score(tile, at, part, r):
         return lax.dot_general(
-            k_scr[pl.ds(at + r * ROWS, ROWS), :],
+            k_scr[pl.ds(at + r * ROWS, ROWS), :].astype(jnp.bfloat16),
             q_scr[tile, part * LANES : (part + 1) * LANES, :],
             (((1,), (1,)), ((), ())),
             preferred_element_type=jnp.float32,
@@ -189,22 +153,22 @@
         l_scr[...] = jnp.zeros_like(l_scr)
         acc_scr[...] = jnp.zeros_like(acc_scr)
 
-        start = pl.multiple_of(low * QUART, 16)
+        start = pl.multiple_of(low * KROWS, 8)
         for r in range(GROUPS):
             s_scr[r * ROWS : (r + 1) * ROWS, :] = score(tile, start, 0, r)
 
         def one_step(step, carry):
-            first = low * QUART + step * CHUNK
-            at = pl.multiple_of(first, 16)
-            first_pos = sorted_ref[lax.div(first, QUART)] * HALF
-            last_pos = sorted_ref[lax.div(first + CHUNK - 1, QUART)] * HALF + HALF - 1
+            first = low * KROWS + step * CHUNK
+            at = pl.multiple_of(first, 8)
+            first_pos = lax.div(first, KROWS) * HALF
+            last_pos = lax.div(first + CHUNK - 1, KROWS) * HALF + HALF - 1
             edge = (last_pos > q_first) | (first_pos < start_last)
 
-            after = pl.multiple_of(jnp.minimum(first + CHUNK, KEYS), 16)
+            after = pl.multiple_of(jnp.minimum(first + CHUNK, KEYS), 8)
 
             def block(masked):
                 parts = TILE // LANES
-                vals = v_scr[pl.ds(at, CHUNK), :]
+                vals = v_scr[pl.ds(at, CHUNK), :].astype(jnp.bfloat16)
                 waiting = []
 
                 def collect():
@@ -327,12 +291,12 @@
     vmem = pl.BlockSpec(memory_space=pltpu.VMEM)
     spread = pl.pallas_call(
         spread_kernel,
-        out_shape=jax.ShapeDtypeStruct((SRC, 4 * QUART, HD), jnp.bfloat16),
+        out_shape=jax.ShapeDtypeStruct((SRC, 4 * KROWS, HD), jnp.bfloat16),
         in_specs=[hbm, hbm],
         out_specs=hbm,
         scratch_shapes=[
-            pltpu.VMEM((4 * QUART, HD), jnp.bfloat16),
-            pltpu.SemaphoreType.DMA((4,)),
+            pltpu.VMEM((2, 4 * KROWS, HD), jnp.bfloat16),
+            pltpu.SemaphoreType.DMA((8,)),
             pltpu.SemaphoreType.DMA((SRC,)),
         ],
         name="spread",
@@ -340,9 +304,7 @@
     spread, queries, out_weight = lax.optimization_barrier(
         (spread, queries, out_weight)
     )
-    kv = lax.all_to_all(
-        spread, DP, 0, 0, axis_index_groups=KV_GROUPS, tiled=True
-    )
+    kv = lax.all_to_all(spread, DP, 0, 0, tiled=True)
     flip = [(0, 1), (1, 0)]
     q_side = lax.ppermute(queries, "xl", flip)
     q = lax.all_gather(queries, ("zl", "core"), axis=0, tiled=True)
@@ -352,21 +314,15 @@
     lane = np.arange(TILE)
     in_half = lane % QUART // 16 * 64 + lane // HALF * 16 + lane % 16
     i32 = jnp.int32
-    rank, in_order, tiles, q_pos, q_start = pl.pallas_call(
+    tiles, q_pos, q_start = pl.pallas_call(
         table_kernel,
         out_shape=(
-            jax.ShapeDtypeStruct((PIECES + 1,), i32),
-            jax.ShapeDtypeStruct((SLOTS,), i32),
             jax.ShapeDtypeStruct((4, 4), i32),
             jax.ShapeDtypeStruct((4, TILE), i32),
             jax.ShapeDtypeStruct((4, TILE), i32),
         ),
         in_specs=[smem, smem, vmem],
-        out_specs=(smem, smem, smem, vmem, vmem),
-        scratch_shapes=[
-            pltpu.SMEM((2 * PIECES,), i32),
-            pltpu.SMEM((2 * PIECES + 1,), i32),
-        ],
+        out_specs=(smem, vmem, vmem),
         compiler_params=pltpu.CompilerParams(vmem_limit_bytes=8 << 20),
         name="tables",
     )(block_of_slot, doc_lengths, jnp.asarray(in_half[None, :], i32))
@@ -374,12 +330,12 @@
     attend = pl.pallas_call(
         attend_kernel,
         out_shape=jax.ShapeDtypeStruct((TEAM_SIZE, SEND, HD), jnp.bfloat16),
-        in_specs=[smem, smem, smem, vmem, vmem, vmem, vmem, vmem],
+        in_specs=[smem, smem, vmem, vmem, vmem, vmem, vmem],
         out_specs=vmem,
         scratch_shapes=[
             pltpu.VMEM((PAD, HD), jnp.int32),
-            pltpu.VMEM((PAD, HD), jnp.bfloat16),
-            pltpu.VMEM((PAD, HD), jnp.bfloat16),
+            pltpu.VMEM((PAD, HD), jnp.float32),
+            pltpu.VMEM((PAD, HD), jnp.float32),
             pltpu.VMEM((4, TILE, HD), jnp.bfloat16),
             pltpu.VMEM((CHUNK, LANES), jnp.float32),
             pltpu.VMEM((1, TILE), jnp.float32),
@@ -395,7 +351,7 @@
         ),
         name="attend",
     )
-    sent = attend(rank, in_order, tiles, kv, q, q_side, q_pos, q_start)
+    sent = attend(block_of_slot, tiles, kv, q, q_side, q_pos, q_start)
     _, w_side = lax.optimization_barrier((sent, w_side))
     got = lax.all_to_all(sent, TEAM, 0, 0, tiled=True)
     w0 = jnp.stack([out_weight, w_side])

time: 110 us -> 110 us (level); the launches traced: 108 us -> 109 us
  waiting for transfers between devices: 23.1 us -> 24.8 us
    all_to_all x1, waiting for transfers between devices: 1.1 us -> 2.86 us  [per_device(): kv = lax.all_to_all(spread, DP, 0, 0, tiled=True)]
  transfers between devices with their start and end apart: 5 -> 5, of which waited for: 3 -> 3; matrix products, arithmetic and copies ran while one was open for 0% -> 0% of each run, Pallas kernels for 2% -> 1%
where the time goes in v8:
time: 110 us; the launch traced here: 109 us
  blocking collectives  45.5 us (41%)
  starting transfers between devices  26.5 us (24%)
  waiting for transfers between devices  24.8 us (23%)
  Pallas kernels  11.3 us (10%)
    all_to_all x1, blocking collectives, per_device(): parts = lax.all_to_all(terms.reshape(6, 16, -1), Z6, 0, 0, tiled=True)  32.8 us
    ppermute x1, waiting for transfers between devices, per_device(): w_side = lax.ppermute(out_weight, 'zl', flip)  19.3 us
    all_to_all x1, starting transfers between devices, per_device(): kv = lax.all_to_all(spread, DP, 0, 0, tiled=True)  13.2 us
    pallas_call x1, Pallas kernels, per_device(): sent = attend(block_of_slot, tiles, kv, q, q_side, q_pos, q_start)  6.7 us
    all_gather x1, blocking collectives, per_device(): q_side = lax.all_gather(q_side, ('zl', 'core'), axis=0, tiled=True)  6.55 us
    all_gather x1, blocking collectives, per_device(): q = lax.all_gather(queries, ('zl', 'core'), axis=0, tiled=True)  6.14 us
    all_to_all x1, starting transfers between devices, per_device(): got = lax.all_to_all(sent, TEAM, 0, 0, tiled=True)  5.25 us
    ppermute x1, starting transfers between devices, per_device(): w_side = lax.ppermute(out_weight, 'zl', flip)  3.36 us
  transfers between devices with their start and end apart: 5, of which 3 were waited for; matrix products, arithmetic and copies ran while one was open for 0% of the time, Pallas kernels for 1%

profile of v8, /device:TPU:6, one launch (start us, length us, event | category | flops | bytes accessed | tf_op | source)
XLA Modules:
  0.0 109.0 jit_solution(5844259518125808162)
XLA Ops:
  0.0 2.0 %spread.1 = bf16[32,96,128]{2,1,0:T(8,128)(2,1)} custom-call(bf16[384,384]{1,0:T(8,128)(2,1)} %k_hbm.1, bf16[384,384]{1,0:T(8,128)(2,1)} %v_hbm.1), custom_call_target="tpu_custom_call" | custom-call | tf_op jit(solution)/shard_map/spread/pallas_call | solution.py:292
  2.0 0.0 copy-start.4
  2.1 0.0 copy-start
  2.1 0.0 copy-start.1
  2.1 0.0 copy-start.2
  2.1 13.2 %all-to-all-start = ((bf16[32,96,128]{2,1,0:T(8,128)(2,1)}), bf16[32,96,128]{2,1,0:T(8,128)(2,1)S(1)}, u32[]{:S(2)}, u32[]{:S(2)}) async-start(bf16[32,96,128]{2,1,0:T(8,128)(2,1)} %spread.1), calls=%async_computation | async-start | bytes 1572864 | tf_op jit(solution)/shard_map/all_to_all | solution.py:307
  15.3 0.0 copy-done.4
  15.3 2.8 %collective-permute-start = (bf16[384,128]{1,0:T(8,128)(2,1)S(1)}, bf16[384,128]{1,0:T(8,128)(2,1)S(1)}, u32[]{:S(2)}, u32[]{:S(2)}) collective-permute-start(bf16[384,128]{1,0:T(8,128)(2,1)S(1)} %copy-done.4), channel_id=1, source_target_pairs={{0,24},{24,0},{1,25},{25,1},{2,26},{26,2},{3,27},{27,3},{4,28},{28... | collective-permute-start | bytes 294920 | tf_op jit(solution)/shard_map/ppermute | solution.py:309
  18.1 0.0 copy-done
  18.1 0.0 copy-done.1
  18.1 0.0 copy-done.2
  18.1 1.2 %tables.1 = (s32[4,4]{1,0:T(4,128)S(1)}, s32[4,768]{1,0:T(4,128)S(1)}, s32[4,768]{1,0:T(4,128)S(1)}) custom-call(s32[64]{0:T(128)S(1)} %copy-done.2, s32[4]{0:T(128)S(1)} %copy-done.1, s32[1,768]{1,0:T(1,128)S(1)} %copy-done), custom_call_target="tpu_custom_call" | custom-call | tf_op jit(solution)/shard_map/tables/pallas_call | solution.py:317
  19.3 6.1 %all_gather.6.q_own_ref = bf16[1536,128]{1,0:T(8,128)(2,1)S(1)} all-gather(bf16[384,128]{1,0:T(8,128)(2,1)S(1)} %copy-done.4), channel_id=1, replica_groups=mesh['y'=8,'xh'=2,'xl'=2,'zh'=3,'zm'=2,'zl'=2,'core'=2] {'zl','core'}, dimensions={0}, use_global_device_ids=true | all-gather | bytes 491520 | tf_op jit(solution)/shard_map/all_gather | solution.py:310
  25.5 0.0 collective-permute-done
  25.5 6.6 %all_gather.7.q_side_ref = bf16[1536,128]{1,0:T(8,128)(2,1)S(1)} all-gather(bf16[384,128]{1,0:T(8,128)(2,1)S(1)} %collective-permute-done), channel_id=1, replica_groups=mesh['y'=8,'xh'=2,'xl'=2,'zh'=3,'zm'=2,'zl'=2,'core'=2] {'zl','core'}, dimensions={0}, use_global_device_ids=true | all-gather | bytes 491520 | tf_op jit(solution)/shard_map/all_gather | solution.py:311
  32.0 2.9 %all-to-all-done.kv_ref = bf16[32,96,128]{2,1,0:T(8,128)(2,1)S(1)} async-done(((bf16[32,96,128]{2,1,0:T(8,128)(2,1)}), bf16[32,96,128]{2,1,0:T(8,128)(2,1)S(1)}, u32[]{:S(2)}, u32[]{:S(2)}) %all-to-all-start) | async-done | bytes 786464 | tf_op jit(solution)/shard_map/all_to_all | solution.py:307
  34.9 6.7 %attend.1 = bf16[8,400,128]{2,1,0:T(8,128)(2,1)} custom-call(s32[64]{0:T(128)S(1)} %copy-done.2, s32[4,4]{1,0:T(4,128)S(1)} %get-tuple-element.12.tile_ref, bf16[32,96,128]{2,1,0:T(8,128)(2,1)S(1)} %all-to-all-done.kv_ref, bf16[1536,128]{1,0:T(8,128)(2,1)S(1)} %all_gather.6.q_own_ref, bf16[1536,128]{1,0:T(8,128)(2,1)S(1)} %all_gather.7.q_side_ref, ...), custom_call_target="tpu_custom_call" | custom-call | flops 2415919104 | bytes 4194304 | tf_op jit(solution)/shard_map/attend/pallas_call | solution.py:354
  41.6 0.0 copy-start.3
  41.6 5.2 %all-to-all-start.1 = ((bf16[8,400,128]{2,1,0:T(8,128)(2,1)}), bf16[8,400,128]{2,1,0:T(8,128)(2,1)S(1)}, u32[]{:S(2)}, u32[]{:S(2)}) async-start(bf16[8,400,128]{2,1,0:T(8,128)(2,1)} %attend.1), calls=%async_computation.1 | async-start | bytes 1638400 | tf_op jit(solution)/shard_map/all_to_all | solution.py:356
  46.8 0.0 copy-done.3
  46.8 3.4 %collective-permute-start.1 = (bf16[128,2048]{1,0:T(8,128)(2,1)S(1)}, bf16[128,2048]{1,0:T(8,128)(2,1)S(1)}, u32[]{:S(2)}, u32[]{:S(2)}) collective-permute-start(bf16[128,2048]{1,0:T(8,128)(2,1)S(1)} %copy-done.3), channel_id=1, source_target_pairs={{0,2},{2,0},{1,3},{3,1},{4,6},{6,4},{5,7},{7,5},{8,10},{10,8},{9,1... | collective-permute-start | bytes 1572872 | tf_op jit(solution)/shard_map/ppermute | solution.py:312
  50.2 19.3 %collective-permute-done.1 = bf16[128,2048]{1,0:T(8,128)(2,1)S(1)} collective-permute-done((bf16[128,2048]{1,0:T(8,128)(2,1)S(1)}, bf16[128,2048]{1,0:T(8,128)(2,1)S(1)}, u32[]{:S(2)}, u32[]{:S(2)}) %collective-permute-start.1) | collective-permute-done | bytes 524320 | tf_op jit(solution)/shard_map/ppermute | solution.py:312
  69.5 0.1 pad_maximum_fusion.w0_ref
  69.6 1.9 %collective-permute-start.2 = (bf16[2,128,2048]{2,1,0:T(8,128)(2,1)S(1)}, bf16[2,128,2048]{2,1,0:T(8,128)(2,1)S(1)}, u32[]{:S(2)}, u32[]{:S(2)}) collective-permute-start(bf16[2,128,2048]{2,1,0:T(8,128)(2,1)S(1)} %pad_maximum_fusion.w0_ref), channel_id=1, source_target_pairs={{0,1},{1,0},{2,3},{3,2},{4,5},{5,4},{6,7},{7,6},{8,9},{9,8},{10,11... | collective-permute-start | bytes 3145736 | tf_op jit(solution)/shard_map/ppermute | solution.py:358
  71.6 2.6 %collective-permute-done.2.w1_ref = bf16[2,128,2048]{2,1,0:T(8,128)(2,1)S(1)} collective-permute-done((bf16[2,128,2048]{2,1,0:T(8,128)(2,1)S(1)}, bf16[2,128,2048]{2,1,0:T(8,128)(2,1)S(1)}, u32[]{:S(2)}, u32[]{:S(2)}) %collective-permute-start.2) | collective-permute-done | bytes 1048608 | tf_op jit(solution)/shard_map/ppermute | solution.py:358
  74.2 0.0 all-to-all-done.1.got_ref
  74.2 1.3 %project.1 = bf16[96,2048]{1,0:T(8,128)(2,1)S(1)} custom-call(bf16[8,400,128]{2,1,0:T(8,128)(2,1)S(1)} %all-to-all-done.1.got_ref, bf16[2,128,2048]{2,1,0:T(8,128)(2,1)S(1)} %pad_maximum_fusion.w0_ref, bf16[2,128,2048]{2,1,0:T(8,128)(2,1)S(1)} %collective-permute-done.2.w1_ref), custom_call_target="tpu_custom_call" | custom-call | tf_op jit(solution)/shard_map/project/pallas_call | solution.py:359
  75.5 32.8 %all_to_all.15 = bf16[6,16,2048]{2,1,0:T(8,128)(2,1)S(1)} all-to-all(bf16[6,16,2048]{2,1,0:T(8,128)(2,1)S(1)} %bitcast.3), channel_id=1, replica_groups=mesh['y'=8,'xh'=2,'xl'=2,'zh'=3,'zm'=2,'zl'=2,'core'=2] {'zh','zm'}, dimensions={0} | all-to-all | bytes 786432 | tf_op jit(solution)/shard_map/all_to_all | solution.py:368
  108.3 0.7 reduce_sum.12
Async XLA Ops:
  2.0 13.2 %copy-start.4 = (bf16[384,128]{1,0:T(8,128)(2,1)S(1)}, bf16[384,128]{1,0:T(8,128)(2,1)}, u32[]{:S(2)}) copy-start(bf16[384,128]{1,0:T(8,128)(2,1)} %param.7) | copy-start | bytes 294916
  2.1 16.0 %copy-start = (s32[1,768]{1,0:T(1,128)S(1)}, s32[1,768]{1,0:T(1,128)}, u32[]{:S(2)}) copy-start(s32[1,768]{1,0:T(1,128)} %constant.5.clone.lane_ref) | copy-start | bytes 9220
  2.1 16.0 %copy-start.1 = (s32[4]{0:T(128)S(1)}, s32[4]{0:T(128)}, u32[]{:S(2)}) copy-start(s32[4]{0:T(128)} %len_ref.1) | copy-start | bytes 52
  2.1 16.0 %copy-start.2 = (s32[64]{0:T(128)S(1)}, s32[64]{0:T(128)}, u32[]{:S(2)}) copy-start(s32[64]{0:T(128)} %slot_ref.3) | copy-start | bytes 772
  2.1 32.8 %all-to-all-start = ((bf16[32,96,128]{2,1,0:T(8,128)(2,1)}), bf16[32,96,128]{2,1,0:T(8,128)(2,1)S(1)}, u32[]{:S(2)}, u32[]{:S(2)}) async-start(bf16[32,96,128]{2,1,0:T(8,128)(2,1)} %spread.1), calls=%async_computation | async-start | bytes 1572864 | tf_op jit(solution)/shard_map/all_to_all | solution.py:307
  15.3 10.2 %collective-permute-start = (bf16[384,128]{1,0:T(8,128)(2,1)S(1)}, bf16[384,128]{1,0:T(8,128)(2,1)S(1)}, u32[]{:S(2)}, u32[]{:S(2)}) collective-permute-start(bf16[384,128]{1,0:T(8,128)(2,1)S(1)} %copy-done.4), channel_id=1, source_target_pairs={{0,24},{24,0},{1,25},{25,1},{2,26},{26,2},{3,27},{27,3},{4,28},{28... | collective-permute-start | bytes 294920 | tf_op jit(solution)/shard_map/ppermute | solution.py:309
  41.6 5.3 %copy-start.3 = (bf16[128,2048]{1,0:T(8,128)(2,1)S(1)}, bf16[128,2048]{1,0:T(8,128)(2,1)}, u32[]{:S(2)}) copy-start(bf16[128,2048]{1,0:T(8,128)(2,1)} %param.12) | copy-start | bytes 1572868
  41.6 32.6 %all-to-all-start.1 = ((bf16[8,400,128]{2,1,0:T(8,128)(2,1)}), bf16[8,400,128]{2,1,0:T(8,128)(2,1)S(1)}, u32[]{:S(2)}, u32[]{:S(2)}) async-start(bf16[8,400,128]{2,1,0:T(8,128)(2,1)} %attend.1), calls=%async_computation.1 | async-start | bytes 1638400 | tf_op jit(solution)/shard_map/all_to_all | solution.py:356
  46.8 22.7 %collective-permute-start.1 = (bf16[128,2048]{1,0:T(8,128)(2,1)S(1)}, bf16[128,2048]{1,0:T(8,128)(2,1)S(1)}, u32[]{:S(2)}, u32[]{:S(2)}) collective-permute-start(bf16[128,2048]{1,0:T(8,128)(2,1)S(1)} %copy-done.3), channel_id=1, source_target_pairs={{0,2},{2,0},{1,3},{3,1},{4,6},{6,4},{5,7},{7,5},{8,10},{10,8},{9,1... | collective-permute-start | bytes 1572872 | tf_op jit(solution)/shard_map/ppermute | solution.py:312
  69.6 4.6 %collective-permute-start.2 = (bf16[2,128,2048]{2,1,0:T(8,128)(2,1)S(1)}, bf16[2,128,2048]{2,1,0:T(8,128)(2,1)S(1)}, u32[]{:S(2)}, u32[]{:S(2)}) collective-permute-start(bf16[2,128,2048]{2,1,0:T(8,128)(2,1)S(1)} %pad_maximum_fusion.w0_ref), channel_id=1, source_target_pairs={{0,1},{1,0},{2,3},{3,2},{4,5},{5,4},{6,7},{7,6},{8,9},{9,8},{10,11... | collective-permute-start | bytes 3145736 | tf_op jit(solution)/shard_map/ppermute | solution.py:358

commit v9 on v8

--- a/solution.py
+++ b/solution.py
@@ -42,7 +42,27 @@
     return lax.axis_index("xl") * 4 + own
 
 
-def spread_kernel(k_hbm, v_hbm, out_hbm, buf, in_sem, out_sem):
+def start_of(pos, bounds):
+    start = jnp.zeros_like(pos)
+    for bound in bounds:
+        start = jnp.where(pos >= bound, jnp.maximum(start, bound), start)
+    return start
+
+
+def spread_kernel(
+    slot_ref,
+    len_ref,
+    lane_ref,
+    k_hbm,
+    v_hbm,
+    out_hbm,
+    tile_ref,
+    qpos_ref,
+    qstart_ref,
+    buf,
+    in_sem,
+    out_sem,
+):
     own = lax.axis_index("zl") * 2 + lax.axis_index("core")
     col = pl.multiple_of(lax.axis_index("zh") * HD, HD)
     loads = []
@@ -66,18 +86,6 @@
     ]
     for copy in stores:
         copy.start()
-    for copy in stores:
-        copy.wait()
-
-
-def start_of(pos, bounds):
-    start = jnp.zeros_like(pos)
-    for bound in bounds:
-        start = jnp.where(pos >= bound, jnp.maximum(start, bound), start)
-    return start
-
-
-def table_kernel(slot_ref, len_ref, lane_ref, tile_ref, qpos_ref, qstart_ref):
     here = lax.axis_index("y") * 2 + lax.axis_index("xh")
     bounds = [len_ref[0]]
     for n in range(1, len_ref.shape[0] - 1):
@@ -94,6 +102,8 @@
         pos = lane_ref[...] + base
         qpos_ref[tile : tile + 1, :] = pos
         qstart_ref[tile : tile + 1, :] = start_of(pos, bounds)
+    for copy in stores:
+        copy.wait()
 
 
 def attend_kernel(
@@ -289,18 +299,32 @@
     hbm = pl.BlockSpec(memory_space=pltpu.HBM)
     smem = pl.BlockSpec(memory_space=pltpu.SMEM)
     vmem = pl.BlockSpec(memory_space=pltpu.VMEM)
-    spread = pl.pallas_call(
+    lane = np.arange(TILE)
+    in_half = lane % QUART // 16 * 64 + lane // HALF * 16 + lane % 16
+    i32 = jnp.int32
+    spread, tiles, q_pos, q_start = pl.pallas_call(
         spread_kernel,
-        out_shape=jax.ShapeDtypeStruct((SRC, 4 * KROWS, HD), jnp.bfloat16),
-        in_specs=[hbm, hbm],
-        out_specs=hbm,
+        out_shape=(
+            jax.ShapeDtypeStruct((SRC, 4 * KROWS, HD), jnp.bfloat16),
+            jax.ShapeDtypeStruct((4, 4), i32),
+            jax.ShapeDtypeStruct((4, TILE), i32),
+            jax.ShapeDtypeStruct((4, TILE), i32),
+        ),
+        in_specs=[smem, smem, vmem, hbm, hbm],
+        out_specs=(hbm, smem, vmem, vmem),
         scratch_shapes=[
             pltpu.VMEM((2, 4 * KROWS, HD), jnp.bfloat16),
             pltpu.SemaphoreType.DMA((8,)),
             pltpu.SemaphoreType.DMA((SRC,)),
         ],
         name="spread",
-    )(keys, values)
+    )(
+        block_of_slot,
+        doc_lengths,
+        jnp.asarray(in_half[None, :], i32),
+        keys,
+        values,
+    )
     spread, queries, out_weight = lax.optimization_barrier(
         (spread, queries, out_weight)
     )
@@ -310,22 +334,6 @@
     q = lax.all_gather(queries, ("zl", "core"), axis=0, tiled=True)
     q_side = lax.all_gather(q_side, ("zl", "core"), axis=0, tiled=True)
     w_side = lax.ppermute(out_weight, "zl", flip)
-
-    lane = np.arange(TILE)
-    in_half = lane % QUART // 16 * 64 + lane // HALF * 16 + lane % 16
-    i32 = jnp.int32
-    tiles, q_pos, q_start = pl.pallas_call(
-        table_kernel,
-        out_shape=(
-            jax.ShapeDtypeStruct((4, 4), i32),
-            jax.ShapeDtypeStruct((4, TILE), i32),
-            jax.ShapeDtypeStruct((4, TILE), i32),
-        ),
-        in_specs=[smem, smem, vmem],
-        out_specs=(smem, vmem, vmem),
-        compiler_params=pltpu.CompilerParams(vmem_limit_bytes=8 << 20),
-        name="tables",
-    )(block_of_slot, doc_lengths, jnp.asarray(in_half[None, :], i32))
 
     attend = pl.pallas_call(
         attend_kernel,

time: 110 us -> 112 us (1.018)
    all_to_all x1, waiting for transfers between devices: 2.86 us -> 3.99 us  [per_device(): kv = lax.all_to_all(spread, DP, 0, 0, tiled=True)]
    pallas_call x2 -> x1, Pallas kernels: 3.28 us -> 3.38 us  [per_device(): pl.pallas_call(spread_kernel, out_shape=(jax.ShapeDtypeStruct((SRC, 4 * K...]
  transfers between devices with their start and end apart: 5 -> 5, of which waited for: 3 -> 3; matrix products, arithmetic and copies ran while one was open for 0% -> 0% of each run, Pallas kernels for 1% -> 0%
where the time goes in v9:
time: 112 us; the launch traced here: 111 us
  blocking collectives  45.7 us (41%)
  starting transfers between devices  26.5 us (24%)
  waiting for transfers between devices  25.9 us (23%)
  Pallas kernels  11.4 us (10%)
    all_to_all x1, blocking collectives, per_device(): parts = lax.all_to_all(terms.reshape(6, 16, -1), Z6, 0, 0, tiled=True)  32.8 us
    ppermute x1, waiting for transfers between devices, per_device(): w_side = lax.ppermute(out_weight, 'zl', flip)  19.3 us
    all_to_all x1, starting transfers between devices, per_device(): kv = lax.all_to_all(spread, DP, 0, 0, tiled=True)  13.2 us
    pallas_call x1, Pallas kernels, per_device(): sent = attend(block_of_slot, tiles, kv, q, q_side, q_pos, q_start)  6.71 us
    all_gather x1, blocking collectives, per_device(): q_side = lax.all_gather(q_side, ('zl', 'core'), axis=0, tiled=True)  6.69 us
    all_gather x1, blocking collectives, per_device(): q = lax.all_gather(queries, ('zl', 'core'), axis=0, tiled=True)  6.14 us
    all_to_all x1, starting transfers between devices, per_device(): got = lax.all_to_all(sent, TEAM, 0, 0, tiled=True)  5.24 us
    all_to_all x1, waiting for transfers between devices, per_device(): kv = lax.all_to_all(spread, DP, 0, 0, tiled=True)  3.99 us
  transfers between devices with their start and end apart: 5, of which 3 were waited for; matrix products, arithmetic and copies ran while one was open for 0% of the time, Pallas kernels for 0%

profile of v9, /device:TPU:6, one launch (start us, length us, event | category | flops | bytes accessed | tf_op | source)
XLA Modules:
  0.0 111.0 jit_solution(17219110036921570651)
XLA Ops:
  0.0 3.4 %spread.1 = (bf16[32,96,128]{2,1,0:T(8,128)(2,1)}, s32[4,4]{1,0:T(4,128)}, s32[4,768]{1,0:T(4,128)}, s32[4,768]{1,0:T(4,128)}) custom-call(s32[64]{0:T(128)} %slot_ref.3, s32[4]{0:T(128)} %len_ref.1, s32[1,768]{1,0:T(1,128)} %constant.5.clone.lane_ref, bf16[384,384]{1,0:T(8,128)(2,1)} %k_hbm.1, bf16[384,384]{1,0:T(8,128)(2,1)} %v_hbm.1), custom_call_target="tpu_custom_call" | custom-call | tf_op jit(solution)/shard_map/spread/pallas_call | solution.py:305
  3.4 0.0 copy-start.5
  3.4 13.2 %all-to-all-start = ((bf16[32,96,128]{2,1,0:T(8,128)(2,1)}), bf16[32,96,128]{2,1,0:T(8,128)(2,1)S(1)}, u32[]{:S(2)}, u32[]{:S(2)}) async-start(bf16[32,96,128]{2,1,0:T(8,128)(2,1)} %get-tuple-element.15), calls=%async_computation | async-start | bytes 1572864 | tf_op jit(solution)/shard_map/all_to_all | solution.py:331
  16.6 0.0 copy-done.5
  16.6 2.8 %collective-permute-start = (bf16[384,128]{1,0:T(8,128)(2,1)S(1)}, bf16[384,128]{1,0:T(8,128)(2,1)S(1)}, u32[]{:S(2)}, u32[]{:S(2)}) collective-permute-start(bf16[384,128]{1,0:T(8,128)(2,1)S(1)} %copy-done.5), channel_id=1, source_target_pairs={{0,24},{24,0},{1,25},{25,1},{2,26},{26,2},{3,27},{27,3},{4,28},{28... | collective-permute-start | bytes 294920 | tf_op jit(solution)/shard_map/ppermute | solution.py:333
  19.4 6.1 %all_gather.6.q_own_ref = bf16[1536,128]{1,0:T(8,128)(2,1)S(1)} all-gather(bf16[384,128]{1,0:T(8,128)(2,1)S(1)} %copy-done.5), channel_id=1, replica_groups=mesh['y'=8,'xh'=2,'xl'=2,'zh'=3,'zm'=2,'zl'=2,'core'=2] {'zl','core'}, dimensions={0}, use_global_device_ids=true | all-gather | bytes 491520 | tf_op jit(solution)/shard_map/all_gather | solution.py:334
  25.5 0.0 copy-start.1
  25.5 0.0 copy-start.2
  25.5 0.0 collective-permute-done
  25.5 6.7 %all_gather.7.q_side_ref = bf16[1536,128]{1,0:T(8,128)(2,1)S(1)} all-gather(bf16[384,128]{1,0:T(8,128)(2,1)S(1)} %collective-permute-done), channel_id=1, replica_groups=mesh['y'=8,'xh'=2,'xl'=2,'zh'=3,'zm'=2,'zl'=2,'core'=2] {'zl','core'}, dimensions={0}, use_global_device_ids=true | all-gather | bytes 491520 | tf_op jit(solution)/shard_map/all_gather | solution.py:335
  32.2 4.0 %all-to-all-done.kv_ref = bf16[32,96,128]{2,1,0:T(8,128)(2,1)S(1)} async-done(((bf16[32,96,128]{2,1,0:T(8,128)(2,1)}), bf16[32,96,128]{2,1,0:T(8,128)(2,1)S(1)}, u32[]{:S(2)}, u32[]{:S(2)}) %all-to-all-start) | async-done | bytes 786464 | tf_op jit(solution)/shard_map/all_to_all | solution.py:331
  36.2 0.0 copy-start.3
  36.2 0.0 copy-start
  36.2 0.0 copy-done.1
  36.2 0.0 copy-done.2
  36.2 0.7 copy-done.3
  36.9 0.0 copy-done
  36.9 6.7 %attend.1 = bf16[8,400,128]{2,1,0:T(8,128)(2,1)} custom-call(s32[64]{0:T(128)S(1)} %copy-done, s32[4,4]{1,0:T(4,128)S(1)} %copy-done.3, bf16[32,96,128]{2,1,0:T(8,128)(2,1)S(1)} %all-to-all-done.kv_ref, bf16[1536,128]{1,0:T(8,128)(2,1)S(1)} %all_gather.6.q_own_ref, bf16[1536,128]{1,0:T(8,128)(2,1)S(1)} %all_gather.7.q_side_ref, s32[4,768]{1,0:T(4,128)S(1)} %copy-done.1, ...), custom_call_target="tpu_custom_call" | custom-call | flops 2415919104 | bytes 4194304 | tf_op jit(solution)/shard_map/attend/pallas_call | solution.py:362
  43.6 0.0 copy-start.4
  43.6 5.2 %all-to-all-start.1 = ((bf16[8,400,128]{2,1,0:T(8,128)(2,1)}), bf16[8,400,128]{2,1,0:T(8,128)(2,1)S(1)}, u32[]{:S(2)}, u32[]{:S(2)}) async-start(bf16[8,400,128]{2,1,0:T(8,128)(2,1)} %attend.1), calls=%async_computation.1 | async-start | bytes 1638400 | tf_op jit(solution)/shard_map/all_to_all | solution.py:364
  48.8 0.0 copy-done.4
  48.8 3.4 %collective-permute-start.1 = (bf16[128,2048]{1,0:T(8,128)(2,1)S(1)}, bf16[128,2048]{1,0:T(8,128)(2,1)S(1)}, u32[]{:S(2)}, u32[]{:S(2)}) collective-permute-start(bf16[128,2048]{1,0:T(8,128)(2,1)S(1)} %copy-done.4), channel_id=1, source_target_pairs={{0,2},{2,0},{1,3},{3,1},{4,6},{6,4},{5,7},{7,5},{8,10},{10,8},{9,1... | collective-permute-start | bytes 1572872 | tf_op jit(solution)/shard_map/ppermute | solution.py:336
  52.2 19.3 %collective-permute-done.1 = bf16[128,2048]{1,0:T(8,128)(2,1)S(1)} collective-permute-done((bf16[128,2048]{1,0:T(8,128)(2,1)S(1)}, bf16[128,2048]{1,0:T(8,128)(2,1)S(1)}, u32[]{:S(2)}, u32[]{:S(2)}) %collective-permute-start.1) | collective-permute-done | bytes 524320 | tf_op jit(solution)/shard_map/ppermute | solution.py:336
  71.5 0.1 pad_maximum_fusion.w0_ref
  71.6 1.9 %collective-permute-start.2 = (bf16[2,128,2048]{2,1,0:T(8,128)(2,1)S(1)}, bf16[2,128,2048]{2,1,0:T(8,128)(2,1)S(1)}, u32[]{:S(2)}, u32[]{:S(2)}) collective-permute-start(bf16[2,128,2048]{2,1,0:T(8,128)(2,1)S(1)} %pad_maximum_fusion.w0_ref), channel_id=1, source_target_pairs={{0,1},{1,0},{2,3},{3,2},{4,5},{5,4},{6,7},{7,6},{8,9},{9,8},{10,11... | collective-permute-start | bytes 3145736 | tf_op jit(solution)/shard_map/ppermute | solution.py:366
  73.5 2.6 %collective-permute-done.2.w1_ref = bf16[2,128,2048]{2,1,0:T(8,128)(2,1)S(1)} collective-permute-done((bf16[2,128,2048]{2,1,0:T(8,128)(2,1)S(1)}, bf16[2,128,2048]{2,1,0:T(8,128)(2,1)S(1)}, u32[]{:S(2)}, u32[]{:S(2)}) %collective-permute-start.2) | collective-permute-done | bytes 1048608 | tf_op jit(solution)/shard_map/ppermute | solution.py:366
  76.2 0.0 all-to-all-done.1.got_ref
  76.2 1.3 %project.1 = bf16[96,2048]{1,0:T(8,128)(2,1)S(1)} custom-call(bf16[8,400,128]{2,1,0:T(8,128)(2,1)S(1)} %all-to-all-done.1.got_ref, bf16[2,128,2048]{2,1,0:T(8,128)(2,1)S(1)} %pad_maximum_fusion.w0_ref, bf16[2,128,2048]{2,1,0:T(8,128)(2,1)S(1)} %collective-permute-done.2.w1_ref), custom_call_target="tpu_custom_call" | custom-call | tf_op jit(solution)/shard_map/project/pallas_call | solution.py:367
  77.5 32.8 %all_to_all.15 = bf16[6,16,2048]{2,1,0:T(8,128)(2,1)S(1)} all-to-all(bf16[6,16,2048]{2,1,0:T(8,128)(2,1)S(1)} %bitcast.3), channel_id=1, replica_groups=mesh['y'=8,'xh'=2,'xl'=2,'zh'=3,'zm'=2,'zl'=2,'core'=2] {'zh','zm'}, dimensions={0} | all-to-all | bytes 786432 | tf_op jit(solution)/shard_map/all_to_all | solution.py:376
  110.3 0.7 reduce_sum.12
Async XLA Ops:
  3.4 13.2 %copy-start.5 = (bf16[384,128]{1,0:T(8,128)(2,1)S(1)}, bf16[384,128]{1,0:T(8,128)(2,1)}, u32[]{:S(2)}) copy-start(bf16[384,128]{1,0:T(8,128)(2,1)} %param.7) | copy-start | bytes 294916
  3.4 32.8 %all-to-all-start = ((bf16[32,96,128]{2,1,0:T(8,128)(2,1)}), bf16[32,96,128]{2,1,0:T(8,128)(2,1)S(1)}, u32[]{:S(2)}, u32[]{:S(2)}) async-start(bf16[32,96,128]{2,1,0:T(8,128)(2,1)} %get-tuple-element.15), calls=%async_computation | async-start | bytes 1572864 | tf_op jit(solution)/shard_map/all_to_all | solution.py:331
  16.6 8.9 %collective-permute-start = (bf16[384,128]{1,0:T(8,128)(2,1)S(1)}, bf16[384,128]{1,0:T(8,128)(2,1)S(1)}, u32[]{:S(2)}, u32[]{:S(2)}) collective-permute-start(bf16[384,128]{1,0:T(8,128)(2,1)S(1)} %copy-done.5), channel_id=1, source_target_pairs={{0,24},{24,0},{1,25},{25,1},{2,26},{26,2},{3,27},{27,3},{4,28},{28... | collective-permute-start | bytes 294920 | tf_op jit(solution)/shard_map/ppermute | solution.py:333
  25.5 10.7 %copy-start.1 = (s32[4,768]{1,0:T(4,128)S(1)}, s32[4,768]{1,0:T(4,128)}, u32[]{:S(2)}) copy-start(s32[4,768]{1,0:T(4,128)} %get-tuple-element.17.qpos_ref) | copy-start | bytes 36868
  25.5 10.7 %copy-start.2 = (s32[4,768]{1,0:T(4,128)S(1)}, s32[4,768]{1,0:T(4,128)}, u32[]{:S(2)}) copy-start(s32[4,768]{1,0:T(4,128)} %get-tuple-element.18.qstart_ref) | copy-start | bytes 36868
  36.2 0.7 copy-start.3
  36.2 0.7 copy-start
  43.6 5.2 %copy-start.4 = (bf16[128,2048]{1,0:T(8,128)(2,1)S(1)}, bf16[128,2048]{1,0:T(8,128)(2,1)}, u32[]{:S(2)}) copy-start(bf16[128,2048]{1,0:T(8,128)(2,1)} %param.12) | copy-start | bytes 1572868
  43.6 32.6 %all-to-all-start.1 = ((bf16[8,400,128]{2,1,0:T(8,128)(2,1)}), bf16[8,400,128]{2,1,0:T(8,128)(2,1)S(1)}, u32[]{:S(2)}, u32[]{:S(2)}) async-start(bf16[8,400,128]{2,1,0:T(8,128)(2,1)} %attend.1), calls=%async_computation.1 | async-start | bytes 1638400 | tf_op jit(solution)/shard_map/all_to_all | solution.py:364
  48.8 22.7 %collective-permute-start.1 = (bf16[128,2048]{1,0:T(8,128)(2,1)S(1)}, bf16[128,2048]{1,0:T(8,128)(2,1)S(1)}, u32[]{:S(2)}, u32[]{:S(2)}) collective-permute-start(bf16[128,2048]{1,0:T(8,128)(2,1)S(1)} %copy-done.4), channel_id=1, source_target_pairs={{0,2},{2,0},{1,3},{3,1},{4,6},{6,4},{5,7},{7,5},{8,10},{10,8},{9,1... | collective-permute-start | bytes 1572872 | tf_op jit(solution)/shard_map/ppermute | solution.py:336
  71.6 4.6 %collective-permute-start.2 = (bf16[2,128,2048]{2,1,0:T(8,128)(2,1)S(1)}, bf16[2,128,2048]{2,1,0:T(8,128)(2,1)S(1)}, u32[]{:S(2)}, u32[]{:S(2)}) collective-permute-start(bf16[2,128,2048]{2,1,0:T(8,128)(2,1)S(1)} %pad_maximum_fusion.w0_ref), channel_id=1, source_target_pairs={{0,1},{1,0},{2,3},{3,2},{4,5},{5,4},{6,7},{7,6},{8,9},{9,8},{10,11... | collective-permute-start | bytes 3145736 | tf_op jit(solution)/shard_map/ppermute | solution.py:366
